TPU v7x, 256 devices: a whole 4x4x8 slice. The times are simulated.
256 devices in a mesh: grp: 4 (over x), tile: 64 (over y, z, core).
Axes of the slice: x: 4, y: 4, z: 8, core: 2. Of those that a mesh axis runs over, the one named last changes fastest.
Arguments:
- temp: bfloat16 [48, 64, 16384], P(None, 'grp', 'tile'), may hold values from -6 to 6
- humid: bfloat16 [48, 64, 16384], P(None, 'grp', 'tile'), may hold values from -5 to 5
- parent: int32 [64, 16384], P('grp', 'tile'), may hold values from 0 to 65535, as said below
- kabs: float32 [112, 48], replicated, may hold values from 0.003 to 1
- planck: float32 [112], replicated, may hold values from 0.5 to 2
- top_flux: float32 [112], replicated, may hold values from 0 to 2
Outputs:
- temp_next: bfloat16 [48, 64, 16384], P(None, 'grp', 'tile')
Inputs may be any that keep to these rules, and one draw needn't show every extreme that they name: parent // 1024 is the tile index, in the same region, of the device owning that parent column; the fine cells of one device name any one owner at most 128 times.
All inputs are finite; a program needn't handle non-finite values.
Results may differ from a plain program's by a relative error of at most 0.005.
Values may be sent and summed in bfloat16 or wider, within the bound.
No kernel may reach another device: no remote copies, remote signals or barrier semaphores. Data moves between devices by JAX's collectives and lax.ppermute only.
A program may use at most 64 MiB of HBM per device.

v0:
```python
import jax
import jax.numpy as jnp
from jax import lax
from jax.sharding import Mesh
from jax.sharding import PartitionSpec as P

TILE = ("tile_0", "tile_1", "tile_2")


def with_halo(shard, sides, width):
    edges = {}
    for axis, dim in sides:
        peers, length = (lax.axis_size(axis), shard.shape[dim])
        up = [(i, (i + 1) % peers) for i in range(peers)]
        last = lax.slice_in_dim(shard, length - width, length, axis=dim)
        leading = lax.slice_in_dim(shard, 0, width, axis=dim)
        edges[dim] = (
            lax.ppermute(last, axis, up),
            lax.ppermute(leading, axis, [(b, a) for a, b in up]),
        )
    done = []
    for _, dim in sides:
        low, high = edges[dim]
        around = [(width, width) if d in done else (0, 0) for d in range(shard.ndim)]
        shard = jnp.concatenate([jnp.pad(low, around), shard, jnp.pad(high, around)], axis=dim)
        done.append(dim)
    return shard


def in_blocks(shard, dim, peers):
    before, after = (shard.shape[:dim], shard.shape[dim + 1 :])
    return jnp.moveaxis(shard.reshape(*before, peers, -1, *after), dim, 0)


def in_order(tiles, dim):
    tiles = jnp.moveaxis(tiles, 0, dim)
    lengths = tiles.shape
    return tiles.reshape(*lengths[:dim], lengths[dim] * lengths[dim + 1], *lengths[dim + 2 :])


def turned_blocks(tiles, axes, turns):
    lengths = [lax.axis_size(a) for a in axes]
    tiles = tiles.reshape(*lengths, *tiles.shape[1:])
    for k in turns:
        tiles = lax.all_to_all(tiles, axes[k], split_axis=k, concat_axis=k, tiled=True)
    return tiles.reshape(-1, *tiles.shape[len(axes) :])


def core_and_chips(shard, groups, turns, split_dim, concat_dim):
    peers = lax.axis_size(groups[0]) * lax.axis_size(groups[1])
    tiles = in_blocks(shard, split_dim, peers)
    return in_order(turned_blocks(tiles, groups, turns), concat_dim)


def recur(coef, source, init):
    levels = coef.shape[0]
    blocks = levels // 8
    rest = coef.shape[1:]
    coef4 = coef.reshape((blocks, 8) + rest)
    source4 = source.reshape((blocks, 8) + rest)
    prod_list = []
    part_list = []
    prod_now = jnp.ones((blocks,) + rest, jnp.float32)
    part_now = jnp.zeros((blocks,) + rest, jnp.float32)
    for inner in range(8):
        prod_now = coef4[:, inner] * prod_now
        part_now = coef4[:, inner] * part_now + source4[:, inner]
        prod_list.append(prod_now)
        part_list.append(part_now)
    starts = []
    carry = init
    for outer in range(blocks):
        starts.append(carry)
        carry = prod_list[7][outer] * carry + part_list[7][outer]
    start = jnp.stack(starts, 0)
    result = jnp.stack([prod_list[j] * start + part_list[j] for j in range(8)], 1)
    return result.reshape((levels,) + rest)


def radiate(tc, hc, kabs, planck, top_flux):
    levels, count = tc.shape
    kblk = kabs.reshape(-1, 16, levels)
    pblk = planck.reshape(-1, 16)
    tblk = top_flux.reshape(-1, 16)
    absorb = jnp.exp(0.5 * hc)[:, None, :]
    emit = jnp.exp(0.25 * tc)[:, None, :]

    def one_block(items):
        k_blk, p_blk, t_blk = items
        tau = jnp.transpose(k_blk)[:, :, None] * absorb
        trans = jnp.exp(-tau)
        source = p_blk[None, :, None] * emit * (1.0 - trans)
        top = jnp.broadcast_to(t_blk[:, None], (16, count))
        down = recur(trans, source, top)
        up = recur(trans[::-1], source[::-1], 0.3 * down[-1])[::-1]
        net = down - up
        top_net = top - up[0]
        before = jnp.concatenate([top_net[None], net[:-1]], 0)
        return jnp.sum(before - net, axis=1)

    parts = lax.map(one_block, (kblk, pblk, tblk))
    return jnp.sum(parts, axis=0) * (levels / kabs.shape[0])


def laplace(padded):
    value = padded.astype(jnp.float32)
    centre = value[:, 1:-1, 1:-1]
    return (
        value[:, :-2, 1:-1]
        + value[:, 2:, 1:-1]
        + value[:, 1:-1, :-2]
        + value[:, 1:-1, 2:]
        - 4.0 * centre
    )


def on_device(temp, humid, parent, kabs, planck, top_flux):
    levels = temp.shape[0]
    fine = temp.shape[1] * temp.shape[2]
    owned = fine // 4
    tiles = lax.axis_size(TILE)
    capacity_limit = 2 * fine // tiles
    width = tiles * capacity_limit
    padded = with_halo(temp, (("grp", 1), (TILE, 2)), 1)
    first = (temp.astype(jnp.float32) + 0.2 * laplace(padded)).astype(jnp.bfloat16)
    flat_parent = parent.reshape(-1)
    owner = flat_parent // owned
    local = flat_parent % owned
    onehot = (owner[:, None] == jnp.arange(tiles, dtype=jnp.int32)[None, :]).astype(jnp.int32)
    position = jnp.sum(jnp.cumsum(onehot, axis=0) * onehot, axis=1) - 1
    slot = owner * capacity_limit + position
    values = jnp.concatenate([temp.reshape(levels, fine), humid.reshape(levels, fine)], 0)
    outgoing = jnp.zeros((2 * levels, width), jnp.bfloat16).at[:, slot].set(values)
    labels = jnp.full((1, width), owned, jnp.int32).at[0, slot].set(local)
    incoming, in_labels = (
        lax.all_to_all(outgoing, TILE, split_axis=1, concat_axis=1, tiled=True),
        lax.all_to_all(labels, TILE, split_axis=1, concat_axis=1, tiled=True),
    )
    received = in_labels[0].astype(jnp.int32)
    sums = jax.ops.segment_sum(
        jnp.transpose(incoming.astype(jnp.float32)), received, num_segments=owned
    )
    counts = jax.ops.segment_sum(jnp.ones((width,), jnp.float32), received, num_segments=owned)
    means = sums / jnp.maximum(counts, 1.0)[:, None]
    tc = jnp.transpose(means[:, :levels])
    hc = jnp.transpose(means[:, levels:])
    heat_c = radiate(tc, hc, kabs, planck, top_flux).astype(jnp.bfloat16)
    hmean = hc.astype(jnp.bfloat16)
    answer = jnp.concatenate([heat_c, hmean], 0)[:, jnp.minimum(received, owned - 1)]
    returned = core_and_chips(answer, (("tile_0", "tile_1"), "tile_2"), (1, 0), 1, 1)
    picked = returned[:, slot]
    heat_cell = picked[:levels]
    hmean_cell = picked[levels:]
    heat_f = heat_cell.astype(jnp.float32) + 0.5 * (
        humid.reshape(levels, fine).astype(jnp.float32) - hmean_cell.astype(jnp.float32)
    )
    second = (first.astype(jnp.float32) + 0.5 * heat_f.reshape(temp.shape)).astype(jnp.bfloat16)
    padded_second = with_halo(second, (("grp", 1), (TILE, 2)), 1)
    return (second.astype(jnp.float32) + 0.2 * laplace(padded_second)).astype(jnp.bfloat16)


def solution(mesh):
    finer = Mesh(
        mesh.devices.reshape(mesh.shape["grp"], 4, 8, 2), ("grp", "tile_0", "tile_1", "tile_2")
    )
    placed = (P(None, "grp", TILE), P(None, "grp", TILE), P("grp", TILE), P(), P(), P())
    return jax.shard_map(
        on_device, mesh=finer, in_specs=placed, out_specs=P(None, "grp", TILE), check_vma=False
    )
```

profile of v0, /device:TPU:6, one launch (start us, length us, event | category | flops | bytes accessed | tf_op | source)
XLA Modules:
  0.0 491.1 jit_solution(7096378762047605938)
XLA Ops:
  0.9 18.4 %reduce-window.6 = s32[64,32,128]{2,1,0:T(8,128)S(1)} reduce-window(s32[64,32,128]{2,1,0:T(8,128)S(1)} %fusion.52, s32[]{:T(128)} %copy.382), window={size=1x1x128 pad=0_0x0_0x127_0}, to_apply=%region_0.1 | reduce-window | flops 33292288 | bytes 2097156 | tf_op jit(solution)/shard_map/reduce-window
  22.0 16.1 %scatter_custom_fusion.3 = s32[8192]{0:T(1024)} fusion(s32[4096]{0:T(1024)S(1)} %broadcast_select_fusion, s32[4096]{0:T(1024)S(1)} %get-tuple-element.125, s32[]{:T(128)} %constant.42.clone.1), kind=kCustom, calls=%fused_computation.237 | custom fusion | bytes 32772
  38.1 12.1 %all-to-all-start = ((s32[1,64,128]{2,0,1:T(1,128)}), s32[1,64,128]{2,0,1:T(1,128)S(1)}, u32[]{:S(2)}, u32[]{:S(2)}) async-start(s32[1,64,128]{2,0,1:T(1,128)} %bitcast.89), calls=%async_computation | async-start | bytes 65536 | tf_op jit(solution)/shard_map/all_to_all | solution.py:137
  52.3 12.8 %scatter_custom_fusion = bf16[96,8192]{0,1:T(8,128)(2,1)S(1)} fusion(s32[4096]{0:T(1024)S(1)} %bitcast.640, bf16[48,4096]{0,1:T(8,128)(2,1)S(1)} %bitcast.631, bf16[]{:T(256)} %constant.114, bf16[48,4096]{0,1:T(8,128)(2,1)} %bitcast.638, bf16[]{:T(256)} %constant.37.clone.1), kind=kCustom, calls=%fused_computation.175 | custom fusion | flops 1572864 | bytes 3014660 | tf_op jit(solution)/shard_map/scatter | solution.py:133
  65.1 2.8 copy.310
  67.9 10.6 %all-to-all-start.1 = ((bf16[96,64,128]{2,0,1:T(8,128)(2,1)}), bf16[96,64,128]{2,0,1:T(8,128)(2,1)}, u32[]{:S(2)}, u32[]{:S(2)}) async-start(bf16[96,64,128]{2,0,1:T(8,128)(2,1)} %copy.310), calls=%async_computation.1 | async-start | bytes 3145728 | tf_op jit(solution)/shard_map/all_to_all | solution.py:136
  78.7 57.9 %scatter_custom_fusion.2 = f32[1024]{0:T(1024)S(1)} fusion(s32[8192]{0:T(1024)S(1)} %bitcast.647, f32[8192]{0:T(1024)S(1)} %broadcast.277, f32[]{:T(128)} %constant.41.clone.1), kind=kCustom, calls=%fused_computation.248 | custom fusion | flops 8192 | bytes 4100 | tf_op jit(solution)/shard_map/scatter-add | solution.py:143
  139.0 3.3 copy.312
  142.4 44.4 %scatter_custom_fusion.1 = f32[1024,96]{1,0:T(8,128)S(1)} fusion(s32[8192]{0:T(1024)S(1)} %bitcast.648, f32[8192,96]{1,0:T(8,128)} %copy.312, f32[]{:T(128)} %constant.41.clone.1), kind=kCustom, calls=%fused_computation.206 | custom fusion | flops 786432 | bytes 393728 | tf_op jit(solution)/shard_map/scatter-add | solution.py:140
  187.8 159.6 %while.10 = (s32[]{:T(128)}, f32[7,48,1024]{2,1,0:T(8,128)}, f32[7,16]{1,0:T(8,128)S(1)}, f32[7,16,48]{2,1,0:T(8,128)S(1)}, f32[48,1,1024]{2,0,1:T(8,128)S(1)}, ...) while((s32[]{:T(128)}, f32[7,48,1024]{2,1,0:T(8,128)}, f32[7,16]{1,0:T(8,128)S(1)}, ...), condition=%wide.region_9.10_spmd, body=%wide.region_7.9_spmd.sunk | while | flops 26214400 | bytes 160786352 | solution.py:101
  193.5 3.5 negate_exponential_fusion.5
  197.0 1.9 rev.14
  198.9 2.1 rev.15
  201.0 2.6 bitcast_add_fusion.22
  216.3 3.5 negate_exponential_fusion.5
  219.8 1.9 rev.14
  221.7 2.1 rev.15
  223.8 2.6 bitcast_add_fusion.22
  239.1 3.5 negate_exponential_fusion.5
  242.6 1.9 rev.14
  244.5 2.1 rev.15
  246.6 2.6 bitcast_add_fusion.22
  261.9 3.5 negate_exponential_fusion.5
  267.2 2.1 rev.15
  269.4 2.6 bitcast_add_fusion.22
  284.7 3.5 negate_exponential_fusion.5
  290.1 2.1 rev.15
  292.2 2.6 bitcast_add_fusion.22
  307.5 3.5 negate_exponential_fusion.5
  312.9 2.1 rev.15
  315.0 2.6 bitcast_add_fusion.22
  330.3 3.5 negate_exponential_fusion.5
  335.7 2.1 rev.15
  337.8 2.6 bitcast_add_fusion.22
  349.9 28.0 %gather_fusion = bf16[8192,96]{1,0:T(8,128)(2,1)S(1)} fusion(bf16[96,1024]{0,1:T(8,128)(2,1)S(1)} %copy.314, s32[8192]{0:T(1024)} %broadcast_clamp_fusion), kind=kCustom, calls=%fused_computation | custom fusion | bytes 3178496 | tf_op jit(solution)/shard_map/gather | solution.py:149
  377.9 2.8 copy.316
  380.7 6.1 %all_to_all.28 = bf16[32,2,96,128]{3,2,0,1:T(8,128)(2,1)S(1)} all-to-all(bf16[32,2,96,128]{3,2,0,1:T(8,128)(2,1)} %copy.316), channel_id=1, replica_groups=mesh['grp'=4,'tile_0'=4,'tile_1'=8,'tile_2'=2] {'tile_2'}, dimensions={1} | all-to-all | bytes 3145728 | tf_op jit(solution)/shard_map/all_to_all | solution.py:45
  388.2 18.1 %all-to-all-start.3 = ((bf16[32,2,96,128]{3,2,1,0:T(8,128)(2,1)}), bf16[32,2,96,128]{3,2,1,0:T(8,128)(2,1)S(1)}, u32[]{:S(2)}, u32[]{:S(2)}) async-start(bf16[32,2,96,128]{3,2,1,0:T(8,128)(2,1)} %copy.317), calls=%async_computation.3 | async-start | bytes 3145728 | tf_op jit(solution)/shard_map/all_to_all | solution.py:45
  406.5 4.6 collective-permute-start.3
  414.5 27.9 %collective-permute-done.3 = bf16[48,16,1]{2,1,0:T(8,128)(2,1)S(1)} collective-permute-done((bf16[48,16,1]{2,1,0:T(8,128)(2,1)S(1)}, bf16[48,16,1]{2,1,0:T(8,128)(2,1)S(1)}, u32[]{:S(2)}, u32[]{:S(2)}) %collective-permute-start.3) | collective-permute-done | bytes 1568 | tf_op jit(solution)/shard_map/ppermute | solution.py:19
  442.4 5.3 %collective-permute-done = bf16[48,16,1]{2,1,0:T(8,128)(2,1)S(1)} collective-permute-done((bf16[48,16,1]{2,1,0:T(8,128)(2,1)S(1)}, bf16[48,16,1]{2,1,0:T(8,128)(2,1)S(1)}, u32[]{:S(2)}, u32[]{:S(2)}) %collective-permute-start) | collective-permute-done | bytes 1568 | tf_op jit(solution)/shard_map/ppermute | solution.py:18
  447.7 2.2 fusion.55
  451.1 3.1 copy.318
  454.2 14.9 %gather_fusion.1 = bf16[4096,96]{1,0:T(8,128)(2,1)} fusion(bf16[96,8192]{0,1:T(8,128)(2,1)S(1)} %bitcast.626, s32[4096]{0:T(1024)S(1)} %broadcast_clamp_fusion.1), kind=kCustom, calls=%fused_computation.1 | custom fusion | bytes 1589248 | tf_op jit(solution)/shard_map/gather | solution.py:151
  469.1 3.7 add_multiply_fusion
  472.7 2.4 copy.319
  480.1 2.7 collective-permute-done.7
  482.8 5.3 %collective-permute-done.4 = bf16[48,16,1]{2,1,0:T(8,128)(2,1)S(1)} collective-permute-done((bf16[48,16,1]{2,1,0:T(8,128)(2,1)S(1)}, bf16[48,16,1]{2,1,0:T(8,128)(2,1)S(1)}, u32[]{:S(2)}, u32[]{:S(2)}) %collective-permute-start.4) | collective-permute-done | bytes 1568 | tf_op jit(solution)/shard_map/ppermute | solution.py:18
  (547 shorter events, 119.6 us)
Async XLA Ops:
  19.3 2.4 copy-start.25
  19.3 2.5 copy-start.22
  19.3 30.9 %copy-start.15 = (bf16[48,16,256]{2,1,0:T(8,128)(2,1)S(1)}, bf16[48,16,256]{2,1,0:T(8,128)(2,1)}, u32[]{:S(2)}) copy-start(bf16[48,16,256]{2,1,0:T(8,128)(2,1)} %param.9) | copy-start | bytes 1179652
  19.7 31.1 %copy-start.10 = (bf16[48,16,256]{2,1,0:T(8,128)(2,1)S(1)}, bf16[48,16,256]{2,1,0:T(8,128)(2,1)}, u32[]{:S(2)}) copy-start(bf16[48,16,256]{2,1,0:T(8,128)(2,1)} %param.8) | copy-start | bytes 1179652
  21.7 43.4 %copy-start.16 = (s32[4096,1]{0,1:T(1,128)}, s32[4096,1]{0,1:T(1,128)S(1)}, u32[]{:S(2)}) copy-start(s32[4096,1]{0,1:T(1,128)S(1)} %compare_select_fusion.1) | copy-start | bytes 49156
  38.1 29.8 %all-to-all-start = ((s32[1,64,128]{2,0,1:T(1,128)}), s32[1,64,128]{2,0,1:T(1,128)S(1)}, u32[]{:S(2)}, u32[]{:S(2)}) async-start(s32[1,64,128]{2,0,1:T(1,128)} %bitcast.89), calls=%async_computation | async-start | bytes 65536 | tf_op jit(solution)/shard_map/all_to_all | solution.py:137
  50.8 17.1 %copy-start.8 = (bf16[48,16,256]{0,2,1:T(8,128)(2,1)}, bf16[48,16,256]{0,2,1:T(8,128)(2,1)S(1)}, u32[]{:S(2)}) copy-start(bf16[48,16,256]{0,2,1:T(8,128)(2,1)S(1)} %copy.309) | copy-start | bytes 1179652
  65.1 13.4 %copy-start.23 = (f32[112]{0:T(128)S(1)}, f32[112]{0:T(128)}, u32[]{:S(2)}) copy-start(f32[112]{0:T(128)} %param.13) | copy-start | bytes 1348
  65.1 13.4 %copy-start.21 = (f32[112,48]{0,1:T(8,128)S(1)}, f32[112,48]{0,1:T(8,128)}, u32[]{:S(2)}) copy-start(f32[112,48]{0,1:T(8,128)} %param.11) | copy-start | bytes 64516
  65.1 13.5 %copy-start.24 = (f32[112]{0:T(128)S(1)}, f32[112]{0:T(128)}, u32[]{:S(2)}) copy-start(f32[112]{0:T(128)} %param.12) | copy-start | bytes 1348
  67.9 69.5 %all-to-all-start.1 = ((bf16[96,64,128]{2,0,1:T(8,128)(2,1)}), bf16[96,64,128]{2,0,1:T(8,128)(2,1)}, u32[]{:S(2)}, u32[]{:S(2)}) async-start(bf16[96,64,128]{2,0,1:T(8,128)(2,1)} %copy.310), calls=%async_computation.1 | async-start | bytes 3145728 | tf_op jit(solution)/shard_map/all_to_all | solution.py:136
  191.4 2.1 copy-start.14
  201.0 2.9 copy-start.2
  203.6 1.9 copy-start
  214.2 2.1 copy-start.14
  223.8 2.9 copy-start.2
  226.4 1.9 copy-start
  237.0 2.1 copy-start.14
  246.6 2.9 copy-start.2
  249.2 1.9 copy-start
  259.8 2.1 copy-start.14
  269.4 2.9 copy-start.2
  272.0 1.9 copy-start
  277.2 1.8 copy-start.4
  277.2 1.8 copy-start.6
  282.6 2.1 copy-start.14
  292.2 2.9 copy-start.2
  294.8 1.9 copy-start
  305.4 2.1 copy-start.14
  315.0 2.9 copy-start.2
  317.6 1.9 copy-start
  328.2 2.1 copy-start.14
  337.8 2.9 copy-start.2
  340.4 1.9 copy-start
  345.6 1.8 copy-start.6
  386.8 19.5 %copy-start.11 = (bf16[48,16,256]{2,1,0:T(8,128)(2,1)S(1)}, bf16[48,16,256]{2,1,0:T(8,128)(2,1)}, u32[]{:S(2)}) copy-start(bf16[48,16,256]{2,1,0:T(8,128)(2,1)} %param.8) | copy-start | bytes 1179652
  386.8 27.7 %copy-start.17 = (s32[4096,1]{0,1:T(1,128)S(1)}, s32[4096,1]{0,1:T(1,128)}, u32[]{:S(2)}) copy-start(s32[4096,1]{0,1:T(1,128)} %copy-done.16) | copy-start | bytes 49156
  388.2 61.7 %all-to-all-start.3 = ((bf16[32,2,96,128]{3,2,1,0:T(8,128)(2,1)}), bf16[32,2,96,128]{3,2,1,0:T(8,128)(2,1)S(1)}, u32[]{:S(2)}, u32[]{:S(2)}) async-start(bf16[32,2,96,128]{3,2,1,0:T(8,128)(2,1)} %copy.317), calls=%async_computation.3 | async-start | bytes 3145728 | tf_op jit(solution)/shard_map/all_to_all | solution.py:45
  406.5 35.9 %collective-permute-start.3 = (bf16[48,16,1]{2,1,0:T(8,128)(2,1)S(1)}, bf16[48,16,1]{2,1,0:T(8,128)(2,1)S(1)}, u32[]{:S(2)}, u32[]{:S(2)}) collective-permute-start(bf16[48,16,1]{2,1,0:T(8,128)(2,1)S(1)} %get-tuple-element.122), channel_id=1, source_target_pairs={{1,0},{2,1},{3,2},{4,3},{5,4},{6,5},{7,6},{8,7},{9,8},{10,9},{11,1... | collective-permute-start | bytes 4616 | tf_op jit(solution)/shard_map/ppermute | solution.py:19
  411.1 36.6 %collective-permute-start = (bf16[48,16,1]{2,1,0:T(8,128)(2,1)S(1)}, bf16[48,16,1]{2,1,0:T(8,128)(2,1)S(1)}, u32[]{:S(2)}, u32[]{:S(2)}) collective-permute-start(bf16[48,16,1]{2,1,0:T(8,128)(2,1)S(1)} %get-tuple-element.121), channel_id=1, source_target_pairs={{0,1},{1,2},{2,3},{3,4},{4,5},{5,6},{6,7},{7,8},{8,9},{9,10},{10,1... | collective-permute-start | bytes 4616 | tf_op jit(solution)/shard_map/ppermute | solution.py:18
  411.2 36.5 %collective-permute-start.2 = (bf16[48,1,256]{2,1,0:T(2,128)(2,1)S(1)}, bf16[48,1,256]{2,1,0:T(2,128)(2,1)S(1)}, u32[]{:S(2)}, u32[]{:S(2)}) collective-permute-start(bf16[48,1,256]{2,1,0:T(2,128)(2,1)S(1)} %get-tuple-element.120), channel_id=1, source_target_pairs={{64,0},{128,64},{192,128},{0,192},{65,1},{129,65},{193,129},{1,193... | collective-permute-start | bytes 73736 | tf_op jit(solution)/shard_map/ppermute | solution.py:19
  412.8 34.9 %collective-permute-start.1 = (bf16[48,1,256]{2,1,0:T(2,128)(2,1)S(1)}, bf16[48,1,256]{2,1,0:T(2,128)(2,1)S(1)}, u32[]{:S(2)}, u32[]{:S(2)}) collective-permute-start(bf16[48,1,256]{2,1,0:T(2,128)(2,1)S(1)} %get-tuple-element.119), channel_id=1, source_target_pairs={{0,64},{64,128},{128,192},{192,0},{1,65},{65,129},{129,193},{193,1... | collective-permute-start | bytes 73736 | tf_op jit(solution)/shard_map/ppermute | solution.py:18
  454.2 14.9 %copy-start.9 = (bf16[48,16,256]{0,2,1:T(8,128)(2,1)S(1)}, bf16[48,16,256]{0,2,1:T(8,128)(2,1)}, u32[]{:S(2)}) copy-start(bf16[48,16,256]{0,2,1:T(8,128)(2,1)} %copy-done.8) | copy-start | bytes 1179652
  469.1 6.1 %copy-start.7 = (f32[48,18,258]{2,1,0:T(8,128)S(1)}, f32[48,18,258]{2,1,0:T(8,128)}, u32[]{:S(2)}) copy-start(f32[48,18,258]{2,1,0:T(8,128)} %fusion.55) | copy-start | bytes 2674948
  476.1 12.0 %collective-permute-start.6 = (bf16[48,1,256]{2,1,0:T(2,128)(2,1)S(1)}, bf16[48,1,256]{2,1,0:T(2,128)(2,1)S(1)}, u32[]{:S(2)}, u32[]{:S(2)}) collective-permute-start(bf16[48,1,256]{2,1,0:T(2,128)(2,1)S(1)} %get-tuple-element.116), channel_id=1, source_target_pairs={{64,0},{128,64},{192,128},{0,192},{65,1},{129,65},{193,129},{1,193... | collective-permute-start | bytes 73736 | tf_op jit(solution)/shard_map/ppermute | solution.py:19
  477.7 10.4 %collective-permute-start.5 = (bf16[48,1,256]{2,1,0:T(2,128)(2,1)S(1)}, bf16[48,1,256]{2,1,0:T(2,128)(2,1)S(1)}, u32[]{:S(2)}, u32[]{:S(2)}) collective-permute-start(bf16[48,1,256]{2,1,0:T(2,128)(2,1)S(1)} %get-tuple-element.115), channel_id=1, source_target_pairs={{0,64},{64,128},{128,192},{192,0},{1,65},{65,129},{129,193},{193,1... | collective-permute-start | bytes 73736 | tf_op jit(solution)/shard_map/ppermute | solution.py:18
  479.5 3.3 collective-permute-start.7
  479.6 8.5 %collective-permute-start.4 = (bf16[48,16,1]{2,1,0:T(8,128)(2,1)S(1)}, bf16[48,16,1]{2,1,0:T(8,128)(2,1)S(1)}, u32[]{:S(2)}, u32[]{:S(2)}) collective-permute-start(bf16[48,16,1]{2,1,0:T(8,128)(2,1)S(1)} %get-tuple-element.117), channel_id=1, source_target_pairs={{0,1},{1,2},{2,3},{3,4},{4,5},{5,6},{6,7},{7,8},{8,9},{9,10},{10,1... | collective-permute-start | bytes 4616 | tf_op jit(solution)/shard_map/ppermute | solution.py:18
  (55 other events, 78.0 us)
where the time goes:
time: 500 us; the launch traced here: 491 us
  other arithmetic  246 us (49%)
  local copies, waits for them, and re-layouts  142 us (28%)
  starting transfers between devices  52.6 us (11%)
  waiting for transfers between devices  41.2 us (8%)
  blocking collectives  6.15 us (1%)
    scatter-add x1, other arithmetic, on_device(): jax.ops.segment_sum(jnp.ones((width,), jnp.float32), received, num_segmen...  57.9 us
    scatter-add x1, other arithmetic, on_device(): jax.ops.segment_sum(jnp.transpose(incoming.astype(jnp.float32)), received...  44.4 us
    ppermute x4, waiting for transfers between devices, with_halo(): lax.ppermute(leading, axis, [(b, a) for a, b in up])  30.6 us
    exp x14, other arithmetic, one_block(): trans = jnp.exp(-tau)  29.3 us
    rev x14, local copies, waits for them, and re-layouts, one_block(): up = recur(trans[::-1], source[::-1], 0.3 * down[-1])[::-1]  28 us
    gather x1, local copies, waits for them, and re-layouts, on_device(): jnp.concatenate([heat_c, hmean], 0)[:, jnp.minimum(received, owned - 1)]  28 us
    add x14, other arithmetic, recur(): part_now = coef4[:, inner] * part_now + source4[:, inner]  22.7 us
    while x161, local copies, waits for them, and re-layouts  22.6 us
  transfers between devices with their start and end apart: 11, of which 4 were waited for; matrix products, arithmetic and copies ran while one was open for 16% of the time, Pallas kernels for 0%

commit v1 on v0

v1 whole, which is shorter than its diff:
```python
import functools
import jax
import jax.numpy as jnp
from jax import lax
from jax.experimental import pallas as pl
from jax.experimental.pallas import tpu as pltpu
from jax.sharding import PartitionSpec as P

F32 = jnp.float32
BF16 = jnp.bfloat16
LEV = 48
G = 112
ROWS = 16
COLS = 256
OWNED = 1024
TILES = 64
CAP = 128
PAIRS = TILES // 2
BLK_ROW = 96
LOW_ROW = 97
ONE_ROW = 98
SEND = 104
WIDE = 112
GB = 8
VMEM = 56 * 1024 * 1024


def params():
    return pltpu.CompilerParams(vmem_limit_bytes=VMEM)


def whole(n):
    return [pl.BlockSpec(memory_space=pltpu.VMEM)] * n


def pack_kernel(temp_ref, humid_ref, parent_ref, send_ref, slot_ref, x_ref, b_ref, pair_ref):
    sub = lax.broadcasted_iota(jnp.int32, (COLS, COLS), 0)
    lane = lax.broadcasted_iota(jnp.int32, (COLS, COLS), 1)
    before = (sub < lane).astype(BF16)
    ones = jnp.ones((COLS, COLS), BF16)
    sub64 = lax.broadcasted_iota(jnp.int32, (TILES, COLS), 0)
    carry = jnp.zeros((TILES, COLS), F32)
    sub16 = lax.broadcasted_iota(jnp.int32, (16, COLS), 0)
    for r in range(ROWS):
        parent = parent_ref[r : r + 1, :]
        owner = parent // OWNED
        local = parent % OWNED
        hit = jnp.where(owner == sub64, 1.0, 0.0).astype(F32)
        hit16 = hit.astype(BF16)
        rank = jnp.dot(hit16, before, preferred_element_type=F32) + carry
        carry = carry + jnp.dot(hit16, ones, preferred_element_type=F32)
        position = jnp.sum(hit * rank, axis=0, keepdims=True).astype(jnp.int32)
        slot = owner * CAP + position
        slot_ref[r : r + 1, :] = slot
        cols = pl.ds(r * COLS, COLS)
        x_ref[0:LEV, cols] = temp_ref[r]
        x_ref[LEV : 2 * LEV, cols] = humid_ref[r]
        blk = (local // 256 + 1).astype(F32)
        low = (local % 256).astype(F32)
        extra = jnp.where(sub16 == 0, blk, jnp.where(sub16 == 1, low, jnp.where(sub16 == 2, 1.0, 0.0)))
        x_ref[2 * LEV : WIDE, cols] = extra.astype(BF16)
        onehot = jnp.where((slot % 256) == sub, 1.0, 0.0).astype(F32)
        b_ref[cols, :] = onehot.T.astype(BF16)
        pair_ref[:, cols] = jnp.broadcast_to((slot // 256).astype(F32), (16, COLS)).astype(BF16)

    def one_pair(p, _):
        mask = pair_ref[...] == p.astype(F32).astype(BF16)
        values = x_ref[...].reshape(WIDE // 16, 16, ROWS * COLS)
        chosen = jnp.where(mask[None], values, jnp.zeros_like(values)).reshape(WIDE, ROWS * COLS)
        moved = jnp.dot(chosen, b_ref[...], preferred_element_type=F32)
        moved = moved[0:SEND].astype(BF16)
        send_ref[2 * p] = moved[:, 0:CAP]
        send_ref[2 * p + 1] = moved[:, CAP : 2 * CAP]
        return 0

    lax.fori_loop(0, PAIRS, one_pair, 0)


def pack(temp_t, humid_t, parent):
    return pl.pallas_call(
        pack_kernel,
        out_shape=(
            jax.ShapeDtypeStruct((TILES, SEND, CAP), BF16),
            jax.ShapeDtypeStruct((ROWS, COLS), jnp.int32),
        ),
        in_specs=whole(3),
        out_specs=tuple(whole(2)),
        scratch_shapes=[
            pltpu.VMEM((WIDE, ROWS * COLS), BF16),
            pltpu.VMEM((ROWS * COLS, COLS), BF16),
            pltpu.VMEM((16, ROWS * COLS), BF16),
        ],
        compiler_params=params(),
    )(temp_t, humid_t, parent)


def owner_kernel(recv_ref, kabs_ref, planck_ref, top_ref, out_ref,
                 b_ref, absorb_ref, emit_ref, hmean_ref, net_ref, trans_ref, sum_ref, q_ref):
    sub = lax.broadcasted_iota(jnp.int32, (256, CAP), 0).astype(F32)

    sum_ref[...] = jnp.zeros_like(sum_ref)

    def one_pair(p, _):
        lhs = []
        for h in range(2):
            got = recv_ref[2 * p + h].astype(F32)
            low = got[LOW_ROW : LOW_ROW + 1]
            blk = got[BLK_ROW : BLK_ROW + 1]
            b_ref[p, :, h * CAP : (h + 1) * CAP] = jnp.where(low == sub, 1.0, 0.0).astype(BF16)
            lhs.append(
                jnp.concatenate(
                    [jnp.where(blk == float(b + 1), got, 0.0).astype(BF16) for b in range(4)], axis=0
                )
            )
        both = jnp.concatenate(lhs, axis=1)
        sum_ref[...] += lax.dot_general(
            both, b_ref[p], (((1,), (1,)), ((), ())), preferred_element_type=F32
        )
        return 0

    lax.fori_loop(0, PAIRS, one_pair, 0)

    rows = []
    for b in range(4):
        for h in range(2):
            rows.append(sum_ref[b * SEND + ONE_ROW : b * SEND + ONE_ROW + 1, h * CAP : (h + 1) * CAP])
    inv = 1.0 / jnp.maximum(jnp.concatenate(rows, axis=0), 1.0)
    for b in range(4):
        for h in range(2):
            lanes = slice(h * CAP, (h + 1) * CAP)
            emit_ref[:, 2 * b + h, :] = sum_ref[b * SEND : b * SEND + LEV, lanes]
            hmean_ref[:, 2 * b + h, :] = sum_ref[b * SEND + LEV : b * SEND + 2 * LEV, lanes]
    hc = hmean_ref[...] * inv[None]
    absorb_ref[...] = jnp.exp(0.5 * hc)
    emit_ref[...] = jnp.exp(0.25 * (emit_ref[...] * inv[None]))
    hmean_ref[...] = hc
    net_ref[...] = jnp.zeros_like(net_ref)

    def one_block(gb, top_sum):
        first = gb * GB
        tops = [top_ref[first + j] for j in range(GB)]
        planck = [planck_ref[first + j] for j in range(GB)]

        def down_step(k, state):
            absorb = absorb_ref[k]
            emit = emit_ref[k]
            new = []
            total = None
            for j in range(GB):
                t = jnp.exp(absorb * (-kabs_ref[first + j, k]))
                trans_ref[k, j] = t
                s = emit * planck[j]
                d = s + t * (state[j] - s)
                new.append(d)
                total = d if total is None else total + d
            net_ref[k] += total
            return tuple(new)

        start = tuple(jnp.full((8, 128), tops[j], F32) for j in range(GB))
        down = lax.fori_loop(0, LEV, down_step, start, unroll=4)

        def up_step(i, state):
            k = LEV - 1 - i
            emit = emit_ref[k]
            new = []
            total = None
            for j in range(GB):
                s = emit * planck[j]
                u = s + trans_ref[k, j] * (state[j] - s)
                new.append(u)
                total = u if total is None else total + u
            net_ref[k] -= total
            return tuple(new)

        up = lax.fori_loop(0, LEV, up_step, tuple(0.3 * d for d in down), unroll=4)
        for j in range(GB):
            top_sum = top_sum + (tops[j] - up[j])
        return top_sum

    top_net = lax.fori_loop(0, G // GB, one_block, jnp.zeros((8, 128), F32))
    net = net_ref[...]
    prev = jnp.concatenate([top_net[None], net[:-1]], axis=0)
    heat = ((prev - net) * (LEV / G)).astype(BF16).astype(F32)
    hm = hmean_ref[...].astype(BF16).astype(F32)
    net_ref[...] = heat - 0.5 * hm
    for b in range(4):
        for h in range(2):
            q_ref[b * LEV : (b + 1) * LEV, h * CAP : (h + 1) * CAP] = net_ref[:, 2 * b + h, :].astype(BF16)

    def answer(p, _):
        both = jnp.dot(q_ref[...], b_ref[p], preferred_element_type=F32)
        for h in range(2):
            lanes = slice(h * CAP, (h + 1) * CAP)
            blk = recv_ref[2 * p + h, BLK_ROW : BLK_ROW + 8, :].astype(F32)[0:1]
            got = jnp.zeros((LEV, CAP), F32)
            for b in range(4):
                got = jnp.where(blk == float(b + 1), both[b * LEV : (b + 1) * LEV, lanes], got)
            out_ref[2 * p + h] = got.astype(BF16)
        return 0

    lax.fori_loop(0, PAIRS, answer, 0)


def owner_step(recv, kabs, planck, top_flux):
    smem = pl.BlockSpec(memory_space=pltpu.SMEM)
    return pl.pallas_call(
        owner_kernel,
        out_shape=jax.ShapeDtypeStruct((TILES, LEV, CAP), BF16),
        in_specs=whole(1) + [smem, smem, smem],
        out_specs=whole(1)[0],
        scratch_shapes=[
            pltpu.VMEM((PAIRS, 256, 256), BF16),
            pltpu.VMEM((LEV, 8, 128), F32),
            pltpu.VMEM((LEV, 8, 128), F32),
            pltpu.VMEM((LEV, 8, 128), F32),
            pltpu.VMEM((LEV, 8, 128), F32),
            pltpu.VMEM((LEV, GB, 8, 128), F32),
            pltpu.VMEM((4 * SEND, 256), F32),
            pltpu.VMEM((4 * LEV, 256), BF16),
        ],
        compiler_params=params(),
    )(recv, kabs, planck, top_flux)


def stencil_row(value, above, below, left, right):
    lane = lax.broadcasted_iota(jnp.int32, value.shape, 1)
    west = jnp.where(lane == 0, left, pltpu.roll(value, 1, axis=1))
    east = jnp.where(lane == COLS - 1, right, pltpu.roll(value, COLS - 1, axis=1))
    return value + 0.2 * (above + below + west + east - 4.0 * value)


def stencil_kernel(field_ref, above_ref, below_ref, left_ref, right_ref, out_ref):
    left = left_ref[...].astype(F32)
    right = right_ref[...].astype(F32)
    for r in range(ROWS):
        value = field_ref[r].astype(F32)
        above = (above_ref[...] if r == 0 else field_ref[r - 1]).astype(F32)
        below = (below_ref[...] if r == ROWS - 1 else field_ref[r + 1]).astype(F32)
        out_ref[r] = stencil_row(
            value, above, below, left[:, r : r + 1], right[:, r : r + 1]
        ).astype(BF16)


def stencil(field, halo):
    return pl.pallas_call(
        stencil_kernel,
        out_shape=jax.ShapeDtypeStruct((ROWS, LEV, COLS), BF16),
        in_specs=whole(5),
        out_specs=whole(1)[0],
        compiler_params=params(),
    )(field, *halo)


def unpack_kernel(ret_ref, slot_ref, first_ref, humid_ref, second_ref, left_ref, right_ref, r_ref):
    sub = lax.broadcasted_iota(jnp.int32, (256, COLS), 0)
    lane = lax.broadcasted_iota(jnp.int32, (LEV, 128), 1)
    for p in range(PAIRS):
        for h in range(2):
            r_ref[p * LEV : (p + 1) * LEV, h * CAP : (h + 1) * CAP] = ret_ref[2 * p + h]
    left_ref[...] = jnp.zeros_like(left_ref)
    right_ref[...] = jnp.zeros_like(right_ref)

    def one_row(r, _):
        slot = slot_ref[pl.ds(r, 1), :]
        onehot = jnp.where((slot % 256) == sub, 1.0, 0.0).astype(BF16)
        pair = slot // 256
        moved = jnp.dot(r_ref[...], onehot, preferred_element_type=F32)
        q = jnp.zeros((LEV, COLS), F32)
        for p in range(PAIRS):
            q = jnp.where(pair == p, moved[p * LEV : (p + 1) * LEV], q)
        heat = q + 0.5 * humid_ref[r].astype(F32)
        second = (first_ref[r].astype(F32) + 0.5 * heat).astype(BF16)
        second_ref[r] = second
        second = second.astype(F32)
        left_ref[...] = jnp.where(lane == r, second[:, 0:1], left_ref[...].astype(F32)).astype(BF16)
        right_ref[...] = jnp.where(lane == r, second[:, COLS - 1 : COLS], right_ref[...].astype(F32)).astype(BF16)
        return 0

    lax.fori_loop(0, ROWS, one_row, 0)


def unpack(ret, slot, first, humid_t):
    edge = jax.ShapeDtypeStruct((LEV, 128), BF16)
    return pl.pallas_call(
        unpack_kernel,
        out_shape=(jax.ShapeDtypeStruct((ROWS, LEV, COLS), BF16), edge, edge),
        in_specs=whole(4),
        out_specs=tuple(whole(3)),
        scratch_shapes=[pltpu.VMEM((PAIRS * LEV, 256), BF16)],
        compiler_params=params(),
    )(ret, slot, first, humid_t)


def exchange(top, bottom, left, right):
    grp = lax.axis_size("grp")
    tile = lax.axis_size("tile")
    up = [(i, (i + 1) % grp) for i in range(grp)]
    along = [(i, (i + 1) % tile) for i in range(tile)]
    above = lax.ppermute(bottom, "grp", up)
    below = lax.ppermute(top, "grp", [(b, a) for a, b in up])
    west = lax.ppermute(right, "tile", along)
    east = lax.ppermute(left, "tile", [(b, a) for a, b in along])
    return above, below, west, east


def edge_columns(column):
    return jnp.pad(jnp.transpose(column), ((0, 0), (0, 128 - ROWS)))


def on_device(temp, humid, parent, kabs, planck, top_flux):
    temp_t = jnp.transpose(temp, (1, 0, 2))
    humid_t = jnp.transpose(humid, (1, 0, 2))
    halo = exchange(
        temp_t[0], temp_t[ROWS - 1], edge_columns(temp_t[:, :, 0]), edge_columns(temp_t[:, :, COLS - 1])
    )
    send, slot = pack(temp_t, humid_t, parent)
    recv = lax.all_to_all(send, "tile", split_axis=0, concat_axis=0, tiled=True)
    first = stencil(temp_t, halo)
    answer = owner_step(recv, kabs, planck, top_flux)
    ret = lax.all_to_all(answer, "tile", split_axis=0, concat_axis=0, tiled=True)
    second, left, right = unpack(ret, slot, first, humid_t)
    halo2 = exchange(second[0], second[ROWS - 1], left, right)
    return jnp.transpose(stencil(second, halo2), (1, 0, 2))


def solution(mesh):
    placed = (P(None, "grp", "tile"), P(None, "grp", "tile"), P("grp", "tile"), P(), P(), P())
    return jax.shard_map(
        on_device, mesh=mesh, in_specs=placed, out_specs=P(None, "grp", "tile"), check_vma=False
    )
```

time: 500 us -> 173 us (0.35); the launches traced: 491 us -> 172 us
  other arithmetic: 246 us -> 0 us
  local copies, waits for them, and re-layouts: 142 us -> 26.7 us
  Pallas kernels: 0 us -> 67.1 us
  starting transfers between devices: 52.6 us -> 33.3 us
  blocking collectives: 6.15 us -> 0 us
    scatter-add x2 -> x0, other arithmetic: 102 us -> none  [the longest x1 57.9 us: on_device(): jax.ops.segment_sum(jnp.ones((width,), jnp.float32), received, num_segmen...]
    pallas_call x0 -> x5, Pallas kernels: none -> 67.1 us  [the longest x1 34.2 us: owner_step(): pl.pallas_call(owner_kernel, out_shape=jax.ShapeDtypeStruct((TILES, LEV,...]
    gather x2 -> x0, local copies, waits for them, and re-layouts: 42.8 us -> none  [the longest x1 28 us: on_device(): jnp.concatenate([heat_c, hmean], 0)[:, jnp.minimum(received, owned - 1)]]
    all_to_all x3 -> x2, waiting for transfers between devices: 0.01 us -> 41.5 us  [the longest x1 41.5 us: on_device(): recv = lax.all_to_all(send, 'tile', split_axis=0, concat_axis=0, tiled=True)]
    ppermute x8, waiting for transfers between devices: 41.2 us -> 3.03 us  [the longest x2 2.95 us: exchange(): west = lax.ppermute(right, 'tile', along)]
    exp x14 -> x0, other arithmetic: 29.3 us -> none  [one_block(): trans = jnp.exp(-tau)]
    rev x14 -> x0, local copies, waits for them, and re-layouts: 28 us -> none  [one_block(): up = recur(trans[::-1], source[::-1], 0.3 * down[-1])[::-1]]
    another operation x31 -> x0, other arithmetic: 23.1 us -> none
  transfers between devices with their start and end apart: 11 -> 10, of which waited for: 4 -> 3; matrix products, arithmetic and copies ran while one was open for 16% -> 10% of each run, Pallas kernels for 0% -> 1%
where the time goes in v1:
time: 173 us; the launch traced here: 172 us
  Pallas kernels  67.1 us (39%)
  waiting for transfers between devices  44.5 us (26%)
  starting transfers between devices  33.3 us (19%)
  local copies, waits for them, and re-layouts  26.7 us (15%)
    all_to_all x1, waiting for transfers between devices, on_device(): recv = lax.all_to_all(send, 'tile', split_axis=0, concat_axis=0, tiled=True)  41.5 us
    pallas_call x1, Pallas kernels, owner_step(): pl.pallas_call(owner_kernel, out_shape=jax.ShapeDtypeStruct((TILES, LEV,...  34.2 us
    pallas_call x1, Pallas kernels, pack(): pl.pallas_call(pack_kernel, out_shape=(jax.ShapeDtypeStruct((TILES, SEND,...  18.3 us
    all_to_all x1, starting transfers between devices, on_device(): recv = lax.all_to_all(send, 'tile', split_axis=0, concat_axis=0, tiled=True)  12.2 us
    pallas_call x1, Pallas kernels, unpack(): pl.pallas_call(unpack_kernel, out_shape=(jax.ShapeDtypeStruct((ROWS, LEV,...  10.1 us
    ppermute x2, starting transfers between devices, exchange(): east = lax.ppermute(left, 'tile', [(b, a) for a, b in along])  10.1 us
    unnamed x25, local copies, waits for them, and re-layouts  9.13 us
    slice x2, local copies, waits for them, and re-layouts, on_device(): temp_t[0]  8.56 us
  transfers between devices with their start and end apart: 10, of which 3 were waited for; matrix products, arithmetic and copies ran while one was open for 10% of the time, Pallas kernels for 1%

profile of v1, /device:TPU:6, one launch (start us, length us, event | category | flops | bytes accessed | tf_op | source)
XLA Modules:
  0.0 171.8 jit_solution(14548377790988034521)
XLA Ops:
  0.0 0.0 copy-start.2
  0.0 1.9 %copy.17.temp_ref.field_ref = bf16[16,48,256]{2,1,0:T(8,128)(2,1)} copy(bf16[16,48,256]{2,0,1:T(8,128)(2,1)} %bitcast.24) | data formatting | bytes 786432 | tf_op jit(solution)/shard_map/transpose | solution.py:311
  1.9 1.9 %copy.25 = bf16[48,16,256]{2,0,1:T(8,128)(2,1)} copy(bf16[48,16,256]{2,1,0:T(8,128)(2,1)} %param.7) | data formatting | bytes 786432 | tf_op args[1]
  3.8 18.3 %shard_map.64 = (bf16[64,104,128]{2,1,0:T(8,128)(2,1)}, s32[16,256]{1,0:T(8,128)}) custom-call(bf16[16,48,256]{2,1,0:T(8,128)(2,1)} %copy.17.temp_ref.field_ref, bf16[16,48,256]{2,1,0:T(8,128)(2,1)} %bitcast.22, s32[16,256]{1,0:T(8,128)} %parent_ref.1), custom_call_target="tpu_custom_call" | custom-call | tf_op jit(solution)/shard_map/pallas_call | solution.py:80
  22.0 0.0 copy-start.1
  22.0 12.2 %all-to-all-start = ((bf16[64,104,128]{2,1,0:T(8,128)(2,1)}), bf16[64,104,128]{2,1,0:T(8,128)(2,1)S(1)}, u32[]{:S(2)}, u32[]{:S(2)}) async-start(bf16[64,104,128]{2,1,0:T(8,128)(2,1)} %get-tuple-element.10), calls=%async_computation | async-start | bytes 3407872 | tf_op jit(solution)/shard_map/all_to_all | solution.py:317
  34.3 0.0 copy-done.2
  34.3 0.7 copy.18.kabs_ref
  35.0 41.5 %all-to-all-done.recv_ref = bf16[64,104,128]{2,1,0:T(8,128)(2,1)S(1)} async-done(((bf16[64,104,128]{2,1,0:T(8,128)(2,1)}), bf16[64,104,128]{2,1,0:T(8,128)(2,1)S(1)}, u32[]{:S(2)}, u32[]{:S(2)}) %all-to-all-start) | async-done | bytes 1703968 | tf_op jit(solution)/shard_map/all_to_all | solution.py:317
  76.5 0.0 copy-start
  76.5 1.2 copy-done
  77.7 34.2 %shard_map.65 = bf16[64,48,128]{2,1,0:T(8,128)(2,1)} custom-call(bf16[64,104,128]{2,1,0:T(8,128)(2,1)} %copy-done, f32[112,48]{1,0:T(8,128)} %copy.18.kabs_ref, f32[112]{0:T(128)} %planck_ref.1, f32[112]{0:T(128)} %top_ref.1), custom_call_target="tpu_custom_call" | custom-call | tf_op jit(solution)/shard_map/pallas_call | solution.py:206
  111.9 6.7 %all-to-all-start.1 = ((bf16[64,48,128]{2,1,0:T(8,128)(2,1)}), bf16[64,48,128]{2,1,0:T(8,128)(2,1)}, u32[]{:S(2)}, u32[]{:S(2)}) async-start(bf16[64,48,128]{2,1,0:T(8,128)(2,1)} %shard_map.65), calls=%async_computation.1 | async-start | bytes 1572864 | tf_op jit(solution)/shard_map/all_to_all | solution.py:320
  118.6 0.0 copy-done.1
  118.6 2.9 %copy.15 = bf16[48,16,256]{1,0,2:T(8,128)(2,1)S(1)} copy(bf16[48,16,256]{2,1,0:T(8,128)(2,1)S(1)} %copy-done.1) | data formatting | bytes 786432 | tf_op args[0]
  121.6 4.0 %fusion = (bf16[1,48,256]{0,1,2:T(8,128)(2,1)}, bf16[1,48,256]{0,1,2:T(8,128)(2,1)}) fusion(bf16[16,48,256]{0,1,2:T(8,128)(2,1)S(1)} %bitcast.20), kind=kLoop, calls=%fused_computation.5 | loop fusion | bytes 98304 | tf_op jit(solution)/shard_map/slice | solution.py:314
  125.6 4.5 %copy.19 = bf16[1,48,256]{2,1,0:T(8,128)(2,1)S(1)} copy(bf16[1,48,256]{0,1,2:T(8,128)(2,1)} %get-tuple-element.18) | data formatting | bytes 49152 | tf_op jit(solution)/shard_map/slice | solution.py:314
  130.1 0.6 collective-permute-start
  130.7 4.5 %copy.20 = bf16[1,48,256]{2,1,0:T(8,128)(2,1)S(1)} copy(bf16[1,48,256]{0,1,2:T(8,128)(2,1)} %get-tuple-element.17) | data formatting | bytes 49152 | tf_op jit(solution)/shard_map/slice | solution.py:314
  135.2 1.6 collective-permute-start.1
  136.9 0.1 collective-permute-start.2
  137.0 5.0 %collective-permute-start.3 = (bf16[48,128]{1,0:T(8,128)(2,1)S(1)}, bf16[48,128]{1,0:T(8,128)(2,1)S(1)}, u32[]{:S(2)}, u32[]{:S(2)}) collective-permute-start(bf16[48,128]{1,0:T(8,128)(2,1)S(1)} %pad.8), channel_id=1, source_target_pairs={{1,0},{2,1},{3,2},{4,3},{5,4},{6,5},{7,6},{8,7},{9,8},{10,9},{11,1... | collective-permute-start | bytes 36872 | tf_op jit(solution)/shard_map/ppermute | solution.py:302
  142.0 1.4 collective-permute-done.2.left_ref
  143.4 0.0 collective-permute-done.3.right_ref
  143.4 0.0 collective-permute-done.above_ref
  143.4 0.0 collective-permute-done.1.below_ref
  143.4 0.5 copy-done.7
  144.0 0.0 copy-done.9
  144.0 0.0 copy-done.3
  144.0 0.6 copy-done.4
  144.6 2.3 %shard_map.66.first_ref = bf16[16,48,256]{2,1,0:T(8,128)(2,1)} custom-call(bf16[16,48,256]{2,1,0:T(8,128)(2,1)} %copy.17.temp_ref.field_ref, bf16[48,256]{1,0:T(8,128)(2,1)} %copy-done.3, bf16[48,256]{1,0:T(8,128)(2,1)} %copy-done.4, bf16[48,128]{1,0:T(8,128)(2,1)} %copy-done.7, bf16[48,128]{1,0:T(8,128)(2,1)} %copy-done.9), custom_call_target="tpu_custom_call" | custom-call | tf_op jit(solution)/shard_map/pallas_call | solution.py:245
  146.9 0.0 all-to-all-done.1.ret_ref
  146.9 10.1 %shard_map.67 = (bf16[16,48,256]{2,1,0:T(8,128)(2,1)}, bf16[48,128]{1,0:T(8,128)(2,1)}, bf16[48,128]{1,0:T(8,128)(2,1)}) custom-call(bf16[64,48,128]{2,1,0:T(8,128)(2,1)} %all-to-all-done.1.ret_ref, s32[16,256]{1,0:T(8,128)} %get-tuple-element.11.slot_ref, bf16[16,48,256]{2,1,0:T(8,128)(2,1)} %shard_map.66.first_ref, bf16[16,48,256]{2,1,0:T(8,128)(2,1)} %bitcast.23), custom_call_target="tpu_custom_call" | custom-call | tf_op jit(solution)/shard_map/pallas_call | solution.py:284
  157.0 0.8 slice_bitcast_fusion
  157.8 1.7 collective-permute-start.4
  159.5 0.3 collective-permute-start.5
  159.8 0.0 collective-permute-start.6
  159.8 5.1 %collective-permute-start.7 = (bf16[48,128]{1,0:T(8,128)(2,1)}, bf16[48,128]{1,0:T(8,128)(2,1)S(1)}, u32[]{:S(2)}, u32[]{:S(2)}) collective-permute-start(bf16[48,128]{1,0:T(8,128)(2,1)} %get-tuple-element.14), channel_id=1, source_target_pairs={{1,0},{2,1},{3,2},{4,3},{5,4},{6,5},{7,6},{8,7},{9,8},{10,9},{11,1... | collective-permute-start | bytes 36872 | tf_op jit(solution)/shard_map/ppermute | solution.py:302
  164.9 1.6 collective-permute-done.6.left_ref
  166.5 0.0 collective-permute-done.7.right_ref
  166.5 0.0 collective-permute-done.4.above_ref
  166.5 0.0 collective-permute-done.5.below_ref
  166.5 0.6 copy-done.8
  167.1 0.0 copy-done.10
  167.1 0.0 copy-done.5
  167.1 0.6 copy-done.6
  167.7 2.3 %shard_map.68 = bf16[16,48,256]{2,1,0:T(8,128)(2,1)} custom-call(bf16[16,48,256]{2,1,0:T(8,128)(2,1)} %get-tuple-element.12.field_ref, bf16[48,256]{1,0:T(8,128)(2,1)} %copy-done.5, bf16[48,256]{1,0:T(8,128)(2,1)} %copy-done.6, bf16[48,128]{1,0:T(8,128)(2,1)} %copy-done.8, bf16[48,128]{1,0:T(8,128)(2,1)} %copy-done.10), custom_call_target="tpu_custom_call" | custom-call | tf_op jit(solution)/shard_map/pallas_call | solution.py:245
  170.0 1.9 %copy.22 = bf16[48,16,256]{2,1,0:T(8,128)(2,1)} copy(bf16[48,16,256]{2,0,1:T(8,128)(2,1)} %bitcast.25) | data formatting | bytes 786432 | tf_op jit(solution)/shard_map/transpose | solution.py:323
  (11 shorter events, 0.0 us)
Async XLA Ops:
  0.0 34.3 %copy-start.2 = (f32[112,48]{0,1:T(8,128)S(1)}, f32[112,48]{0,1:T(8,128)}, u32[]{:S(2)}) copy-start(f32[112,48]{0,1:T(8,128)} %param.9) | copy-start | bytes 64516
  22.0 96.6 %copy-start.1 = (bf16[48,16,256]{2,1,0:T(8,128)(2,1)S(1)}, bf16[48,16,256]{2,1,0:T(8,128)(2,1)}, u32[]{:S(2)}) copy-start(bf16[48,16,256]{2,1,0:T(8,128)(2,1)} %param.6) | copy-start | bytes 1179652
  22.0 54.5 %all-to-all-start = ((bf16[64,104,128]{2,1,0:T(8,128)(2,1)}), bf16[64,104,128]{2,1,0:T(8,128)(2,1)S(1)}, u32[]{:S(2)}, u32[]{:S(2)}) async-start(bf16[64,104,128]{2,1,0:T(8,128)(2,1)} %get-tuple-element.10), calls=%async_computation | async-start | bytes 3407872 | tf_op jit(solution)/shard_map/all_to_all | solution.py:317
  76.5 1.2 copy-start
  111.9 35.0 %all-to-all-start.1 = ((bf16[64,48,128]{2,1,0:T(8,128)(2,1)}), bf16[64,48,128]{2,1,0:T(8,128)(2,1)}, u32[]{:S(2)}, u32[]{:S(2)}) async-start(bf16[64,48,128]{2,1,0:T(8,128)(2,1)} %shard_map.65), calls=%async_computation.1 | async-start | bytes 1572864 | tf_op jit(solution)/shard_map/all_to_all | solution.py:320
  130.1 13.3 %collective-permute-start = (bf16[48,256]{1,0:T(8,128)(2,1)S(1)}, bf16[48,256]{1,0:T(8,128)(2,1)S(1)}, u32[]{:S(2)}, u32[]{:S(2)}) collective-permute-start(bf16[48,256]{1,0:T(8,128)(2,1)S(1)} %bitcast.26), channel_id=1, source_target_pairs={{0,64},{64,128},{128,192},{192,0},{1,65},{65,129},{129,193},{193,1... | collective-permute-start | bytes 73736 | tf_op jit(solution)/shard_map/ppermute | solution.py:299
  135.2 8.2 %collective-permute-start.1 = (bf16[48,256]{1,0:T(8,128)(2,1)S(1)}, bf16[48,256]{1,0:T(8,128)(2,1)S(1)}, u32[]{:S(2)}, u32[]{:S(2)}) collective-permute-start(bf16[48,256]{1,0:T(8,128)(2,1)S(1)} %bitcast.27), channel_id=1, source_target_pairs={{64,0},{128,64},{192,128},{0,192},{65,1},{129,65},{193,129},{1,193... | collective-permute-start | bytes 73736 | tf_op jit(solution)/shard_map/ppermute | solution.py:300
  136.9 6.5 %collective-permute-start.2 = (bf16[48,128]{1,0:T(8,128)(2,1)S(1)}, bf16[48,128]{1,0:T(8,128)(2,1)S(1)}, u32[]{:S(2)}, u32[]{:S(2)}) collective-permute-start(bf16[48,128]{1,0:T(8,128)(2,1)S(1)} %pad.7), channel_id=1, source_target_pairs={{0,1},{1,2},{2,3},{3,4},{4,5},{5,6},{6,7},{7,8},{8,9},{9,10},{10,1... | collective-permute-start | bytes 36872 | tf_op jit(solution)/shard_map/ppermute | solution.py:301
  137.0 6.5 %collective-permute-start.3 = (bf16[48,128]{1,0:T(8,128)(2,1)S(1)}, bf16[48,128]{1,0:T(8,128)(2,1)S(1)}, u32[]{:S(2)}, u32[]{:S(2)}) collective-permute-start(bf16[48,128]{1,0:T(8,128)(2,1)S(1)} %pad.8), channel_id=1, source_target_pairs={{1,0},{2,1},{3,2},{4,3},{5,4},{6,5},{7,6},{8,7},{9,8},{10,9},{11,1... | collective-permute-start | bytes 36872 | tf_op jit(solution)/shard_map/ppermute | solution.py:302
  143.4 0.6 copy-start.7
  143.4 0.6 copy-start.9
  143.4 0.6 copy-start.3
  144.0 0.6 copy-start.4
  157.8 8.7 %collective-permute-start.4 = (bf16[48,256]{1,0:T(8,128)(2,1)S(1)}, bf16[48,256]{1,0:T(8,128)(2,1)S(1)}, u32[]{:S(2)}, u32[]{:S(2)}) collective-permute-start(bf16[48,256]{1,0:T(8,128)(2,1)S(1)} %get-tuple-element.20), channel_id=1, source_target_pairs={{0,64},{64,128},{128,192},{192,0},{1,65},{65,129},{129,193},{193,1... | collective-permute-start | bytes 73736 | tf_op jit(solution)/shard_map/ppermute | solution.py:299
  159.5 7.0 %collective-permute-start.5 = (bf16[48,256]{1,0:T(8,128)(2,1)S(1)}, bf16[48,256]{1,0:T(8,128)(2,1)S(1)}, u32[]{:S(2)}, u32[]{:S(2)}) collective-permute-start(bf16[48,256]{1,0:T(8,128)(2,1)S(1)} %get-tuple-element.19), channel_id=1, source_target_pairs={{64,0},{128,64},{192,128},{0,192},{65,1},{129,65},{193,129},{1,193... | collective-permute-start | bytes 73736 | tf_op jit(solution)/shard_map/ppermute | solution.py:300
  159.8 6.7 %collective-permute-start.6 = (bf16[48,128]{1,0:T(8,128)(2,1)}, bf16[48,128]{1,0:T(8,128)(2,1)S(1)}, u32[]{:S(2)}, u32[]{:S(2)}) collective-permute-start(bf16[48,128]{1,0:T(8,128)(2,1)} %get-tuple-element.13), channel_id=1, source_target_pairs={{0,1},{1,2},{2,3},{3,4},{4,5},{5,6},{6,7},{7,8},{8,9},{9,10},{10,1... | collective-permute-start | bytes 36872 | tf_op jit(solution)/shard_map/ppermute | solution.py:301
  159.8 6.7 %collective-permute-start.7 = (bf16[48,128]{1,0:T(8,128)(2,1)}, bf16[48,128]{1,0:T(8,128)(2,1)S(1)}, u32[]{:S(2)}, u32[]{:S(2)}) collective-permute-start(bf16[48,128]{1,0:T(8,128)(2,1)} %get-tuple-element.14), channel_id=1, source_target_pairs={{1,0},{2,1},{3,2},{4,3},{5,4},{6,5},{7,6},{8,7},{9,8},{10,9},{11,1... | collective-permute-start | bytes 36872 | tf_op jit(solution)/shard_map/ppermute | solution.py:302
  166.5 0.6 copy-start.8
  166.5 0.6 copy-start.10
  166.5 0.6 copy-start.5
  167.1 0.6 copy-start.6

commit v2 on v1

v2 whole, which is shorter than its diff:
```python
import jax
import jax.numpy as jnp
from jax import lax
from jax.experimental import pallas as pl
from jax.experimental.pallas import tpu as pltpu
from jax.sharding import PartitionSpec as P

F32 = jnp.float32
BF16 = jnp.bfloat16
LEV = 48
G = 112
ROWS = 16
COLS = 256
CELLS = ROWS * COLS
OWNED = 1024
TILES = 64
CAP = 128
PAIRS = TILES // 2
BLK_ROW = 96
ONE_ROW = 98
SEND = 104
WIDE = 112
GROUP = 8
GB = 4
LOG2E = 1.4426950408889634
VMEM = 56 * 1024 * 1024


def call(kernel, out_shape, operands, scratch=(), scalars=0):
    vmem = pl.BlockSpec(memory_space=pltpu.VMEM)
    smem = pl.BlockSpec(memory_space=pltpu.SMEM)
    many = isinstance(out_shape, tuple)
    return pl.pallas_call(
        kernel,
        out_shape=out_shape,
        in_specs=[vmem] * (len(operands) - scalars) + [smem] * scalars,
        out_specs=(vmem,) * len(out_shape) if many else vmem,
        scratch_shapes=list(scratch),
        compiler_params=pltpu.CompilerParams(vmem_limit_bytes=VMEM),
    )(*operands)


def pack_kernel(temp_ref, humid_ref, parent_ref, send_ref, slot_ref, t_ref, h_ref, x_ref, b_ref, pair_ref):
    t_ref[...] = temp_ref[...].astype(F32)
    h_ref[...] = humid_ref[...].astype(F32)
    sub = lax.broadcasted_iota(jnp.int32, (COLS, COLS), 0)
    lane = lax.broadcasted_iota(jnp.int32, (COLS, COLS), 1)
    before = (sub < lane).astype(BF16)
    ones = jnp.ones((COLS, COLS), BF16)
    sub64 = lax.broadcasted_iota(jnp.int32, (TILES, COLS), 0)
    sub16 = lax.broadcasted_iota(jnp.int32, (16, COLS), 0)
    parent = parent_ref[...]
    owner = parent // OWNED
    local = parent % OWNED
    blk = (local // 256 + 1).astype(F32)
    low = (local % 256).astype(F32)
    hits = [jnp.where(owner[r : r + 1] == sub64, 1.0, 0.0).astype(F32) for r in range(ROWS)]
    stacked = jnp.concatenate([h.astype(BF16) for h in hits], axis=0)
    ranks = jnp.dot(stacked, before, preferred_element_type=F32)
    totals = jnp.dot(stacked, ones, preferred_element_type=F32)
    carry = jnp.zeros((TILES, COLS), F32)
    position = []
    for r in range(ROWS):
        span = slice(r * TILES, (r + 1) * TILES)
        position.append(jnp.sum(hits[r] * (ranks[span] + carry), axis=0, keepdims=True))
        carry = carry + totals[span]
    slot = owner * CAP + jnp.concatenate(position, axis=0).astype(jnp.int32)
    slot_ref[...] = slot
    pair = (slot // 256).astype(F32)
    within = (slot % 256).astype(F32).T
    lane_f = lane.astype(F32)
    for r in range(ROWS):
        cols = slice(r * COLS, (r + 1) * COLS)
        x_ref[0:LEV, cols] = t_ref[:, r, :].astype(BF16)
        x_ref[LEV : 2 * LEV, cols] = h_ref[:, r, :].astype(BF16)
        extra = jnp.where(
            sub16 == 0, blk[r : r + 1], jnp.where(sub16 == 1, low[r : r + 1], jnp.where(sub16 == 2, 1.0, 0.0))
        )
        x_ref[2 * LEV : WIDE, cols] = extra.astype(BF16)
        b_ref[cols, :] = jnp.where(within[:, r : r + 1] == lane_f, 1.0, 0.0).astype(BF16)
        pair_ref[:, cols] = jnp.broadcast_to(pair[r : r + 1], (16, COLS)).astype(BF16)

    def one_group(step, _):
        values = x_ref[...].reshape(WIDE // 16, 16, CELLS)
        chosen = []
        for j in range(GROUP):
            mask = pair_ref[...] == (step * GROUP + j).astype(F32).astype(BF16)
            chosen.append(jnp.where(mask[None], values, jnp.zeros_like(values)).reshape(WIDE, CELLS))
        moved = jnp.dot(jnp.concatenate(chosen, axis=0), b_ref[...], preferred_element_type=F32)
        for j in range(GROUP):
            p = step * GROUP + j
            part = moved[j * WIDE : j * WIDE + SEND].astype(BF16)
            send_ref[2 * p] = part[:, 0:CAP]
            send_ref[2 * p + 1] = part[:, CAP : 2 * CAP]
        return 0

    lax.fori_loop(0, PAIRS // GROUP, one_group, 0)


def pack(temp, humid, parent):
    return call(
        pack_kernel,
        (
            jax.ShapeDtypeStruct((TILES, SEND, CAP), BF16),
            jax.ShapeDtypeStruct((ROWS, COLS), jnp.int32),
        ),
        (temp, humid, parent),
        [
            pltpu.VMEM((LEV, ROWS, COLS), F32),
            pltpu.VMEM((LEV, ROWS, COLS), F32),
            pltpu.VMEM((WIDE, CELLS), BF16),
            pltpu.VMEM((CELLS, COLS), BF16),
            pltpu.VMEM((16, CELLS), BF16),
        ],
    )


def owner_kernel(recv_ref, kabs_ref, planck_ref, top_ref, out_ref,
                 b_ref, absorb_ref, emit_ref, step_ref, hmean_ref, net_ref, trans_ref, sum_ref, q_ref):
    sub = lax.broadcasted_iota(jnp.int32, (256, CAP), 0).astype(F32)
    lane = lax.broadcasted_iota(jnp.int32, (CAP, 256), 1).astype(F32)
    lows = jnp.concatenate([recv_ref[s, BLK_ROW:SEND, :].astype(F32)[1:2] for s in range(TILES)], axis=0)
    low_cols = lows.T

    for first in range(0, TILES, 4):
        lhs = []
        rhs = []
        for s in range(first, first + 4):
            got = recv_ref[s]
            blk = jnp.broadcast_to(got[BLK_ROW:SEND].astype(F32)[0:1], (SEND, CAP)).astype(BF16)
            half = slice((s % 2) * CAP, (s % 2 + 1) * CAP)
            b_ref[s // 2, :, half] = jnp.where(lows[s : s + 1] == sub, 1.0, 0.0).astype(BF16)
            rhs.append(jnp.where(low_cols[:, s : s + 1] == lane, 1.0, 0.0).astype(BF16))
            zero = jnp.zeros_like(got)
            lhs.append(
                jnp.concatenate([jnp.where(blk == jnp.asarray(b + 1, BF16), got, zero) for b in range(4)], axis=0)
            )
        part = jnp.dot(
            jnp.concatenate(lhs, axis=1), jnp.concatenate(rhs, axis=0), preferred_element_type=F32
        )
        if first == 0:
            sum_ref[...] = part
        else:
            sum_ref[...] += part

    counts = []
    for b in range(4):
        for h in range(2):
            lanes = slice(h * CAP, (h + 1) * CAP)
            row = b * SEND + ONE_ROW
            counts.append(sum_ref[row : row + 1, lanes])
            emit_ref[:, 2 * b + h, :] = sum_ref[b * SEND : b * SEND + LEV, lanes]
            hmean_ref[:, 2 * b + h, :] = sum_ref[b * SEND + LEV : b * SEND + 2 * LEV, lanes]
    inv = 1.0 / jnp.maximum(jnp.concatenate(counts, axis=0), 1.0)
    hc = hmean_ref[...] * inv[None]
    absorb_ref[...] = jnp.exp(0.5 * hc)
    emit = jnp.exp(0.25 * (emit_ref[...] * inv[None]))
    emit_ref[...] = emit
    step_ref[0 : LEV - 1] = emit[1:LEV] - emit[0 : LEV - 1]
    hmean_ref[...] = hc
    net_ref[...] = jnp.zeros_like(net_ref)
    emit_top = emit_ref[0]
    emit_low = emit_ref[LEV - 1]

    def one_block(block, top_net):
        first = block * GB
        tops = [top_ref[first + j] for j in range(GB)]
        planck = [planck_ref[first + j] for j in range(GB)]
        state = [tops[j] - emit_top * planck[j] for j in range(GB)]
        for k in range(LEV):
            absorb = absorb_ref[k]
            total = None
            for j in range(GB):
                t = jnp.exp2(absorb * kabs_ref[first + j, k])
                trans_ref[k, j] = t
                state[j] = t * state[j]
                total = state[j] if total is None else total + state[j]
            net_ref[k] += total
            if k < LEV - 1:
                step = step_ref[k]
                state = [state[j] - step * planck[j] for j in range(GB)]
        state = [
            0.3 * (state[j] + emit_low * planck[j]) - emit_low * planck[j] for j in range(GB)
        ]
        for k in range(LEV - 1, -1, -1):
            total = None
            for j in range(GB):
                state[j] = trans_ref[k, j] * state[j]
                total = state[j] if total is None else total + state[j]
            net_ref[k] -= total
            if k > 0:
                step = step_ref[k - 1]
                state = [state[j] + step * planck[j] for j in range(GB)]
        for j in range(GB):
            top_net = top_net + (tops[j] - (state[j] + emit_top * planck[j]))
        return top_net

    top_net = lax.fori_loop(0, G // GB, one_block, jnp.zeros((8, 128), F32))
    net = net_ref[...]
    prev = jnp.concatenate([top_net[None], net[:-1]], axis=0)
    heat = ((prev - net) * (LEV / G)).astype(BF16).astype(F32)
    hm = hmean_ref[...].astype(BF16).astype(F32)
    net_ref[...] = heat - 0.5 * hm
    for b in range(4):
        for h in range(2):
            q_ref[b * LEV : (b + 1) * LEV, h * CAP : (h + 1) * CAP] = net_ref[:, 2 * b + h, :].astype(BF16)

    for p in range(PAIRS):
        both = jnp.dot(q_ref[...], b_ref[p], preferred_element_type=F32)
        for h in range(2):
            lanes = slice(h * CAP, (h + 1) * CAP)
            blk = recv_ref[2 * p + h, BLK_ROW:SEND, :].astype(F32)[0:1]
            got = jnp.zeros((LEV, CAP), F32)
            for b in range(4):
                got = jnp.where(blk == float(b + 1), both[b * LEV : (b + 1) * LEV, lanes], got)
            out_ref[2 * p + h] = got.astype(BF16)


def owner_step(recv, kabs, planck, top_flux):
    column = pltpu.VMEM((LEV, 8, 128), F32)
    return call(
        owner_kernel,
        jax.ShapeDtypeStruct((TILES, LEV, CAP), BF16),
        (recv, kabs * (-LOG2E), planck, top_flux),
        [
            pltpu.VMEM((PAIRS, 256, 256), BF16),
            column,
            column,
            column,
            column,
            column,
            pltpu.VMEM((LEV, GB, 8, 128), F32),
            pltpu.VMEM((4 * SEND, 256), F32),
            pltpu.VMEM((4 * LEV, 256), BF16),
        ],
        scalars=3,
    )


def gather_columns(row_of):
    first = row_of(0)
    lane = lax.broadcasted_iota(jnp.int32, (first.shape[0], 128), 1)
    kept = jnp.zeros((first.shape[0], 128), first.dtype)
    for r in range(ROWS):
        row = row_of(r)
        kept = jnp.where(lane == r, row[:, 0:1], kept)
        kept = jnp.where(lane == ROWS + r, row[:, COLS - 1 : COLS], kept)
    return kept


def split_columns(columns):
    return columns.astype(BF16), pltpu.roll(columns, 128 - ROWS, axis=1).astype(BF16)


def edge_shapes():
    row = jax.ShapeDtypeStruct((LEV, COLS), BF16)
    column = jax.ShapeDtypeStruct((LEV, 128), BF16)
    return row, row, column, column


def edges_kernel(temp_ref, top_ref, bottom_ref, left_ref, right_ref, t_ref):
    t_ref[...] = temp_ref[...].astype(F32)
    top_ref[...] = t_ref[:, 0, :].astype(BF16)
    bottom_ref[...] = t_ref[:, ROWS - 1, :].astype(BF16)
    left_ref[...], right_ref[...] = split_columns(gather_columns(lambda r: t_ref[:, r, :]))


def edges(temp):
    return call(edges_kernel, edge_shapes(), (temp,), [pltpu.VMEM((LEV, ROWS, COLS), F32)])


def stencil_row(value, above, below, left, right):
    lane = lax.broadcasted_iota(jnp.int32, value.shape, 1)
    west = jnp.where(lane == 0, left, pltpu.roll(value, 1, axis=1))
    east = jnp.where(lane == COLS - 1, right, pltpu.roll(value, COLS - 1, axis=1))
    return value + 0.2 * (above + below + west + east - 4.0 * value)


def stencil_rows(row_of, above_ref, below_ref, left_ref, right_ref):
    left = left_ref[...].astype(F32)
    right = right_ref[...].astype(F32)
    above = above_ref[...].astype(F32)
    value = row_of(0)
    for r in range(ROWS):
        below = row_of(r + 1) if r < ROWS - 1 else below_ref[...].astype(F32)
        yield r, stencil_row(value, above, below, left[:, r : r + 1], right[:, r : r + 1])
        above, value = value, below


def base_kernel(temp_ref, humid_ref, slot_ref, above_ref, below_ref, left_ref, right_ref,
                base_ref, base_cols_ref, slot_cols_ref, t_ref, h_ref):
    t_ref[...] = temp_ref[...].astype(F32)
    h_ref[...] = humid_ref[...].astype(F32)
    for r, first in stencil_rows(lambda r: t_ref[:, r, :], above_ref, below_ref, left_ref, right_ref):
        base_ref[r] = first.astype(BF16).astype(F32) + 0.25 * h_ref[:, r, :]
    base_cols_ref[...] = gather_columns(lambda r: base_ref[r])
    slot = slot_ref[...]
    slots = gather_columns(lambda r: slot[r : r + 1])
    slot_cols_ref[...] = jnp.broadcast_to(slots, (8, 128))


def base_step(temp, humid, slot, halo):
    return call(
        base_kernel,
        (
            jax.ShapeDtypeStruct((ROWS, LEV, COLS), F32),
            jax.ShapeDtypeStruct((LEV, 128), F32),
            jax.ShapeDtypeStruct((8, 128), jnp.int32),
        ),
        (temp, humid, slot, *halo),
        [pltpu.VMEM((LEV, ROWS, COLS), F32), pltpu.VMEM((LEV, ROWS, COLS), F32)],
    )


def in_pairs(ret_ref, r_ref):
    for p in range(PAIRS):
        for h in range(2):
            r_ref[p * LEV : (p + 1) * LEV, h * CAP : (h + 1) * CAP] = ret_ref[2 * p + h]


def picked(r_ref, slot):
    count = slot.shape[1]
    sub = lax.broadcasted_iota(jnp.int32, (256, count), 0)
    onehot = jnp.where((slot % 256) == sub, 1.0, 0.0).astype(BF16)
    pair = slot // 256
    moved = jnp.dot(r_ref[...], onehot, preferred_element_type=F32)
    q = jnp.zeros((LEV, count), F32)
    for p in range(PAIRS):
        q = jnp.where(pair == p, moved[p * LEV : (p + 1) * LEV], q)
    return q


def rim_kernel(ret_ref, slot_ref, slot_cols_ref, base_top_ref, base_bottom_ref, base_cols_ref,
               top_ref, bottom_ref, left_ref, right_ref, r_ref):
    in_pairs(ret_ref, r_ref)
    slot = jnp.concatenate(
        [slot_ref[0:1, :], slot_ref[ROWS - 1 : ROWS, :], slot_cols_ref[0:1, :]], axis=1
    )
    q = 0.5 * picked(r_ref, slot)
    top_ref[...] = (base_top_ref[0] + q[:, 0:COLS]).astype(BF16)
    bottom_ref[...] = (base_bottom_ref[0] + q[:, COLS : 2 * COLS]).astype(BF16)
    left_ref[...], right_ref[...] = split_columns(base_cols_ref[...] + q[:, 2 * COLS :])


def rim(ret, slot, slot_cols, base, base_cols):
    return call(
        rim_kernel,
        edge_shapes(),
        (ret, slot, slot_cols, base[0:1], base[ROWS - 1 : ROWS], base_cols),
        [pltpu.VMEM((PAIRS * LEV, 256), BF16)],
    )


def unpack_kernel(ret_ref, slot_ref, base_ref, second_ref, r_ref):
    in_pairs(ret_ref, r_ref)
    for r in range(ROWS):
        q = picked(r_ref, slot_ref[r : r + 1, :])
        second_ref[r] = (base_ref[r] + 0.5 * q).astype(BF16)


def unpack(ret, slot, base):
    return call(
        unpack_kernel,
        jax.ShapeDtypeStruct((ROWS, LEV, COLS), BF16),
        (ret, slot, base),
        [pltpu.VMEM((PAIRS * LEV, 256), BF16)],
    )


def last_kernel(second_ref, above_ref, below_ref, left_ref, right_ref, out_ref, o_ref):
    row_of = lambda r: second_ref[r].astype(F32)
    for r, value in stencil_rows(row_of, above_ref, below_ref, left_ref, right_ref):
        o_ref[:, r, :] = value
    out_ref[...] = o_ref[...].astype(BF16)


def last_step(second, halo):
    return call(
        last_kernel,
        jax.ShapeDtypeStruct((LEV, ROWS, COLS), BF16),
        (second, *halo),
        [pltpu.VMEM((LEV, ROWS, COLS), F32)],
    )


def exchange(top, bottom, left, right):
    grp = lax.axis_size("grp")
    tile = lax.axis_size("tile")
    up = [(i, (i + 1) % grp) for i in range(grp)]
    along = [(i, (i + 1) % tile) for i in range(tile)]
    above = lax.ppermute(bottom, "grp", up)
    below = lax.ppermute(top, "grp", [(b, a) for a, b in up])
    west = lax.ppermute(right, "tile", along)
    east = lax.ppermute(left, "tile", [(b, a) for a, b in along])
    return above, below, west, east


def on_device(temp, humid, parent, kabs, planck, top_flux):
    send, slot = pack(temp, humid, parent)
    recv = lax.all_to_all(send, "tile", split_axis=0, concat_axis=0, tiled=True)
    base, base_cols, slot_cols = base_step(temp, humid, slot, exchange(*edges(temp)))
    recv, base, base_cols, slot_cols = lax.optimization_barrier((recv, base, base_cols, slot_cols))
    answer = owner_step(recv, kabs, planck, top_flux)
    ret = lax.all_to_all(answer, "tile", split_axis=0, concat_axis=0, tiled=True)
    halo = exchange(*rim(ret, slot, slot_cols, base, base_cols))
    second = unpack(ret, slot, base)
    return last_step(second, halo)


def solution(mesh):
    placed = (P(None, "grp", "tile"), P(None, "grp", "tile"), P("grp", "tile"), P(), P(), P())
    return jax.shard_map(
        on_device, mesh=mesh, in_specs=placed, out_specs=P(None, "grp", "tile"), check_vma=False
    )
```

time: 173 us -> 141 us (0.82)
  local copies, waits for them, and re-layouts: 26.7 us -> 5.43 us
  Pallas kernels: 67.1 us -> 49.1 us
  waiting for transfers between devices: 44.5 us -> 50.3 us
    all_to_all x1, waiting for transfers between devices: 41.5 us -> 0.01 us  [on_device(): recv = lax.all_to_all(send, 'tile', split_axis=0, concat_axis=0, tiled=True)]
    ppermute x2, waiting for transfers between devices: 2.95 us -> 28.8 us  [exchange(): west = lax.ppermute(right, 'tile', along)]
    all_to_all x1, waiting for transfers between devices: 0.01 us -> 21.5 us  [on_device(): lax.all_to_all(answer, 'tile', split_axis=0, concat_axis=0, tiled=True)]
    pallas_call x5 -> x7, Pallas kernels: 67.1 us -> 49.1 us  [call(): pl.pallas_call(kernel, out_shape=out_shape, in_specs=[vmem] * (len(operan...]
    slice x3 -> x1, local copies, waits for them, and re-layouts: 13.1 us -> 1.46 us  [rim(): base[ROWS - 1:ROWS]]
    unnamed x25 -> x23, local copies, waits for them, and re-layouts: 9.13 us -> 3.97 us
    transpose x3 -> x0, local copies, waits for them, and re-layouts: 3.72 us -> none  [the longest x1 1.86 us: on_device(): temp_t = jnp.transpose(temp, (1, 0, 2))]
  transfers between devices with their start and end apart: 10 -> 10, of which waited for: 3 -> 2; matrix products, arithmetic and copies ran while one was open for 10% -> 2% of each run, Pallas kernels for 1% -> 9%
where the time goes in v2:
time: 141 us; the launch traced here: 140 us
  waiting for transfers between devices  50.3 us (36%)
  Pallas kernels  49.1 us (35%)
  starting transfers between devices  34.5 us (24%)
  local copies, waits for them, and re-layouts  5.43 us (4%)
    pallas_call x7, Pallas kernels, call(): pl.pallas_call(kernel, out_shape=out_shape, in_specs=[vmem] * (len(operan...  49.1 us
    ppermute x2, waiting for transfers between devices, exchange(): west = lax.ppermute(right, 'tile', along)  28.8 us
    all_to_all x1, waiting for transfers between devices, on_device(): lax.all_to_all(answer, 'tile', split_axis=0, concat_axis=0, tiled=True)  21.5 us
    all_to_all x1, starting transfers between devices, on_device(): recv = lax.all_to_all(send, 'tile', split_axis=0, concat_axis=0, tiled=True)  12.2 us
    ppermute x2, starting transfers between devices, exchange(): east = lax.ppermute(left, 'tile', [(b, a) for a, b in along])  10.1 us
    all_to_all x1, starting transfers between devices, on_device(): lax.all_to_all(answer, 'tile', split_axis=0, concat_axis=0, tiled=True)  8.04 us
    unnamed x23, local copies, waits for them, and re-layouts  3.97 us
    ppermute x2, starting transfers between devices, exchange(): below = lax.ppermute(top, 'grp', [(b, a) for a, b in up])  3.1 us
  transfers between devices with their start and end apart: 10, of which 2 were waited for; matrix products, arithmetic and copies ran while one was open for 2% of the time, Pallas kernels for 9%

profile of v2, /device:TPU:6, one launch (start us, length us, event | category | flops | bytes accessed | tf_op | source)
XLA Modules:
  0.0 140.0 jit_solution(1266472622874749649)
XLA Ops:
  0.0 13.8 %shard_map.64 = (bf16[64,104,128]{2,1,0:T(8,128)(2,1)}, s32[16,256]{1,0:T(8,128)}) custom-call(bf16[48,16,256]{2,1,0:T(8,128)(2,1)} %temp_ref.5, bf16[48,16,256]{2,1,0:T(8,128)(2,1)} %humid_ref.3, s32[16,256]{1,0:T(8,128)} %parent_ref.1), custom_call_target="tpu_custom_call" | custom-call | tf_op jit(solution)/shard_map/pallas_call | solution.py:33
  13.8 0.0 copy-start.4
  13.8 12.2 %all-to-all-start = ((bf16[64,104,128]{2,1,0:T(8,128)(2,1)}), bf16[64,104,128]{2,1,0:T(8,128)(2,1)S(1)}, u32[]{:S(2)}, u32[]{:S(2)}) async-start(bf16[64,104,128]{2,1,0:T(8,128)(2,1)} %get-tuple-element.22), calls=%async_computation | async-start | bytes 3407872 | tf_op jit(solution)/shard_map/all_to_all | solution.py:400
  26.0 3.5 %shard_map.65 = (bf16[48,256]{1,0:T(8,128)(2,1)}, bf16[48,256]{1,0:T(8,128)(2,1)}, bf16[48,128]{1,0:T(8,128)(2,1)}, bf16[48,128]{1,0:T(8,128)(2,1)}) custom-call(bf16[48,16,256]{2,1,0:T(8,128)(2,1)} %temp_ref.5), custom_call_target="tpu_custom_call" | custom-call | tf_op jit(solution)/shard_map/pallas_call | solution.py:33
  29.6 0.5 collective-permute-start
  30.0 1.5 %collective-permute-start.1 = (bf16[48,256]{1,0:T(8,128)(2,1)}, bf16[48,256]{1,0:T(8,128)(2,1)S(1)}, u32[]{:S(2)}, u32[]{:S(2)}) collective-permute-start(bf16[48,256]{1,0:T(8,128)(2,1)} %get-tuple-element.25), channel_id=1, source_target_pairs={{64,0},{128,64},{192,128},{0,192},{65,1},{129,65},{193,129},{1,193... | collective-permute-start | bytes 73736 | tf_op jit(solution)/shard_map/ppermute | solution.py:392
  31.6 0.0 collective-permute-start.2
  31.6 5.1 %collective-permute-start.3 = (bf16[48,128]{1,0:T(8,128)(2,1)}, bf16[48,128]{1,0:T(8,128)(2,1)S(1)}, u32[]{:S(2)}, u32[]{:S(2)}) collective-permute-start(bf16[48,128]{1,0:T(8,128)(2,1)} %get-tuple-element.27), channel_id=1, source_target_pairs={{1,0},{2,1},{3,2},{4,3},{5,4},{6,5},{7,6},{8,7},{9,8},{10,9},{11,1... | collective-permute-start | bytes 36872 | tf_op jit(solution)/shard_map/ppermute | solution.py:394
  36.7 0.0 copy-done.4
  36.7 0.1 copy.8
  36.8 0.6 broadcast_multiply_fusion.kabs_ref
  37.4 28.8 %collective-permute-done.2.left_ref = bf16[48,128]{1,0:T(8,128)(2,1)S(1)} collective-permute-done((bf16[48,128]{1,0:T(8,128)(2,1)}, bf16[48,128]{1,0:T(8,128)(2,1)S(1)}, u32[]{:S(2)}, u32[]{:S(2)}) %collective-permute-start.2) | collective-permute-done | bytes 12320 | tf_op jit(solution)/shard_map/ppermute | solution.py:393
  66.2 0.0 copy-start.7
  66.2 0.0 collective-permute-done.3.right_ref
  66.2 0.0 copy-start.8
  66.2 0.0 collective-permute-done.above_ref
  66.2 0.0 copy-start.2
  66.2 0.0 collective-permute-done.1.below_ref
  66.3 0.0 copy-start.3
  66.3 0.5 copy-done.7
  66.8 0.0 copy-done.8
  66.8 0.0 copy-done.2
  66.8 0.0 copy-done.3
  66.9 4.0 %shard_map.66 = (f32[16,48,256]{2,1,0:T(8,128)}, f32[48,128]{1,0:T(8,128)}, s32[8,128]{1,0:T(8,128)}) custom-call(bf16[48,16,256]{2,1,0:T(8,128)(2,1)} %temp_ref.5, bf16[48,16,256]{2,1,0:T(8,128)(2,1)} %humid_ref.3, s32[16,256]{1,0:T(8,128)} %get-tuple-element.23.slot_ref, bf16[48,256]{1,0:T(8,128)(2,1)} %copy-done.2, bf16[48,256]{1,0:T(8,128)(2,1)} %copy-done.3, ...), custom_call_target="tpu_custom_call" | custom-call | tf_op jit(solution)/shard_map/pallas_call | solution.py:33
  70.8 0.0 all-to-all-done.recv_ref
  70.8 1.2 copy-done.1
  72.0 16.8 %shard_map.67 = bf16[64,48,128]{2,1,0:T(8,128)(2,1)} custom-call(bf16[64,104,128]{2,1,0:T(8,128)(2,1)} %copy-done.1, f32[112,48]{1,0:T(8,128)} %broadcast_multiply_fusion.kabs_ref, f32[112]{0:T(128)} %planck_ref.1, f32[112]{0:T(128)} %top_ref.1), custom_call_target="tpu_custom_call" | custom-call | tf_op jit(solution)/shard_map/pallas_call | solution.py:33
  88.9 8.0 %all-to-all-start.1 = ((bf16[64,48,128]{2,1,0:T(8,128)(2,1)}), bf16[64,48,128]{2,1,0:T(8,128)(2,1)S(1)}, u32[]{:S(2)}, u32[]{:S(2)}) async-start(bf16[64,48,128]{2,1,0:T(8,128)(2,1)} %shard_map.67), calls=%async_computation.1 | async-start | bytes 1572864 | tf_op jit(solution)/shard_map/all_to_all | solution.py:404
  96.9 1.5 %fusion = (f32[1,48,256]{2,1,0:T(8,128)}, f32[1,48,256]{2,1,0:T(8,128)}) fusion(f32[16,48,256]{2,1,0:T(8,128)} %get-tuple-element.32.base_ref), kind=kLoop, calls=%fused_computation.1 | loop fusion | bytes 196608 | tf_op jit(solution)/shard_map/slice | solution.py:349
  98.4 21.5 %all-to-all-done.1.ret_ref = bf16[64,48,128]{2,1,0:T(8,128)(2,1)S(1)} async-done(((bf16[64,48,128]{2,1,0:T(8,128)(2,1)}), bf16[64,48,128]{2,1,0:T(8,128)(2,1)S(1)}, u32[]{:S(2)}, u32[]{:S(2)}) %all-to-all-start.1) | async-done | bytes 786464 | tf_op jit(solution)/shard_map/all_to_all | solution.py:404
  119.8 0.9 copy-done
  120.7 2.7 %shard_map.69 = (bf16[48,256]{1,0:T(8,128)(2,1)}, bf16[48,256]{1,0:T(8,128)(2,1)}, bf16[48,128]{1,0:T(8,128)(2,1)}, bf16[48,128]{1,0:T(8,128)(2,1)}) custom-call(bf16[64,48,128]{2,1,0:T(8,128)(2,1)} %copy-done, s32[16,256]{1,0:T(8,128)} %get-tuple-element.23.slot_ref, s32[8,128]{1,0:T(8,128)} %get-tuple-element.33.slot_cols_ref, ...), custom_call_target="tpu_custom_call" | custom-call | tf_op jit(solution)/shard_map/pallas_call | solution.py:33
  123.4 0.5 collective-permute-start.4
  123.9 1.5 %collective-permute-start.5 = (bf16[48,256]{1,0:T(8,128)(2,1)}, bf16[48,256]{1,0:T(8,128)(2,1)S(1)}, u32[]{:S(2)}, u32[]{:S(2)}) collective-permute-start(bf16[48,256]{1,0:T(8,128)(2,1)} %get-tuple-element.36), channel_id=1, source_target_pairs={{64,0},{128,64},{192,128},{0,192},{65,1},{129,65},{193,129},{1,193... | collective-permute-start | bytes 73736 | tf_op jit(solution)/shard_map/ppermute | solution.py:392
  125.4 0.0 collective-permute-start.6
  125.4 5.1 %collective-permute-start.7 = (bf16[48,128]{1,0:T(8,128)(2,1)}, bf16[48,128]{1,0:T(8,128)(2,1)S(1)}, u32[]{:S(2)}, u32[]{:S(2)}) collective-permute-start(bf16[48,128]{1,0:T(8,128)(2,1)} %get-tuple-element.38), channel_id=1, source_target_pairs={{1,0},{2,1},{3,2},{4,3},{5,4},{6,5},{7,6},{8,7},{9,8},{10,9},{11,1... | collective-permute-start | bytes 36872 | tf_op jit(solution)/shard_map/ppermute | solution.py:394
  130.5 5.6 %shard_map.68.second_ref = bf16[16,48,256]{2,1,0:T(8,128)(2,1)} custom-call(bf16[64,48,128]{2,1,0:T(8,128)(2,1)} %copy-done, s32[16,256]{1,0:T(8,128)} %get-tuple-element.23.slot_ref, f32[16,48,256]{2,1,0:T(8,128)} %get-tuple-element.32.base_ref), custom_call_target="tpu_custom_call" | custom-call | tf_op jit(solution)/shard_map/pallas_call | solution.py:33
  136.1 0.0 collective-permute-done.6.left_ref
  136.1 0.0 collective-permute-done.7.right_ref
  136.1 0.0 copy-start.10
  136.2 0.0 collective-permute-done.4.above_ref
  136.2 0.0 copy-start.5
  136.2 0.0 collective-permute-done.5.below_ref
  136.2 0.5 copy-done.9
  136.7 0.0 copy-done.10
  136.7 0.0 copy-done.5
  136.8 0.6 copy-done.6
  137.4 2.6 %shard_map.70 = bf16[48,16,256]{2,1,0:T(8,128)(2,1)} custom-call(bf16[16,48,256]{2,1,0:T(8,128)(2,1)} %shard_map.68.second_ref, bf16[48,256]{1,0:T(8,128)(2,1)} %copy-done.5, bf16[48,256]{1,0:T(8,128)(2,1)} %copy-done.6, bf16[48,128]{1,0:T(8,128)(2,1)} %copy-done.9, bf16[48,128]{1,0:T(8,128)(2,1)} %copy-done.10), custom_call_target="tpu_custom_call" | custom-call | tf_op jit(solution)/shard_map/pallas_call | solution.py:33
  (4 shorter events, 0.0 us)
Async XLA Ops:
  13.8 22.9 %copy-start.4 = (f32[112,48]{0,1:T(8,128)S(1)}, f32[112,48]{0,1:T(8,128)}, u32[]{:S(2)}) copy-start(f32[112,48]{0,1:T(8,128)} %param.9) | copy-start | bytes 64516
  13.8 57.0 %all-to-all-start = ((bf16[64,104,128]{2,1,0:T(8,128)(2,1)}), bf16[64,104,128]{2,1,0:T(8,128)(2,1)S(1)}, u32[]{:S(2)}, u32[]{:S(2)}) async-start(bf16[64,104,128]{2,1,0:T(8,128)(2,1)} %get-tuple-element.22), calls=%async_computation | async-start | bytes 3407872 | tf_op jit(solution)/shard_map/all_to_all | solution.py:400
  29.6 36.7 %collective-permute-start = (bf16[48,256]{1,0:T(8,128)(2,1)}, bf16[48,256]{1,0:T(8,128)(2,1)S(1)}, u32[]{:S(2)}, u32[]{:S(2)}) collective-permute-start(bf16[48,256]{1,0:T(8,128)(2,1)} %get-tuple-element.24), channel_id=1, source_target_pairs={{0,64},{64,128},{128,192},{192,0},{1,65},{65,129},{129,193},{193,1... | collective-permute-start | bytes 73736 | tf_op jit(solution)/shard_map/ppermute | solution.py:391
  30.0 36.2 %collective-permute-start.1 = (bf16[48,256]{1,0:T(8,128)(2,1)}, bf16[48,256]{1,0:T(8,128)(2,1)S(1)}, u32[]{:S(2)}, u32[]{:S(2)}) collective-permute-start(bf16[48,256]{1,0:T(8,128)(2,1)} %get-tuple-element.25), channel_id=1, source_target_pairs={{64,0},{128,64},{192,128},{0,192},{65,1},{129,65},{193,129},{1,193... | collective-permute-start | bytes 73736 | tf_op jit(solution)/shard_map/ppermute | solution.py:392
  31.6 34.6 %collective-permute-start.2 = (bf16[48,128]{1,0:T(8,128)(2,1)}, bf16[48,128]{1,0:T(8,128)(2,1)S(1)}, u32[]{:S(2)}, u32[]{:S(2)}) collective-permute-start(bf16[48,128]{1,0:T(8,128)(2,1)} %get-tuple-element.26), channel_id=1, source_target_pairs={{0,1},{1,2},{2,3},{3,4},{4,5},{5,6},{6,7},{7,8},{8,9},{9,10},{10,1... | collective-permute-start | bytes 36872 | tf_op jit(solution)/shard_map/ppermute | solution.py:393
  31.6 34.6 %collective-permute-start.3 = (bf16[48,128]{1,0:T(8,128)(2,1)}, bf16[48,128]{1,0:T(8,128)(2,1)S(1)}, u32[]{:S(2)}, u32[]{:S(2)}) collective-permute-start(bf16[48,128]{1,0:T(8,128)(2,1)} %get-tuple-element.27), channel_id=1, source_target_pairs={{1,0},{2,1},{3,2},{4,3},{5,4},{6,5},{7,6},{8,7},{9,8},{10,9},{11,1... | collective-permute-start | bytes 36872 | tf_op jit(solution)/shard_map/ppermute | solution.py:394
  66.2 0.6 copy-start.7
  66.2 0.6 copy-start.8
  66.2 0.6 copy-start.2
  66.3 0.6 copy-start.3
  70.8 1.2 copy-start.1
  88.9 31.0 %all-to-all-start.1 = ((bf16[64,48,128]{2,1,0:T(8,128)(2,1)}), bf16[64,48,128]{2,1,0:T(8,128)(2,1)S(1)}, u32[]{:S(2)}, u32[]{:S(2)}) async-start(bf16[64,48,128]{2,1,0:T(8,128)(2,1)} %shard_map.67), calls=%async_computation.1 | async-start | bytes 1572864 | tf_op jit(solution)/shard_map/all_to_all | solution.py:404
  119.8 0.9 copy-start
  123.4 12.8 %collective-permute-start.4 = (bf16[48,256]{1,0:T(8,128)(2,1)}, bf16[48,256]{1,0:T(8,128)(2,1)S(1)}, u32[]{:S(2)}, u32[]{:S(2)}) collective-permute-start(bf16[48,256]{1,0:T(8,128)(2,1)} %get-tuple-element.35), channel_id=1, source_target_pairs={{0,64},{64,128},{128,192},{192,0},{1,65},{65,129},{129,193},{193,1... | collective-permute-start | bytes 73736 | tf_op jit(solution)/shard_map/ppermute | solution.py:391
  123.9 12.3 %collective-permute-start.5 = (bf16[48,256]{1,0:T(8,128)(2,1)}, bf16[48,256]{1,0:T(8,128)(2,1)S(1)}, u32[]{:S(2)}, u32[]{:S(2)}) collective-permute-start(bf16[48,256]{1,0:T(8,128)(2,1)} %get-tuple-element.36), channel_id=1, source_target_pairs={{64,0},{128,64},{192,128},{0,192},{65,1},{129,65},{193,129},{1,193... | collective-permute-start | bytes 73736 | tf_op jit(solution)/shard_map/ppermute | solution.py:392
  125.4 10.7 %collective-permute-start.6 = (bf16[48,128]{1,0:T(8,128)(2,1)}, bf16[48,128]{1,0:T(8,128)(2,1)S(1)}, u32[]{:S(2)}, u32[]{:S(2)}) collective-permute-start(bf16[48,128]{1,0:T(8,128)(2,1)} %get-tuple-element.37), channel_id=1, source_target_pairs={{0,1},{1,2},{2,3},{3,4},{4,5},{5,6},{6,7},{7,8},{8,9},{9,10},{10,1... | collective-permute-start | bytes 36872 | tf_op jit(solution)/shard_map/ppermute | solution.py:393
  125.4 10.7 %collective-permute-start.7 = (bf16[48,128]{1,0:T(8,128)(2,1)}, bf16[48,128]{1,0:T(8,128)(2,1)S(1)}, u32[]{:S(2)}, u32[]{:S(2)}) collective-permute-start(bf16[48,128]{1,0:T(8,128)(2,1)} %get-tuple-element.38), channel_id=1, source_target_pairs={{1,0},{2,1},{3,2},{4,3},{5,4},{6,5},{7,6},{8,7},{9,8},{10,9},{11,1... | collective-permute-start | bytes 36872 | tf_op jit(solution)/shard_map/ppermute | solution.py:394
  136.1 0.6 copy-start.9
  136.1 0.6 copy-start.10
  136.2 0.6 copy-start.5
  136.8 0.6 copy-start.6

commit v3 on v2

--- a/solution.py
+++ b/solution.py
@@ -23,26 +23,39 @@
 GROUP = 8
 GB = 4
 LOG2E = 1.4426950408889634
-VMEM = 56 * 1024 * 1024
-
-
-def call(kernel, out_shape, operands, scratch=(), scalars=0):
+VMEM = 32 * 1024 * 1024
+
+
+def call(kernel, out_shape, operands, scratch=(), scalars=0, resident_in=True, resident_out=True):
     vmem = pl.BlockSpec(memory_space=pltpu.VMEM)
     smem = pl.BlockSpec(memory_space=pltpu.SMEM)
     many = isinstance(out_shape, tuple)
+    arrays = len(operands) - scalars
+    if resident_in:
+        operands = [
+            pltpu.with_memory_space_constraint(x, pltpu.VMEM) if i < arrays else x for i, x in enumerate(operands)
+        ]
+    if resident_out:
+        place = lambda x: pltpu.VMEM(x.shape, x.dtype)
+        out_shape = tuple(place(x) for x in out_shape) if many else place(out_shape)
     return pl.pallas_call(
         kernel,
         out_shape=out_shape,
-        in_specs=[vmem] * (len(operands) - scalars) + [smem] * scalars,
+        in_specs=[vmem] * arrays + [smem] * scalars,
         out_specs=(vmem,) * len(out_shape) if many else vmem,
         scratch_shapes=list(scratch),
         compiler_params=pltpu.CompilerParams(vmem_limit_bytes=VMEM),
     )(*operands)
 
 
-def pack_kernel(temp_ref, humid_ref, parent_ref, send_ref, slot_ref, t_ref, h_ref, x_ref, b_ref, pair_ref):
-    t_ref[...] = temp_ref[...].astype(F32)
-    h_ref[...] = humid_ref[...].astype(F32)
+def pack_kernel(temp_ref, humid_ref, parent_ref, send_ref, slot_ref,
+                temp_in, humid_in, send_out, t_ref, h_ref, x_ref, b_ref, pair_ref, in_sem, out_sem):
+    arriving = [
+        pltpu.make_async_copy(temp_ref, temp_in, in_sem.at[0]),
+        pltpu.make_async_copy(humid_ref, humid_in, in_sem.at[1]),
+    ]
+    for copy in arriving:
+        copy.start()
     sub = lax.broadcasted_iota(jnp.int32, (COLS, COLS), 0)
     lane = lax.broadcasted_iota(jnp.int32, (COLS, COLS), 1)
     before = (sub < lane).astype(BF16)
@@ -67,60 +80,96 @@
     slot = owner * CAP + jnp.concatenate(position, axis=0).astype(jnp.int32)
     slot_ref[...] = slot
     pair = (slot // 256).astype(F32)
-    within = (slot % 256).astype(F32).T
-    lane_f = lane.astype(F32)
+    within = (slot % 256).astype(F32).T.astype(BF16)
     for r in range(ROWS):
         cols = slice(r * COLS, (r + 1) * COLS)
-        x_ref[0:LEV, cols] = t_ref[:, r, :].astype(BF16)
-        x_ref[LEV : 2 * LEV, cols] = h_ref[:, r, :].astype(BF16)
         extra = jnp.where(
             sub16 == 0, blk[r : r + 1], jnp.where(sub16 == 1, low[r : r + 1], jnp.where(sub16 == 2, 1.0, 0.0))
         )
         x_ref[2 * LEV : WIDE, cols] = extra.astype(BF16)
-        b_ref[cols, :] = jnp.where(within[:, r : r + 1] == lane_f, 1.0, 0.0).astype(BF16)
+        b_ref[cols, :] = hot_across(within[:, r : r + 1])
         pair_ref[:, cols] = jnp.broadcast_to(pair[r : r + 1], (16, COLS)).astype(BF16)
 
-    def one_group(step, _):
-        values = x_ref[...].reshape(WIDE // 16, 16, CELLS)
+    for copy in arriving:
+        copy.wait()
+    t_ref[...] = temp_in[...].astype(F32)
+    h_ref[...] = humid_in[...].astype(F32)
+    for r in range(ROWS):
+        cols = slice(r * COLS, (r + 1) * COLS)
+        x_ref[0:LEV, cols] = t_ref[:, r, :].astype(BF16)
+        x_ref[LEV : 2 * LEV, cols] = h_ref[:, r, :].astype(BF16)
+
+    values = x_ref[...].reshape(WIDE // 16, 16, CELLS)
+    leaving = []
+    for step in range(PAIRS // GROUP):
         chosen = []
         for j in range(GROUP):
-            mask = pair_ref[...] == (step * GROUP + j).astype(F32).astype(BF16)
+            mask = pair_ref[...] == jnp.asarray(step * GROUP + j, BF16)
             chosen.append(jnp.where(mask[None], values, jnp.zeros_like(values)).reshape(WIDE, CELLS))
         moved = jnp.dot(jnp.concatenate(chosen, axis=0), b_ref[...], preferred_element_type=F32)
         for j in range(GROUP):
             p = step * GROUP + j
             part = moved[j * WIDE : j * WIDE + SEND].astype(BF16)
-            send_ref[2 * p] = part[:, 0:CAP]
-            send_ref[2 * p + 1] = part[:, CAP : 2 * CAP]
-        return 0
-
-    lax.fori_loop(0, PAIRS // GROUP, one_group, 0)
+            send_out[2 * p] = part[:, 0:CAP]
+            send_out[2 * p + 1] = part[:, CAP : 2 * CAP]
+        done = pl.ds(2 * step * GROUP, 2 * GROUP)
+        copy = pltpu.make_async_copy(send_out.at[done], send_ref.at[done], out_sem.at[step])
+        copy.start()
+        leaving.append(copy)
+    for copy in leaving:
+        copy.wait()
 
 
 def pack(temp, humid, parent):
-    return call(
+    vmem = pl.BlockSpec(memory_space=pltpu.VMEM)
+    hbm = pl.BlockSpec(memory_space=pltpu.HBM)
+    field = (LEV, ROWS, COLS)
+    return pl.pallas_call(
         pack_kernel,
-        (
-            jax.ShapeDtypeStruct((TILES, SEND, CAP), BF16),
-            jax.ShapeDtypeStruct((ROWS, COLS), jnp.int32),
+        out_shape=(
+            pltpu.HBM((TILES, SEND, CAP), BF16),
+            pltpu.VMEM((ROWS, COLS), jnp.int32),
         ),
-        (temp, humid, parent),
-        [
-            pltpu.VMEM((LEV, ROWS, COLS), F32),
-            pltpu.VMEM((LEV, ROWS, COLS), F32),
+        in_specs=[hbm, hbm, vmem],
+        out_specs=(hbm, vmem),
+        scratch_shapes=[
+            pltpu.VMEM(field, BF16),
+            pltpu.VMEM(field, BF16),
+            pltpu.VMEM((TILES, SEND, CAP), BF16),
+            pltpu.VMEM(field, F32),
+            pltpu.VMEM(field, F32),
             pltpu.VMEM((WIDE, CELLS), BF16),
             pltpu.VMEM((CELLS, COLS), BF16),
             pltpu.VMEM((16, CELLS), BF16),
+            pltpu.SemaphoreType.DMA((2,)),
+            pltpu.SemaphoreType.DMA((PAIRS // GROUP,)),
         ],
-    )
+        compiler_params=pltpu.CompilerParams(vmem_limit_bytes=VMEM),
+    )(
+        pltpu.with_memory_space_constraint(temp, pltpu.HBM),
+        pltpu.with_memory_space_constraint(humid, pltpu.HBM),
+        parent,
+    )
+
+
+def hot_down(row):
+    n = row.shape[1]
+    index = lax.broadcasted_iota(jnp.int32, (256, n), 0).astype(F32).astype(BF16).reshape(16, 16, n)
+    hit = index == jnp.broadcast_to(row, (16, n)).astype(BF16)[None]
+    return jnp.where(hit, jnp.ones_like(index), jnp.zeros_like(index)).reshape(256, n)
+
+
+def hot_across(column):
+    n = column.shape[0]
+    index = lax.broadcasted_iota(jnp.int32, (n, 256), 1).astype(F32).astype(BF16)
+    hit = index == jnp.broadcast_to(column, (n, 256))
+    return jnp.where(hit, jnp.ones_like(index), jnp.zeros_like(index))
 
 
 def owner_kernel(recv_ref, kabs_ref, planck_ref, top_ref, out_ref,
                  b_ref, absorb_ref, emit_ref, step_ref, hmean_ref, net_ref, trans_ref, sum_ref, q_ref):
-    sub = lax.broadcasted_iota(jnp.int32, (256, CAP), 0).astype(F32)
-    lane = lax.broadcasted_iota(jnp.int32, (CAP, 256), 1).astype(F32)
     lows = jnp.concatenate([recv_ref[s, BLK_ROW:SEND, :].astype(F32)[1:2] for s in range(TILES)], axis=0)
-    low_cols = lows.T
+    low_cols = lows.T.astype(BF16)
 
     for first in range(0, TILES, 4):
         lhs = []
@@ -129,8 +178,8 @@
             got = recv_ref[s]
             blk = jnp.broadcast_to(got[BLK_ROW:SEND].astype(F32)[0:1], (SEND, CAP)).astype(BF16)
             half = slice((s % 2) * CAP, (s % 2 + 1) * CAP)
-            b_ref[s // 2, :, half] = jnp.where(lows[s : s + 1] == sub, 1.0, 0.0).astype(BF16)
-            rhs.append(jnp.where(low_cols[:, s : s + 1] == lane, 1.0, 0.0).astype(BF16))
+            b_ref[s // 2, :, half] = hot_down(lows[s : s + 1])
+            rhs.append(hot_across(low_cols[:, s : s + 1]))
             zero = jnp.zeros_like(got)
             lhs.append(
                 jnp.concatenate([jnp.where(blk == jnp.asarray(b + 1, BF16), got, zero) for b in range(4)], axis=0)
@@ -266,7 +315,9 @@
 
 
 def edges(temp):
-    return call(edges_kernel, edge_shapes(), (temp,), [pltpu.VMEM((LEV, ROWS, COLS), F32)])
+    return call(
+        edges_kernel, edge_shapes(), (temp,), [pltpu.VMEM((LEV, ROWS, COLS), F32)], resident_in=False
+    )
 
 
 def stencil_row(value, above, below, left, right):
@@ -320,25 +371,23 @@
 
 def picked(r_ref, slot):
     count = slot.shape[1]
-    sub = lax.broadcasted_iota(jnp.int32, (256, count), 0)
-    onehot = jnp.where((slot % 256) == sub, 1.0, 0.0).astype(BF16)
     pair = slot // 256
-    moved = jnp.dot(r_ref[...], onehot, preferred_element_type=F32)
+    moved = jnp.dot(r_ref[...], hot_down((slot % 256).astype(F32)), preferred_element_type=F32)
     q = jnp.zeros((LEV, count), F32)
     for p in range(PAIRS):
         q = jnp.where(pair == p, moved[p * LEV : (p + 1) * LEV], q)
     return q
 
 
-def rim_kernel(ret_ref, slot_ref, slot_cols_ref, base_top_ref, base_bottom_ref, base_cols_ref,
+def rim_kernel(ret_ref, slot_ref, slot_cols_ref, base_ref, base_cols_ref,
                top_ref, bottom_ref, left_ref, right_ref, r_ref):
     in_pairs(ret_ref, r_ref)
     slot = jnp.concatenate(
         [slot_ref[0:1, :], slot_ref[ROWS - 1 : ROWS, :], slot_cols_ref[0:1, :]], axis=1
     )
     q = 0.5 * picked(r_ref, slot)
-    top_ref[...] = (base_top_ref[0] + q[:, 0:COLS]).astype(BF16)
-    bottom_ref[...] = (base_bottom_ref[0] + q[:, COLS : 2 * COLS]).astype(BF16)
+    top_ref[...] = (base_ref[0] + q[:, 0:COLS]).astype(BF16)
+    bottom_ref[...] = (base_ref[ROWS - 1] + q[:, COLS : 2 * COLS]).astype(BF16)
     left_ref[...], right_ref[...] = split_columns(base_cols_ref[...] + q[:, 2 * COLS :])
 
 
@@ -346,7 +395,7 @@
     return call(
         rim_kernel,
         edge_shapes(),
-        (ret, slot, slot_cols, base[0:1], base[ROWS - 1 : ROWS], base_cols),
+        (ret, slot, slot_cols, base, base_cols),
         [pltpu.VMEM((PAIRS * LEV, 256), BF16)],
     )
 
@@ -380,6 +429,7 @@
         jax.ShapeDtypeStruct((LEV, ROWS, COLS), BF16),
         (second, *halo),
         [pltpu.VMEM((LEV, ROWS, COLS), F32)],
+        resident_out=False,
     )
 
 
@@ -398,10 +448,11 @@
 def on_device(temp, humid, parent, kabs, planck, top_flux):
     send, slot = pack(temp, humid, parent)
     recv = lax.all_to_all(send, "tile", split_axis=0, concat_axis=0, tiled=True)
-    base, base_cols, slot_cols = base_step(temp, humid, slot, exchange(*edges(temp)))
-    recv, base, base_cols, slot_cols = lax.optimization_barrier((recv, base, base_cols, slot_cols))
+    recv, halo = lax.optimization_barrier((recv, exchange(*edges(temp))))
     answer = owner_step(recv, kabs, planck, top_flux)
+    answer, halo = lax.optimization_barrier((answer, halo))
     ret = lax.all_to_all(answer, "tile", split_axis=0, concat_axis=0, tiled=True)
+    base, base_cols, slot_cols = base_step(temp, humid, slot, halo)
     halo = exchange(*rim(ret, slot, slot_cols, base, base_cols))
     second = unpack(ret, slot, base)
     return last_step(second, halo)

time: 141 us -> 125 us (0.89)
  Pallas kernels: 49.1 us -> 36.6 us
  waiting for transfers between devices: 50.3 us -> 55.7 us
  local copies, waits for them, and re-layouts: 5.43 us -> 0.84 us
  starting transfers between devices: 34.5 us -> 31.8 us
    pallas_call x7, Pallas kernels: 49.1 us -> 36.6 us  [the longest x6 25.6 us: call(): pl.pallas_call(kernel, out_shape=out_shape, in_specs=[vmem] * arrays + [s...]
    all_to_all x1, waiting for transfers between devices: 0.01 us -> 3.15 us  [on_device(): recv = lax.all_to_all(send, 'tile', split_axis=0, concat_axis=0, tiled=True)]
    unnamed x23 -> x13, local copies, waits for them, and re-layouts: 3.97 us -> 0.84 us
    ppermute x2, waiting for transfers between devices: 28.8 us -> 31.7 us  [exchange(): west = lax.ppermute(right, 'tile', along)]
    all_to_all x1, starting transfers between devices: 8.04 us -> 5.36 us  [on_device(): lax.all_to_all(answer, 'tile', split_axis=0, concat_axis=0, tiled=True)]
    slice x1 -> x0, local copies, waits for them, and re-layouts: 1.46 us -> none  [rim(): base[ROWS - 1:ROWS]]
  transfers between devices with their start and end apart: 10 -> 10, of which waited for: 2 -> 3; matrix products, arithmetic and copies ran while one was open for 2% -> 0% of each run, Pallas kernels for 9% -> 5%
where the time goes in v3:
time: 125 us
  waiting for transfers between devices  55.7 us (45%)
  Pallas kernels  36.6 us (29%)
  starting transfers between devices  31.8 us (25%)
    ppermute x2, waiting for transfers between devices, exchange(): west = lax.ppermute(right, 'tile', along)  31.7 us
    pallas_call x6, Pallas kernels, call(): pl.pallas_call(kernel, out_shape=out_shape, in_specs=[vmem] * arrays + [s...  25.6 us
    all_to_all x1, waiting for transfers between devices, on_device(): lax.all_to_all(answer, 'tile', split_axis=0, concat_axis=0, tiled=True)  20.8 us
    all_to_all x1, starting transfers between devices, on_device(): recv = lax.all_to_all(send, 'tile', split_axis=0, concat_axis=0, tiled=True)  12.3 us
    pallas_call x1, Pallas kernels, pack(): pl.pallas_call(pack_kernel, out_shape=(pltpu.HBM((TILES, SEND, CAP), BF16...  10.9 us
    ppermute x2, starting transfers between devices, exchange(): east = lax.ppermute(left, 'tile', [(b, a) for a, b in along])  10.1 us
    all_to_all x1, starting transfers between devices, on_device(): lax.all_to_all(answer, 'tile', split_axis=0, concat_axis=0, tiled=True)  5.36 us
    all_to_all x1, waiting for transfers between devices, on_device(): recv = lax.all_to_all(send, 'tile', split_axis=0, concat_axis=0, tiled=True)  3.15 us
  transfers between devices with their start and end apart: 10, of which 3 were waited for; matrix products, arithmetic and copies ran while one was open for 0% of the time, Pallas kernels for 5%

profile of v3, /device:TPU:6, one launch (start us, length us, event | category | flops | bytes accessed | tf_op | source)
XLA Modules:
  0.0 125.1 jit_solution(9490398958477692921)
XLA Ops:
  0.0 0.0 copy-start.2
  0.0 0.7 copy-done.2
  0.7 10.9 %shard_map.64 = (bf16[64,104,128]{2,1,0:T(8,128)(2,1)}, s32[16,256]{1,0:T(8,128)S(1)}) custom-call(bf16[48,16,256]{2,1,0:T(8,128)(2,1)} %temp_ref.5, bf16[48,16,256]{2,1,0:T(8,128)(2,1)} %humid_ref.3, s32[16,256]{1,0:T(8,128)S(1)} %copy-done.2), custom_call_target="tpu_custom_call" | custom-call | tf_op jit(solution)/shard_map/pallas_call | solution.py:127
  11.7 0.0 copy-start
  11.7 0.0 copy-start.5
  11.7 0.0 copy-start.3
  11.7 0.0 copy-start.4
  11.7 12.3 %all-to-all-start = ((bf16[64,104,128]{2,1,0:T(8,128)(2,1)}), bf16[64,104,128]{2,1,0:T(8,128)(2,1)S(1)}, u32[]{:S(2)}, u32[]{:S(2)}) async-start(bf16[64,104,128]{2,1,0:T(8,128)(2,1)} %get-tuple-element.28), calls=%async_computation | async-start | bytes 3407872 | tf_op jit(solution)/shard_map/all_to_all | solution.py:450
  24.0 0.0 copy-done
  24.0 1.2 shard_map.65
  25.2 0.5 collective-permute-start
  25.7 1.6 %collective-permute-start.1 = (bf16[48,256]{1,0:T(8,128)(2,1)S(1)}, bf16[48,256]{1,0:T(8,128)(2,1)S(1)}, u32[]{:S(2)}, u32[]{:S(2)}) collective-permute-start(bf16[48,256]{1,0:T(8,128)(2,1)S(1)} %get-tuple-element.30), channel_id=1, source_target_pairs={{64,0},{128,64},{192,128},{0,192},{65,1},{129,65},{193,129},{1,193... | collective-permute-start | bytes 73736 | tf_op jit(solution)/shard_map/ppermute | solution.py:442
  27.2 0.0 collective-permute-start.2
  27.2 5.1 %collective-permute-start.3 = (bf16[48,128]{1,0:T(8,128)(2,1)S(1)}, bf16[48,128]{1,0:T(8,128)(2,1)S(1)}, u32[]{:S(2)}, u32[]{:S(2)}) collective-permute-start(bf16[48,128]{1,0:T(8,128)(2,1)S(1)} %get-tuple-element.32), channel_id=1, source_target_pairs={{1,0},{2,1},{3,2},{4,3},{5,4},{6,5},{7,6},{8,7},{9,8},{10,9},{11,1... | collective-permute-start | bytes 36872 | tf_op jit(solution)/shard_map/ppermute | solution.py:444
  32.3 0.0 copy-done.5
  32.3 0.1 copy.8
  32.4 0.0 copy-start.1
  32.4 31.7 %collective-permute-done.2.left_ref = bf16[48,128]{1,0:T(8,128)(2,1)S(1)} collective-permute-done((bf16[48,128]{1,0:T(8,128)(2,1)S(1)}, bf16[48,128]{1,0:T(8,128)(2,1)S(1)}, u32[]{:S(2)}, u32[]{:S(2)}) %collective-permute-start.2) | collective-permute-done | bytes 12320 | tf_op jit(solution)/shard_map/ppermute | solution.py:443
  64.1 0.0 collective-permute-done.3.right_ref
  64.2 0.0 collective-permute-done.above_ref
  64.2 0.0 collective-permute-done.1.below_ref
  64.2 3.1 %all-to-all-done.recv_ref = bf16[64,104,128]{2,1,0:T(8,128)(2,1)S(1)} async-done(((bf16[64,104,128]{2,1,0:T(8,128)(2,1)}), bf16[64,104,128]{2,1,0:T(8,128)(2,1)S(1)}, u32[]{:S(2)}, u32[]{:S(2)}) %all-to-all-start) | async-done | bytes 1703968 | tf_op jit(solution)/shard_map/all_to_all | solution.py:450
  67.3 0.0 copy-done.3
  67.3 0.0 copy-done.4
  67.3 16.2 %shard_map.66 = bf16[64,48,128]{2,1,0:T(8,128)(2,1)} custom-call(bf16[64,104,128]{2,1,0:T(8,128)(2,1)S(1)} %all-to-all-done.recv_ref, f32[112,48]{1,0:T(8,128)S(1)} %broadcast_multiply_fusion.kabs_ref, f32[112]{0:T(128)S(1)} %copy-done.3, f32[112]{0:T(128)S(1)} %copy-done.4), custom_call_target="tpu_custom_call" | custom-call | tf_op jit(solution)/shard_map/pallas_call | solution.py:41
  83.5 5.4 %all-to-all-start.1 = ((bf16[64,48,128]{2,1,0:T(8,128)(2,1)}), bf16[64,48,128]{2,1,0:T(8,128)(2,1)S(1)}, u32[]{:S(2)}, u32[]{:S(2)}) async-start(bf16[64,48,128]{2,1,0:T(8,128)(2,1)} %shard_map.66), calls=%async_computation.1 | async-start | bytes 1572864 | tf_op jit(solution)/shard_map/all_to_all | solution.py:454
  88.9 0.0 copy-done.1
  88.9 2.1 %shard_map.67 = (f32[16,48,256]{2,1,0:T(8,128)S(1)}, f32[48,128]{1,0:T(8,128)S(1)}, s32[8,128]{1,0:T(8,128)S(1)}) custom-call(bf16[48,16,256]{2,1,0:T(8,128)(2,1)S(1)} %copy-done, bf16[48,16,256]{2,1,0:T(8,128)(2,1)S(1)} %copy-done.1, s32[16,256]{1,0:T(8,128)S(1)} %get-tuple-element.39.slot_ref, bf16[48,256]{1,0:T(8,128)(2,1)S(1)} %collective-permute-done.above_ref, ...), custom_call_target="tpu_custom_call" | custom-call | tf_op jit(solution)/shard_map/pallas_call | solution.py:41
  91.1 20.8 %all-to-all-done.1.ret_ref = bf16[64,48,128]{2,1,0:T(8,128)(2,1)S(1)} async-done(((bf16[64,48,128]{2,1,0:T(8,128)(2,1)}), bf16[64,48,128]{2,1,0:T(8,128)(2,1)S(1)}, u32[]{:S(2)}, u32[]{:S(2)}) %all-to-all-start.1) | async-done | bytes 786464 | tf_op jit(solution)/shard_map/all_to_all | solution.py:454
  111.8 0.9 shard_map.69
  112.8 0.5 collective-permute-start.4
  113.3 1.6 %collective-permute-start.5 = (bf16[48,256]{1,0:T(8,128)(2,1)S(1)}, bf16[48,256]{1,0:T(8,128)(2,1)S(1)}, u32[]{:S(2)}, u32[]{:S(2)}) collective-permute-start(bf16[48,256]{1,0:T(8,128)(2,1)S(1)} %get-tuple-element.48), channel_id=1, source_target_pairs={{64,0},{128,64},{192,128},{0,192},{65,1},{129,65},{193,129},{1,193... | collective-permute-start | bytes 73736 | tf_op jit(solution)/shard_map/ppermute | solution.py:442
  114.8 0.0 collective-permute-start.6
  114.8 5.1 %collective-permute-start.7 = (bf16[48,128]{1,0:T(8,128)(2,1)S(1)}, bf16[48,128]{1,0:T(8,128)(2,1)S(1)}, u32[]{:S(2)}, u32[]{:S(2)}) collective-permute-start(bf16[48,128]{1,0:T(8,128)(2,1)S(1)} %get-tuple-element.50), channel_id=1, source_target_pairs={{1,0},{2,1},{3,2},{4,3},{5,4},{6,5},{7,6},{8,7},{9,8},{10,9},{11,1... | collective-permute-start | bytes 36872 | tf_op jit(solution)/shard_map/ppermute | solution.py:444
  119.9 3.5 %shard_map.68.second_ref = bf16[16,48,256]{2,1,0:T(8,128)(2,1)S(1)} custom-call(bf16[64,48,128]{2,1,0:T(8,128)(2,1)S(1)} %all-to-all-done.1.ret_ref, s32[16,256]{1,0:T(8,128)S(1)} %get-tuple-element.39.slot_ref, f32[16,48,256]{2,1,0:T(8,128)S(1)} %get-tuple-element.44.base_ref), custom_call_target="tpu_custom_call" | custom-call | tf_op jit(solution)/shard_map/pallas_call | solution.py:41
  123.4 0.0 collective-permute-done.6.left_ref
  123.4 0.0 collective-permute-done.7.right_ref
  123.4 0.0 collective-permute-done.4.above_ref
  123.4 0.0 collective-permute-done.5.below_ref
  123.4 1.6 %shard_map.70 = bf16[48,16,256]{2,1,0:T(8,128)(2,1)} custom-call(bf16[16,48,256]{2,1,0:T(8,128)(2,1)S(1)} %shard_map.68.second_ref, bf16[48,256]{1,0:T(8,128)(2,1)S(1)} %collective-permute-done.4.above_ref, bf16[48,256]{1,0:T(8,128)(2,1)S(1)} %collective-permute-done.5.below_ref, bf16[48,128]{1,0:T(8,128)(2,1)S(1)} %collective-permute-done.6.left_ref, ...), custom_call_target="tpu_custom_call" | custom-call | tf_op jit(solution)/shard_map/pallas_call | solution.py:41
  (1 shorter events, 0.0 us)
Async XLA Ops:
  0.0 0.7 copy-start.2
  11.7 12.3 %copy-start = (bf16[48,16,256]{2,1,0:T(8,128)(2,1)S(1)}, bf16[48,16,256]{2,1,0:T(8,128)(2,1)}, u32[]{:S(2)}) copy-start(bf16[48,16,256]{2,1,0:T(8,128)(2,1)} %temp_ref.5) | copy-start | bytes 1179652
  11.7 20.6 %copy-start.5 = (f32[112,48]{0,1:T(8,128)S(1)}, f32[112,48]{0,1:T(8,128)}, u32[]{:S(2)}) copy-start(f32[112,48]{0,1:T(8,128)} %param.9) | copy-start | bytes 64516
  11.7 55.6 %copy-start.3 = (f32[112]{0:T(128)S(1)}, f32[112]{0:T(128)}, u32[]{:S(2)}) copy-start(f32[112]{0:T(128)} %planck_ref.1) | copy-start | bytes 1348
  11.7 55.6 %copy-start.4 = (f32[112]{0:T(128)S(1)}, f32[112]{0:T(128)}, u32[]{:S(2)}) copy-start(f32[112]{0:T(128)} %top_ref.1) | copy-start | bytes 1348
  11.7 55.6 %all-to-all-start = ((bf16[64,104,128]{2,1,0:T(8,128)(2,1)}), bf16[64,104,128]{2,1,0:T(8,128)(2,1)S(1)}, u32[]{:S(2)}, u32[]{:S(2)}) async-start(bf16[64,104,128]{2,1,0:T(8,128)(2,1)} %get-tuple-element.28), calls=%async_computation | async-start | bytes 3407872 | tf_op jit(solution)/shard_map/all_to_all | solution.py:450
  25.2 39.0 %collective-permute-start = (bf16[48,256]{1,0:T(8,128)(2,1)S(1)}, bf16[48,256]{1,0:T(8,128)(2,1)S(1)}, u32[]{:S(2)}, u32[]{:S(2)}) collective-permute-start(bf16[48,256]{1,0:T(8,128)(2,1)S(1)} %get-tuple-element.29), channel_id=1, source_target_pairs={{0,64},{64,128},{128,192},{192,0},{1,65},{65,129},{129,193},{193,1... | collective-permute-start | bytes 73736 | tf_op jit(solution)/shard_map/ppermute | solution.py:441
  25.7 38.5 %collective-permute-start.1 = (bf16[48,256]{1,0:T(8,128)(2,1)S(1)}, bf16[48,256]{1,0:T(8,128)(2,1)S(1)}, u32[]{:S(2)}, u32[]{:S(2)}) collective-permute-start(bf16[48,256]{1,0:T(8,128)(2,1)S(1)} %get-tuple-element.30), channel_id=1, source_target_pairs={{64,0},{128,64},{192,128},{0,192},{65,1},{129,65},{193,129},{1,193... | collective-permute-start | bytes 73736 | tf_op jit(solution)/shard_map/ppermute | solution.py:442
  27.2 36.9 %collective-permute-start.2 = (bf16[48,128]{1,0:T(8,128)(2,1)S(1)}, bf16[48,128]{1,0:T(8,128)(2,1)S(1)}, u32[]{:S(2)}, u32[]{:S(2)}) collective-permute-start(bf16[48,128]{1,0:T(8,128)(2,1)S(1)} %get-tuple-element.31), channel_id=1, source_target_pairs={{0,1},{1,2},{2,3},{3,4},{4,5},{5,6},{6,7},{7,8},{8,9},{9,10},{10,1... | collective-permute-start | bytes 36872 | tf_op jit(solution)/shard_map/ppermute | solution.py:443
  27.2 36.9 %collective-permute-start.3 = (bf16[48,128]{1,0:T(8,128)(2,1)S(1)}, bf16[48,128]{1,0:T(8,128)(2,1)S(1)}, u32[]{:S(2)}, u32[]{:S(2)}) collective-permute-start(bf16[48,128]{1,0:T(8,128)(2,1)S(1)} %get-tuple-element.32), channel_id=1, source_target_pairs={{1,0},{2,1},{3,2},{4,3},{5,4},{6,5},{7,6},{8,7},{9,8},{10,9},{11,1... | collective-permute-start | bytes 36872 | tf_op jit(solution)/shard_map/ppermute | solution.py:444
  32.4 56.5 %copy-start.1 = (bf16[48,16,256]{2,1,0:T(8,128)(2,1)S(1)}, bf16[48,16,256]{2,1,0:T(8,128)(2,1)}, u32[]{:S(2)}) copy-start(bf16[48,16,256]{2,1,0:T(8,128)(2,1)} %humid_ref.3) | copy-start | bytes 1179652
  83.5 28.3 %all-to-all-start.1 = ((bf16[64,48,128]{2,1,0:T(8,128)(2,1)}), bf16[64,48,128]{2,1,0:T(8,128)(2,1)S(1)}, u32[]{:S(2)}, u32[]{:S(2)}) async-start(bf16[64,48,128]{2,1,0:T(8,128)(2,1)} %shard_map.66), calls=%async_computation.1 | async-start | bytes 1572864 | tf_op jit(solution)/shard_map/all_to_all | solution.py:454
  112.8 10.7 %collective-permute-start.4 = (bf16[48,256]{1,0:T(8,128)(2,1)S(1)}, bf16[48,256]{1,0:T(8,128)(2,1)S(1)}, u32[]{:S(2)}, u32[]{:S(2)}) collective-permute-start(bf16[48,256]{1,0:T(8,128)(2,1)S(1)} %get-tuple-element.47), channel_id=1, source_target_pairs={{0,64},{64,128},{128,192},{192,0},{1,65},{65,129},{129,193},{193,1... | collective-permute-start | bytes 73736 | tf_op jit(solution)/shard_map/ppermute | solution.py:441
  113.3 10.2 %collective-permute-start.5 = (bf16[48,256]{1,0:T(8,128)(2,1)S(1)}, bf16[48,256]{1,0:T(8,128)(2,1)S(1)}, u32[]{:S(2)}, u32[]{:S(2)}) collective-permute-start(bf16[48,256]{1,0:T(8,128)(2,1)S(1)} %get-tuple-element.48), channel_id=1, source_target_pairs={{64,0},{128,64},{192,128},{0,192},{65,1},{129,65},{193,129},{1,193... | collective-permute-start | bytes 73736 | tf_op jit(solution)/shard_map/ppermute | solution.py:442
  114.8 8.6 %collective-permute-start.6 = (bf16[48,128]{1,0:T(8,128)(2,1)S(1)}, bf16[48,128]{1,0:T(8,128)(2,1)S(1)}, u32[]{:S(2)}, u32[]{:S(2)}) collective-permute-start(bf16[48,128]{1,0:T(8,128)(2,1)S(1)} %get-tuple-element.49), channel_id=1, source_target_pairs={{0,1},{1,2},{2,3},{3,4},{4,5},{5,6},{6,7},{7,8},{8,9},{9,10},{10,1... | collective-permute-start | bytes 36872 | tf_op jit(solution)/shard_map/ppermute | solution.py:443
  114.8 8.6 %collective-permute-start.7 = (bf16[48,128]{1,0:T(8,128)(2,1)S(1)}, bf16[48,128]{1,0:T(8,128)(2,1)S(1)}, u32[]{:S(2)}, u32[]{:S(2)}) collective-permute-start(bf16[48,128]{1,0:T(8,128)(2,1)S(1)} %get-tuple-element.50), channel_id=1, source_target_pairs={{1,0},{2,1},{3,2},{4,3},{5,4},{6,5},{7,6},{8,7},{9,8},{10,9},{11,1... | collective-permute-start | bytes 36872 | tf_op jit(solution)/shard_map/ppermute | solution.py:444

commit v4 on v3

--- a/solution.py
+++ b/solution.py
@@ -19,14 +19,14 @@
 BLK_ROW = 96
 ONE_ROW = 98
 SEND = 104
-WIDE = 112
+VALUES = 96
 GROUP = 8
-GB = 4
+GB = 7
 LOG2E = 1.4426950408889634
 VMEM = 32 * 1024 * 1024
 
 
-def call(kernel, out_shape, operands, scratch=(), scalars=0, resident_in=True, resident_out=True):
+def call(kernel, out_shape, operands, scratch=(), scalars=0, resident_in=True, out_space=pltpu.VMEM):
     vmem = pl.BlockSpec(memory_space=pltpu.VMEM)
     smem = pl.BlockSpec(memory_space=pltpu.SMEM)
     many = isinstance(out_shape, tuple)
@@ -35,21 +35,22 @@
         operands = [
             pltpu.with_memory_space_constraint(x, pltpu.VMEM) if i < arrays else x for i, x in enumerate(operands)
         ]
-    if resident_out:
-        place = lambda x: pltpu.VMEM(x.shape, x.dtype)
+    if out_space is not None:
+        place = lambda x: out_space(x.shape, x.dtype)
         out_shape = tuple(place(x) for x in out_shape) if many else place(out_shape)
+    out = pl.BlockSpec(memory_space=pltpu.HBM if out_space is pltpu.HBM else pltpu.VMEM)
     return pl.pallas_call(
         kernel,
         out_shape=out_shape,
         in_specs=[vmem] * arrays + [smem] * scalars,
-        out_specs=(vmem,) * len(out_shape) if many else vmem,
+        out_specs=(out,) * len(out_shape) if many else out,
         scratch_shapes=list(scratch),
         compiler_params=pltpu.CompilerParams(vmem_limit_bytes=VMEM),
     )(*operands)
 
 
 def pack_kernel(temp_ref, humid_ref, parent_ref, send_ref, slot_ref,
-                temp_in, humid_in, send_out, t_ref, h_ref, x_ref, b_ref, pair_ref, in_sem, out_sem):
+                temp_in, humid_in, send_out, t_ref, h_ref, x_ref, l_ref, b_ref, pair_ref, in_sem, out_sem):
     arriving = [
         pltpu.make_async_copy(temp_ref, temp_in, in_sem.at[0]),
         pltpu.make_async_copy(humid_ref, humid_in, in_sem.at[1]),
@@ -61,7 +62,7 @@
     before = (sub < lane).astype(BF16)
     ones = jnp.ones((COLS, COLS), BF16)
     sub64 = lax.broadcasted_iota(jnp.int32, (TILES, COLS), 0)
-    sub16 = lax.broadcasted_iota(jnp.int32, (16, COLS), 0)
+    sub8 = lax.broadcasted_iota(jnp.int32, (8, COLS), 0)
     parent = parent_ref[...]
     owner = parent // OWNED
     local = parent % OWNED
@@ -83,10 +84,9 @@
     within = (slot % 256).astype(F32).T.astype(BF16)
     for r in range(ROWS):
         cols = slice(r * COLS, (r + 1) * COLS)
-        extra = jnp.where(
-            sub16 == 0, blk[r : r + 1], jnp.where(sub16 == 1, low[r : r + 1], jnp.where(sub16 == 2, 1.0, 0.0))
+        l_ref[:, cols] = jnp.where(
+            sub8 == 0, blk[r : r + 1], jnp.where(sub8 == 1, low[r : r + 1], jnp.where(sub8 == 2, 1.0, 0.0))
         )
-        x_ref[2 * LEV : WIDE, cols] = extra.astype(BF16)
         b_ref[cols, :] = hot_across(within[:, r : r + 1])
         pair_ref[:, cols] = jnp.broadcast_to(pair[r : r + 1], (16, COLS)).astype(BF16)
 
@@ -99,19 +99,26 @@
         x_ref[0:LEV, cols] = t_ref[:, r, :].astype(BF16)
         x_ref[LEV : 2 * LEV, cols] = h_ref[:, r, :].astype(BF16)
 
-    values = x_ref[...].reshape(WIDE // 16, 16, CELLS)
+    values = x_ref[...].reshape(VALUES // 16, 16, CELLS)
+    labels = l_ref[...]
     leaving = []
     for step in range(PAIRS // GROUP):
         chosen = []
-        for j in range(GROUP):
-            mask = pair_ref[...] == jnp.asarray(step * GROUP + j, BF16)
-            chosen.append(jnp.where(mask[None], values, jnp.zeros_like(values)).reshape(WIDE, CELLS))
-        moved = jnp.dot(jnp.concatenate(chosen, axis=0), b_ref[...], preferred_element_type=F32)
+        extra = []
         for j in range(GROUP):
             p = step * GROUP + j
-            part = moved[j * WIDE : j * WIDE + SEND].astype(BF16)
-            send_out[2 * p] = part[:, 0:CAP]
-            send_out[2 * p + 1] = part[:, CAP : 2 * CAP]
+            mask = pair_ref[...] == jnp.asarray(p, BF16)
+            chosen.append(jnp.where(mask[None], values, jnp.zeros_like(values)).reshape(VALUES, CELLS))
+            extra.append(jnp.where(pair_ref[0:8, :].astype(F32) == float(p), labels, 0.0))
+        chosen.append(jnp.concatenate(extra, axis=0).astype(BF16))
+        moved = jnp.dot(jnp.concatenate(chosen, axis=0), b_ref[...], preferred_element_type=F32).astype(BF16)
+        for j in range(GROUP):
+            p = step * GROUP + j
+            part = moved[j * VALUES : (j + 1) * VALUES]
+            label = moved[GROUP * VALUES + 8 * j : GROUP * VALUES + 8 * (j + 1)]
+            for h in range(2):
+                send_out[2 * p + h, 0:VALUES, :] = part[:, h * CAP : (h + 1) * CAP]
+                send_out[2 * p + h, VALUES:SEND, :] = label[:, h * CAP : (h + 1) * CAP]
         done = pl.ds(2 * step * GROUP, 2 * GROUP)
         copy = pltpu.make_async_copy(send_out.at[done], send_ref.at[done], out_sem.at[step])
         copy.start()
@@ -138,7 +145,8 @@
             pltpu.VMEM((TILES, SEND, CAP), BF16),
             pltpu.VMEM(field, F32),
             pltpu.VMEM(field, F32),
-            pltpu.VMEM((WIDE, CELLS), BF16),
+            pltpu.VMEM((VALUES, CELLS), BF16),
+            pltpu.VMEM((8, CELLS), F32),
             pltpu.VMEM((CELLS, COLS), BF16),
             pltpu.VMEM((16, CELLS), BF16),
             pltpu.SemaphoreType.DMA((2,)),
@@ -167,7 +175,8 @@
 
 
 def owner_kernel(recv_ref, kabs_ref, planck_ref, top_ref, out_ref,
-                 b_ref, absorb_ref, emit_ref, step_ref, hmean_ref, net_ref, trans_ref, sum_ref, q_ref):
+                 b_ref, absorb_ref, emit_ref, step_ref, hmean_ref, net_ref, trans_ref, rise_ref, sum_ref, q_ref,
+                 answer_ref, out_sem):
     lows = jnp.concatenate([recv_ref[s, BLK_ROW:SEND, :].astype(F32)[1:2] for s in range(TILES)], axis=0)
     low_cols = lows.T.astype(BF16)
 
@@ -227,7 +236,10 @@
             net_ref[k] += total
             if k < LEV - 1:
                 step = step_ref[k]
-                state = [state[j] - step * planck[j] for j in range(GB)]
+                for j in range(GB):
+                    rise = step * planck[j]
+                    rise_ref[k, j] = rise
+                    state[j] = state[j] - rise
         state = [
             0.3 * (state[j] + emit_low * planck[j]) - emit_low * planck[j] for j in range(GB)
         ]
@@ -238,13 +250,12 @@
                 total = state[j] if total is None else total + state[j]
             net_ref[k] -= total
             if k > 0:
-                step = step_ref[k - 1]
-                state = [state[j] + step * planck[j] for j in range(GB)]
+                state = [state[j] + rise_ref[k - 1, j] for j in range(GB)]
         for j in range(GB):
             top_net = top_net + (tops[j] - (state[j] + emit_top * planck[j]))
         return top_net
 
-    top_net = lax.fori_loop(0, G // GB, one_block, jnp.zeros((8, 128), F32))
+    top_net = lax.fori_loop(0, G // GB, one_block, jnp.zeros((8, 128), F32), unroll=2)
     net = net_ref[...]
     prev = jnp.concatenate([top_net[None], net[:-1]], axis=0)
     heat = ((prev - net) * (LEV / G)).astype(BF16).astype(F32)
@@ -254,6 +265,7 @@
         for h in range(2):
             q_ref[b * LEV : (b + 1) * LEV, h * CAP : (h + 1) * CAP] = net_ref[:, 2 * b + h, :].astype(BF16)
 
+    leaving = []
     for p in range(PAIRS):
         both = jnp.dot(q_ref[...], b_ref[p], preferred_element_type=F32)
         for h in range(2):
@@ -262,7 +274,15 @@
             got = jnp.zeros((LEV, CAP), F32)
             for b in range(4):
                 got = jnp.where(blk == float(b + 1), both[b * LEV : (b + 1) * LEV, lanes], got)
-            out_ref[2 * p + h] = got.astype(BF16)
+            answer_ref[2 * p + h] = got.astype(BF16)
+        if p % (PAIRS // 4) == PAIRS // 4 - 1:
+            step = p // (PAIRS // 4)
+            done = pl.ds(step * (TILES // 4), TILES // 4)
+            copy = pltpu.make_async_copy(answer_ref.at[done], out_ref.at[done], out_sem.at[step])
+            copy.start()
+            leaving.append(copy)
+    for copy in leaving:
+        copy.wait()
 
 
 def owner_step(recv, kabs, planck, top_flux):
@@ -279,10 +299,14 @@
             column,
             column,
             pltpu.VMEM((LEV, GB, 8, 128), F32),
+            pltpu.VMEM((LEV, GB, 8, 128), F32),
             pltpu.VMEM((4 * SEND, 256), F32),
             pltpu.VMEM((4 * LEV, 256), BF16),
+            pltpu.VMEM((TILES, LEV, CAP), BF16),
+            pltpu.SemaphoreType.DMA((4,)),
         ],
         scalars=3,
+        out_space=pltpu.HBM,
     )
 
 
@@ -400,18 +424,20 @@
     )
 
 
-def unpack_kernel(ret_ref, slot_ref, base_ref, second_ref, r_ref):
+def unpack_kernel(ret_ref, slot_ref, base_ref, top_ref, bottom_ref, second_ref, r_ref):
     in_pairs(ret_ref, r_ref)
-    for r in range(ROWS):
+    second_ref[0] = top_ref[...]
+    second_ref[ROWS - 1] = bottom_ref[...]
+    for r in range(1, ROWS - 1):
         q = picked(r_ref, slot_ref[r : r + 1, :])
         second_ref[r] = (base_ref[r] + 0.5 * q).astype(BF16)
 
 
-def unpack(ret, slot, base):
+def unpack(ret, slot, base, top, bottom):
     return call(
         unpack_kernel,
         jax.ShapeDtypeStruct((ROWS, LEV, COLS), BF16),
-        (ret, slot, base),
+        (ret, slot, base, top, bottom),
         [pltpu.VMEM((PAIRS * LEV, 256), BF16)],
     )
 
@@ -429,7 +455,7 @@
         jax.ShapeDtypeStruct((LEV, ROWS, COLS), BF16),
         (second, *halo),
         [pltpu.VMEM((LEV, ROWS, COLS), F32)],
-        resident_out=False,
+        out_space=None,
     )
 
 
@@ -453,8 +479,9 @@
     answer, halo = lax.optimization_barrier((answer, halo))
     ret = lax.all_to_all(answer, "tile", split_axis=0, concat_axis=0, tiled=True)
     base, base_cols, slot_cols = base_step(temp, humid, slot, halo)
-    halo = exchange(*rim(ret, slot, slot_cols, base, base_cols))
-    second = unpack(ret, slot, base)
+    top, bottom, left, right = rim(ret, slot, slot_cols, base, base_cols)
+    halo = exchange(top, bottom, left, right)
+    second = unpack(ret, slot, base, top, bottom)
     return last_step(second, halo)
 
 

time: 125 us -> 124 us (level)
  Pallas kernels: 36.6 us -> 34.9 us
where the time goes in v4:
time: 124 us; the launch traced here: 123 us
  waiting for transfers between devices  55.7 us (45%)
  Pallas kernels  34.9 us (28%)
  starting transfers between devices  31.8 us (26%)
    ppermute x2, waiting for transfers between devices, exchange(): west = lax.ppermute(right, 'tile', along)  31.7 us
    pallas_call x6, Pallas kernels, call(): pl.pallas_call(kernel, out_shape=out_shape, in_specs=[vmem] * arrays + [s...  24.4 us
    all_to_all x1, waiting for transfers between devices, on_device(): lax.all_to_all(answer, 'tile', split_axis=0, concat_axis=0, tiled=True)  20.8 us
    all_to_all x1, starting transfers between devices, on_device(): recv = lax.all_to_all(send, 'tile', split_axis=0, concat_axis=0, tiled=True)  12.2 us
    pallas_call x1, Pallas kernels, pack(): pl.pallas_call(pack_kernel, out_shape=(pltpu.HBM((TILES, SEND, CAP), BF16...  10.5 us
    ppermute x2, starting transfers between devices, exchange(): east = lax.ppermute(left, 'tile', [(b, a) for a, b in along])  10.1 us
    all_to_all x1, starting transfers between devices, on_device(): lax.all_to_all(answer, 'tile', split_axis=0, concat_axis=0, tiled=True)  5.38 us
    all_to_all x1, waiting for transfers between devices, on_device(): recv = lax.all_to_all(send, 'tile', split_axis=0, concat_axis=0, tiled=True)  3.15 us
  transfers between devices with their start and end apart: 10, of which 3 were waited for; matrix products, arithmetic and copies ran while one was open for 0% of the time, Pallas kernels for 5%

profile of v4, /device:TPU:6, one launch (start us, length us, event | category | flops | bytes accessed | tf_op | source)
XLA Modules:
  0.0 123.4 jit_solution(12948235955190129689)
XLA Ops:
  0.0 0.0 copy-start.2
  0.0 0.7 copy-done.2
  0.7 10.5 %shard_map.64 = (bf16[64,104,128]{2,1,0:T(8,128)(2,1)}, s32[16,256]{1,0:T(8,128)S(1)}) custom-call(bf16[48,16,256]{2,1,0:T(8,128)(2,1)} %temp_ref.5, bf16[48,16,256]{2,1,0:T(8,128)(2,1)} %humid_ref.3, s32[16,256]{1,0:T(8,128)S(1)} %copy-done.2), custom_call_target="tpu_custom_call" | custom-call | tf_op jit(solution)/shard_map/pallas_call | solution.py:134
  11.2 0.0 copy-start
  11.2 0.0 copy-start.5
  11.2 0.0 copy-start.3
  11.2 0.0 copy-start.4
  11.2 12.2 %all-to-all-start = ((bf16[64,104,128]{2,1,0:T(8,128)(2,1)}), bf16[64,104,128]{2,1,0:T(8,128)(2,1)S(1)}, u32[]{:S(2)}, u32[]{:S(2)}) async-start(bf16[64,104,128]{2,1,0:T(8,128)(2,1)} %get-tuple-element.28), calls=%async_computation | async-start | bytes 3407872 | tf_op jit(solution)/shard_map/all_to_all | solution.py:476
  23.5 0.0 copy-done
  23.5 1.2 shard_map.65
  24.7 0.5 collective-permute-start
  25.2 1.5 %collective-permute-start.1 = (bf16[48,256]{1,0:T(8,128)(2,1)S(1)}, bf16[48,256]{1,0:T(8,128)(2,1)S(1)}, u32[]{:S(2)}, u32[]{:S(2)}) collective-permute-start(bf16[48,256]{1,0:T(8,128)(2,1)S(1)} %get-tuple-element.30), channel_id=1, source_target_pairs={{64,0},{128,64},{192,128},{0,192},{65,1},{129,65},{193,129},{1,193... | collective-permute-start | bytes 73736 | tf_op jit(solution)/shard_map/ppermute | solution.py:468
  26.8 0.0 collective-permute-start.2
  26.8 5.1 %collective-permute-start.3 = (bf16[48,128]{1,0:T(8,128)(2,1)S(1)}, bf16[48,128]{1,0:T(8,128)(2,1)S(1)}, u32[]{:S(2)}, u32[]{:S(2)}) collective-permute-start(bf16[48,128]{1,0:T(8,128)(2,1)S(1)} %get-tuple-element.32), channel_id=1, source_target_pairs={{1,0},{2,1},{3,2},{4,3},{5,4},{6,5},{7,6},{8,7},{9,8},{10,9},{11,1... | collective-permute-start | bytes 36872 | tf_op jit(solution)/shard_map/ppermute | solution.py:470
  31.8 0.0 copy-done.5
  31.8 0.1 copy.8
  31.9 0.0 copy-start.1
  31.9 31.7 %collective-permute-done.2.left_ref = bf16[48,128]{1,0:T(8,128)(2,1)S(1)} collective-permute-done((bf16[48,128]{1,0:T(8,128)(2,1)S(1)}, bf16[48,128]{1,0:T(8,128)(2,1)S(1)}, u32[]{:S(2)}, u32[]{:S(2)}) %collective-permute-start.2) | collective-permute-done | bytes 12320 | tf_op jit(solution)/shard_map/ppermute | solution.py:469
  63.7 0.0 collective-permute-done.3.right_ref
  63.7 0.0 collective-permute-done.above_ref
  63.7 0.0 collective-permute-done.1.below_ref
  63.7 3.1 %all-to-all-done.recv_ref = bf16[64,104,128]{2,1,0:T(8,128)(2,1)S(1)} async-done(((bf16[64,104,128]{2,1,0:T(8,128)(2,1)}), bf16[64,104,128]{2,1,0:T(8,128)(2,1)S(1)}, u32[]{:S(2)}, u32[]{:S(2)}) %all-to-all-start) | async-done | bytes 1703968 | tf_op jit(solution)/shard_map/all_to_all | solution.py:476
  66.8 0.0 copy-done.3
  66.8 0.0 copy-done.4
  66.8 15.4 %shard_map.66 = bf16[64,48,128]{2,1,0:T(8,128)(2,1)} custom-call(bf16[64,104,128]{2,1,0:T(8,128)(2,1)S(1)} %all-to-all-done.recv_ref, f32[112,48]{1,0:T(8,128)S(1)} %broadcast_multiply_fusion.kabs_ref, f32[112]{0:T(128)S(1)} %copy-done.3, f32[112]{0:T(128)S(1)} %copy-done.4), custom_call_target="tpu_custom_call" | custom-call | tf_op jit(solution)/shard_map/pallas_call | solution.py:42
  82.3 5.4 %all-to-all-start.1 = ((bf16[64,48,128]{2,1,0:T(8,128)(2,1)}), bf16[64,48,128]{2,1,0:T(8,128)(2,1)S(1)}, u32[]{:S(2)}, u32[]{:S(2)}) async-start(bf16[64,48,128]{2,1,0:T(8,128)(2,1)} %shard_map.66), calls=%async_computation.1 | async-start | bytes 1572864 | tf_op jit(solution)/shard_map/all_to_all | solution.py:480
  87.6 0.0 copy-done.1
  87.6 2.1 %shard_map.67 = (f32[16,48,256]{2,1,0:T(8,128)S(1)}, f32[48,128]{1,0:T(8,128)S(1)}, s32[8,128]{1,0:T(8,128)S(1)}) custom-call(bf16[48,16,256]{2,1,0:T(8,128)(2,1)S(1)} %copy-done, bf16[48,16,256]{2,1,0:T(8,128)(2,1)S(1)} %copy-done.1, s32[16,256]{1,0:T(8,128)S(1)} %get-tuple-element.39.slot_ref, bf16[48,256]{1,0:T(8,128)(2,1)S(1)} %collective-permute-done.above_ref, ...), custom_call_target="tpu_custom_call" | custom-call | tf_op jit(solution)/shard_map/pallas_call | solution.py:42
  89.8 20.8 %all-to-all-done.1.ret_ref = bf16[64,48,128]{2,1,0:T(8,128)(2,1)S(1)} async-done(((bf16[64,48,128]{2,1,0:T(8,128)(2,1)}), bf16[64,48,128]{2,1,0:T(8,128)(2,1)S(1)}, u32[]{:S(2)}, u32[]{:S(2)}) %all-to-all-start.1) | async-done | bytes 786464 | tf_op jit(solution)/shard_map/all_to_all | solution.py:480
  110.6 0.9 shard_map.68
  111.5 0.5 collective-permute-start.4
  112.0 1.5 %collective-permute-start.5 = (bf16[48,256]{1,0:T(8,128)(2,1)S(1)}, bf16[48,256]{1,0:T(8,128)(2,1)S(1)}, u32[]{:S(2)}, u32[]{:S(2)}) collective-permute-start(bf16[48,256]{1,0:T(8,128)(2,1)S(1)} %get-tuple-element.47.top_ref), channel_id=1, source_target_pairs={{64,0},{128,64},{192,128},{0,192},{65,1},{129,65},{193,129},{1,193... | collective-permute-start | bytes 73736 | tf_op jit(solution)/shard_map/ppermute | solution.py:468
  113.5 0.0 collective-permute-start.6
  113.5 5.1 %collective-permute-start.7 = (bf16[48,128]{1,0:T(8,128)(2,1)S(1)}, bf16[48,128]{1,0:T(8,128)(2,1)S(1)}, u32[]{:S(2)}, u32[]{:S(2)}) collective-permute-start(bf16[48,128]{1,0:T(8,128)(2,1)S(1)} %get-tuple-element.50), channel_id=1, source_target_pairs={{1,0},{2,1},{3,2},{4,3},{5,4},{6,5},{7,6},{8,7},{9,8},{10,9},{11,1... | collective-permute-start | bytes 36872 | tf_op jit(solution)/shard_map/ppermute | solution.py:470
  118.6 3.1 %shard_map.69.second_ref = bf16[16,48,256]{2,1,0:T(8,128)(2,1)S(1)} custom-call(bf16[64,48,128]{2,1,0:T(8,128)(2,1)S(1)} %all-to-all-done.1.ret_ref, s32[16,256]{1,0:T(8,128)S(1)} %get-tuple-element.39.slot_ref, f32[16,48,256]{2,1,0:T(8,128)S(1)} %get-tuple-element.44.base_ref, bf16[48,256]{1,0:T(8,128)(2,1)S(1)} %get-tuple-element.47.top_ref, ...), custom_call_target="tpu_custom_call" | custom-call | tf_op jit(solution)/shard_map/pallas_call | solution.py:42
  121.7 0.0 collective-permute-done.6.left_ref
  121.7 0.0 collective-permute-done.7.right_ref
  121.7 0.0 collective-permute-done.4.above_ref
  121.7 0.0 collective-permute-done.5.below_ref
  121.8 1.6 %shard_map.70 = bf16[48,16,256]{2,1,0:T(8,128)(2,1)} custom-call(bf16[16,48,256]{2,1,0:T(8,128)(2,1)S(1)} %shard_map.69.second_ref, bf16[48,256]{1,0:T(8,128)(2,1)S(1)} %collective-permute-done.4.above_ref, bf16[48,256]{1,0:T(8,128)(2,1)S(1)} %collective-permute-done.5.below_ref, bf16[48,128]{1,0:T(8,128)(2,1)S(1)} %collective-permute-done.6.left_ref, ...), custom_call_target="tpu_custom_call" | custom-call | tf_op jit(solution)/shard_map/pallas_call | solution.py:42
  (1 shorter events, 0.0 us)
Async XLA Ops:
  0.0 0.7 copy-start.2
  11.2 12.3 %copy-start = (bf16[48,16,256]{2,1,0:T(8,128)(2,1)S(1)}, bf16[48,16,256]{2,1,0:T(8,128)(2,1)}, u32[]{:S(2)}) copy-start(bf16[48,16,256]{2,1,0:T(8,128)(2,1)} %temp_ref.5) | copy-start | bytes 1179652
  11.2 20.6 %copy-start.5 = (f32[112,48]{0,1:T(8,128)S(1)}, f32[112,48]{0,1:T(8,128)}, u32[]{:S(2)}) copy-start(f32[112,48]{0,1:T(8,128)} %param.9) | copy-start | bytes 64516
  11.2 55.6 %copy-start.3 = (f32[112]{0:T(128)S(1)}, f32[112]{0:T(128)}, u32[]{:S(2)}) copy-start(f32[112]{0:T(128)} %planck_ref.1) | copy-start | bytes 1348
  11.2 55.6 %copy-start.4 = (f32[112]{0:T(128)S(1)}, f32[112]{0:T(128)}, u32[]{:S(2)}) copy-start(f32[112]{0:T(128)} %top_ref.1) | copy-start | bytes 1348
  11.2 55.6 %all-to-all-start = ((bf16[64,104,128]{2,1,0:T(8,128)(2,1)}), bf16[64,104,128]{2,1,0:T(8,128)(2,1)S(1)}, u32[]{:S(2)}, u32[]{:S(2)}) async-start(bf16[64,104,128]{2,1,0:T(8,128)(2,1)} %get-tuple-element.28), calls=%async_computation | async-start | bytes 3407872 | tf_op jit(solution)/shard_map/all_to_all | solution.py:476
  24.7 39.0 %collective-permute-start = (bf16[48,256]{1,0:T(8,128)(2,1)S(1)}, bf16[48,256]{1,0:T(8,128)(2,1)S(1)}, u32[]{:S(2)}, u32[]{:S(2)}) collective-permute-start(bf16[48,256]{1,0:T(8,128)(2,1)S(1)} %get-tuple-element.29), channel_id=1, source_target_pairs={{0,64},{64,128},{128,192},{192,0},{1,65},{65,129},{129,193},{193,1... | collective-permute-start | bytes 73736 | tf_op jit(solution)/shard_map/ppermute | solution.py:467
  25.2 38.5 %collective-permute-start.1 = (bf16[48,256]{1,0:T(8,128)(2,1)S(1)}, bf16[48,256]{1,0:T(8,128)(2,1)S(1)}, u32[]{:S(2)}, u32[]{:S(2)}) collective-permute-start(bf16[48,256]{1,0:T(8,128)(2,1)S(1)} %get-tuple-element.30), channel_id=1, source_target_pairs={{64,0},{128,64},{192,128},{0,192},{65,1},{129,65},{193,129},{1,193... | collective-permute-start | bytes 73736 | tf_op jit(solution)/shard_map/ppermute | solution.py:468
  26.8 36.9 %collective-permute-start.2 = (bf16[48,128]{1,0:T(8,128)(2,1)S(1)}, bf16[48,128]{1,0:T(8,128)(2,1)S(1)}, u32[]{:S(2)}, u32[]{:S(2)}) collective-permute-start(bf16[48,128]{1,0:T(8,128)(2,1)S(1)} %get-tuple-element.31), channel_id=1, source_target_pairs={{0,1},{1,2},{2,3},{3,4},{4,5},{5,6},{6,7},{7,8},{8,9},{9,10},{10,1... | collective-permute-start | bytes 36872 | tf_op jit(solution)/shard_map/ppermute | solution.py:469
  26.8 36.9 %collective-permute-start.3 = (bf16[48,128]{1,0:T(8,128)(2,1)S(1)}, bf16[48,128]{1,0:T(8,128)(2,1)S(1)}, u32[]{:S(2)}, u32[]{:S(2)}) collective-permute-start(bf16[48,128]{1,0:T(8,128)(2,1)S(1)} %get-tuple-element.32), channel_id=1, source_target_pairs={{1,0},{2,1},{3,2},{4,3},{5,4},{6,5},{7,6},{8,7},{9,8},{10,9},{11,1... | collective-permute-start | bytes 36872 | tf_op jit(solution)/shard_map/ppermute | solution.py:470
  31.9 55.7 %copy-start.1 = (bf16[48,16,256]{2,1,0:T(8,128)(2,1)S(1)}, bf16[48,16,256]{2,1,0:T(8,128)(2,1)}, u32[]{:S(2)}) copy-start(bf16[48,16,256]{2,1,0:T(8,128)(2,1)} %humid_ref.3) | copy-start | bytes 1179652
  82.3 28.3 %all-to-all-start.1 = ((bf16[64,48,128]{2,1,0:T(8,128)(2,1)}), bf16[64,48,128]{2,1,0:T(8,128)(2,1)S(1)}, u32[]{:S(2)}, u32[]{:S(2)}) async-start(bf16[64,48,128]{2,1,0:T(8,128)(2,1)} %shard_map.66), calls=%async_computation.1 | async-start | bytes 1572864 | tf_op jit(solution)/shard_map/all_to_all | solution.py:480
  111.5 10.2 %collective-permute-start.4 = (bf16[48,256]{1,0:T(8,128)(2,1)S(1)}, bf16[48,256]{1,0:T(8,128)(2,1)S(1)}, u32[]{:S(2)}, u32[]{:S(2)}) collective-permute-start(bf16[48,256]{1,0:T(8,128)(2,1)S(1)} %get-tuple-element.48.bottom_ref), channel_id=1, source_target_pairs={{0,64},{64,128},{128,192},{192,0},{1,65},{65,129},{129,193},{193,1... | collective-permute-start | bytes 73736 | tf_op jit(solution)/shard_map/ppermute | solution.py:467
  112.0 9.8 %collective-permute-start.5 = (bf16[48,256]{1,0:T(8,128)(2,1)S(1)}, bf16[48,256]{1,0:T(8,128)(2,1)S(1)}, u32[]{:S(2)}, u32[]{:S(2)}) collective-permute-start(bf16[48,256]{1,0:T(8,128)(2,1)S(1)} %get-tuple-element.47.top_ref), channel_id=1, source_target_pairs={{64,0},{128,64},{192,128},{0,192},{65,1},{129,65},{193,129},{1,193... | collective-permute-start | bytes 73736 | tf_op jit(solution)/shard_map/ppermute | solution.py:468
  113.5 8.2 %collective-permute-start.6 = (bf16[48,128]{1,0:T(8,128)(2,1)S(1)}, bf16[48,128]{1,0:T(8,128)(2,1)S(1)}, u32[]{:S(2)}, u32[]{:S(2)}) collective-permute-start(bf16[48,128]{1,0:T(8,128)(2,1)S(1)} %get-tuple-element.49), channel_id=1, source_target_pairs={{0,1},{1,2},{2,3},{3,4},{4,5},{5,6},{6,7},{7,8},{8,9},{9,10},{10,1... | collective-permute-start | bytes 36872 | tf_op jit(solution)/shard_map/ppermute | solution.py:469
  113.5 8.2 %collective-permute-start.7 = (bf16[48,128]{1,0:T(8,128)(2,1)S(1)}, bf16[48,128]{1,0:T(8,128)(2,1)S(1)}, u32[]{:S(2)}, u32[]{:S(2)}) collective-permute-start(bf16[48,128]{1,0:T(8,128)(2,1)S(1)} %get-tuple-element.50), channel_id=1, source_target_pairs={{1,0},{2,1},{3,2},{4,3},{5,4},{6,5},{7,6},{8,7},{9,8},{10,9},{11,1... | collective-permute-start | bytes 36872 | tf_op jit(solution)/shard_map/ppermute | solution.py:470

commit v5 on v4

--- a/solution.py
+++ b/solution.py
@@ -50,11 +50,13 @@
 
 
 def pack_kernel(temp_ref, humid_ref, parent_ref, send_ref, slot_ref,
-                temp_in, humid_in, send_out, t_ref, h_ref, x_ref, l_ref, b_ref, pair_ref, in_sem, out_sem):
+                temp_in, humid_in, parent_in, send_out, t_ref, h_ref, x_ref, l_ref, b_ref, pair_ref, in_sem, out_sem):
     arriving = [
         pltpu.make_async_copy(temp_ref, temp_in, in_sem.at[0]),
         pltpu.make_async_copy(humid_ref, humid_in, in_sem.at[1]),
     ]
+    named = pltpu.make_async_copy(parent_ref, parent_in, in_sem.at[2])
+    named.start()
     for copy in arriving:
         copy.start()
     sub = lax.broadcasted_iota(jnp.int32, (COLS, COLS), 0)
@@ -63,7 +65,8 @@
     ones = jnp.ones((COLS, COLS), BF16)
     sub64 = lax.broadcasted_iota(jnp.int32, (TILES, COLS), 0)
     sub8 = lax.broadcasted_iota(jnp.int32, (8, COLS), 0)
-    parent = parent_ref[...]
+    named.wait()
+    parent = parent_in[...]
     owner = parent // OWNED
     local = parent % OWNED
     blk = (local // 256 + 1).astype(F32)
@@ -137,11 +140,12 @@
             pltpu.HBM((TILES, SEND, CAP), BF16),
             pltpu.VMEM((ROWS, COLS), jnp.int32),
         ),
-        in_specs=[hbm, hbm, vmem],
+        in_specs=[hbm, hbm, hbm],
         out_specs=(hbm, vmem),
         scratch_shapes=[
             pltpu.VMEM(field, BF16),
             pltpu.VMEM(field, BF16),
+            pltpu.VMEM((ROWS, COLS), jnp.int32),
             pltpu.VMEM((TILES, SEND, CAP), BF16),
             pltpu.VMEM(field, F32),
             pltpu.VMEM(field, F32),
@@ -149,14 +153,14 @@
             pltpu.VMEM((8, CELLS), F32),
             pltpu.VMEM((CELLS, COLS), BF16),
             pltpu.VMEM((16, CELLS), BF16),
-            pltpu.SemaphoreType.DMA((2,)),
+            pltpu.SemaphoreType.DMA((3,)),
             pltpu.SemaphoreType.DMA((PAIRS // GROUP,)),
         ],
         compiler_params=pltpu.CompilerParams(vmem_limit_bytes=VMEM),
     )(
         pltpu.with_memory_space_constraint(temp, pltpu.HBM),
         pltpu.with_memory_space_constraint(humid, pltpu.HBM),
-        parent,
+        pltpu.with_memory_space_constraint(parent, pltpu.HBM),
     )
 
 
@@ -174,9 +178,11 @@
     return jnp.where(hit, jnp.ones_like(index), jnp.zeros_like(index))
 
 
-def owner_kernel(recv_ref, kabs_ref, planck_ref, top_ref, out_ref,
-                 b_ref, absorb_ref, emit_ref, step_ref, hmean_ref, net_ref, trans_ref, rise_ref, sum_ref, q_ref,
+def owner_kernel(recv_ref, kabs_in, planck_ref, top_ref, out_ref,
+                 kabs_ref, kabs_sem, b_ref, absorb_ref, emit_ref, step_ref, hmean_ref, net_ref, trans_ref, rise_ref, sum_ref, q_ref,
                  answer_ref, out_sem):
+    arriving = pltpu.make_async_copy(kabs_in, kabs_ref, kabs_sem)
+    arriving.start()
     lows = jnp.concatenate([recv_ref[s, BLK_ROW:SEND, :].astype(F32)[1:2] for s in range(TILES)], axis=0)
     low_cols = lows.T.astype(BF16)
 
@@ -255,6 +261,7 @@
             top_net = top_net + (tops[j] - (state[j] + emit_top * planck[j]))
         return top_net
 
+    arriving.wait()
     top_net = lax.fori_loop(0, G // GB, one_block, jnp.zeros((8, 128), F32), unroll=2)
     net = net_ref[...]
     prev = jnp.concatenate([top_net[None], net[:-1]], axis=0)
@@ -292,6 +299,8 @@
         jax.ShapeDtypeStruct((TILES, LEV, CAP), BF16),
         (recv, kabs * (-LOG2E), planck, top_flux),
         [
+            pltpu.SMEM((G, LEV), F32),
+            pltpu.SemaphoreType.DMA,
             pltpu.VMEM((PAIRS, 256, 256), BF16),
             column,
             column,
@@ -305,7 +314,7 @@
             pltpu.VMEM((TILES, LEV, CAP), BF16),
             pltpu.SemaphoreType.DMA((4,)),
         ],
-        scalars=3,
+        scalars=2,
         out_space=pltpu.HBM,
     )
 
@@ -442,20 +451,29 @@
     )
 
 
-def last_kernel(second_ref, above_ref, below_ref, left_ref, right_ref, out_ref, o_ref):
+def last_kernel(second_ref, above_ref, below_ref, left_ref, right_ref, out_ref, o_ref, whole_ref, out_sem):
     row_of = lambda r: second_ref[r].astype(F32)
     for r, value in stencil_rows(row_of, above_ref, below_ref, left_ref, right_ref):
         o_ref[:, r, :] = value
-    out_ref[...] = o_ref[...].astype(BF16)
+    leaving = []
+    for step in range(4):
+        done = pl.ds(step * (LEV // 4), LEV // 4)
+        whole_ref[done] = o_ref[done].astype(BF16)
+        copy = pltpu.make_async_copy(whole_ref.at[done], out_ref.at[done], out_sem.at[step])
+        copy.start()
+        leaving.append(copy)
+    for copy in leaving:
+        copy.wait()
 
 
 def last_step(second, halo):
+    field = (LEV, ROWS, COLS)
     return call(
         last_kernel,
-        jax.ShapeDtypeStruct((LEV, ROWS, COLS), BF16),
+        jax.ShapeDtypeStruct(field, BF16),
         (second, *halo),
-        [pltpu.VMEM((LEV, ROWS, COLS), F32)],
-        out_space=None,
+        [pltpu.VMEM(field, F32), pltpu.VMEM(field, BF16), pltpu.SemaphoreType.DMA((4,))],
+        out_space=pltpu.HBM,
     )
 
 

time: 124 us -> 122 us (0.984)
  no operation moved by 1% of the time
where the time goes in v5:
time: 122 us
  waiting for transfers between devices  55.7 us (46%)
  Pallas kernels  34.1 us (28%)
  starting transfers between devices  31.9 us (26%)
    ppermute x2, waiting for transfers between devices, exchange(): west = lax.ppermute(right, 'tile', along)  31.7 us
    pallas_call x6, Pallas kernels, call(): pl.pallas_call(kernel, out_shape=out_shape, in_specs=[vmem] * arrays + [s...  23.5 us
    all_to_all x1, waiting for transfers between devices, on_device(): lax.all_to_all(answer, 'tile', split_axis=0, concat_axis=0, tiled=True)  20.8 us
    all_to_all x1, starting transfers between devices, on_device(): recv = lax.all_to_all(send, 'tile', split_axis=0, concat_axis=0, tiled=True)  12.3 us
    pallas_call x1, Pallas kernels, pack(): pl.pallas_call(pack_kernel, out_shape=(pltpu.HBM((TILES, SEND, CAP), BF16...  10.6 us
    ppermute x2, starting transfers between devices, exchange(): east = lax.ppermute(left, 'tile', [(b, a) for a, b in along])  10.1 us
    all_to_all x1, starting transfers between devices, on_device(): lax.all_to_all(answer, 'tile', split_axis=0, concat_axis=0, tiled=True)  5.38 us
    all_to_all x1, waiting for transfers between devices, on_device(): recv = lax.all_to_all(send, 'tile', split_axis=0, concat_axis=0, tiled=True)  3.15 us
  transfers between devices with their start and end apart: 10, of which 3 were waited for; matrix products, arithmetic and copies ran while one was open for 0% of the time, Pallas kernels for 5%

profile of v5, /device:TPU:6, one launch (start us, length us, event | category | flops | bytes accessed | tf_op | source)
XLA Modules:
  0.0 122.1 jit_solution(15285050279893139793)
XLA Ops:
  0.0 10.6 %shard_map.64 = (bf16[64,104,128]{2,1,0:T(8,128)(2,1)}, s32[16,256]{1,0:T(8,128)S(1)}) custom-call(bf16[48,16,256]{2,1,0:T(8,128)(2,1)} %temp_ref.5, bf16[48,16,256]{2,1,0:T(8,128)(2,1)} %humid_ref.3, s32[16,256]{1,0:T(8,128)} %parent_ref.1), custom_call_target="tpu_custom_call" | custom-call | tf_op jit(solution)/shard_map/pallas_call | solution.py:137
  10.6 0.0 copy-start
  10.6 0.0 copy-start.4
  10.7 0.0 copy-start.2
  10.7 0.0 copy-start.3
  10.7 12.3 %all-to-all-start = ((bf16[64,104,128]{2,1,0:T(8,128)(2,1)}), bf16[64,104,128]{2,1,0:T(8,128)(2,1)S(1)}, u32[]{:S(2)}, u32[]{:S(2)}) async-start(bf16[64,104,128]{2,1,0:T(8,128)(2,1)} %get-tuple-element.28), calls=%async_computation | async-start | bytes 3407872 | tf_op jit(solution)/shard_map/all_to_all | solution.py:494
  22.9 0.0 copy-done
  22.9 1.2 shard_map.65
  24.1 0.5 collective-permute-start
  24.6 1.5 %collective-permute-start.1 = (bf16[48,256]{1,0:T(8,128)(2,1)S(1)}, bf16[48,256]{1,0:T(8,128)(2,1)S(1)}, u32[]{:S(2)}, u32[]{:S(2)}) collective-permute-start(bf16[48,256]{1,0:T(8,128)(2,1)S(1)} %get-tuple-element.30), channel_id=1, source_target_pairs={{64,0},{128,64},{192,128},{0,192},{65,1},{129,65},{193,129},{1,193... | collective-permute-start | bytes 73736 | tf_op jit(solution)/shard_map/ppermute | solution.py:486
  26.2 0.0 collective-permute-start.2
  26.2 5.1 %collective-permute-start.3 = (bf16[48,128]{1,0:T(8,128)(2,1)S(1)}, bf16[48,128]{1,0:T(8,128)(2,1)S(1)}, u32[]{:S(2)}, u32[]{:S(2)}) collective-permute-start(bf16[48,128]{1,0:T(8,128)(2,1)S(1)} %get-tuple-element.32), channel_id=1, source_target_pairs={{1,0},{2,1},{3,2},{4,3},{5,4},{6,5},{7,6},{8,7},{9,8},{10,9},{11,1... | collective-permute-start | bytes 36872 | tf_op jit(solution)/shard_map/ppermute | solution.py:488
  31.3 0.0 copy-done.4
  31.3 0.1 copy.8
  31.4 0.0 copy-start.1
  31.4 31.7 %collective-permute-done.2.left_ref = bf16[48,128]{1,0:T(8,128)(2,1)S(1)} collective-permute-done((bf16[48,128]{1,0:T(8,128)(2,1)S(1)}, bf16[48,128]{1,0:T(8,128)(2,1)S(1)}, u32[]{:S(2)}, u32[]{:S(2)}) %collective-permute-start.2) | collective-permute-done | bytes 12320 | tf_op jit(solution)/shard_map/ppermute | solution.py:487
  63.1 0.0 collective-permute-done.3.right_ref
  63.1 0.0 collective-permute-done.above_ref
  63.1 0.0 collective-permute-done.1.below_ref
  63.1 3.1 %all-to-all-done.recv_ref = bf16[64,104,128]{2,1,0:T(8,128)(2,1)S(1)} async-done(((bf16[64,104,128]{2,1,0:T(8,128)(2,1)}), bf16[64,104,128]{2,1,0:T(8,128)(2,1)S(1)}, u32[]{:S(2)}, u32[]{:S(2)}) %all-to-all-start) | async-done | bytes 1703968 | tf_op jit(solution)/shard_map/all_to_all | solution.py:494
  66.3 0.0 copy-done.2
  66.3 0.0 copy-done.3
  66.3 14.5 %shard_map.66 = bf16[64,48,128]{2,1,0:T(8,128)(2,1)} custom-call(bf16[64,104,128]{2,1,0:T(8,128)(2,1)S(1)} %all-to-all-done.recv_ref, f32[112,48]{1,0:T(8,128)S(1)} %broadcast_multiply_fusion.kabs_in, f32[112]{0:T(128)S(1)} %copy-done.2, f32[112]{0:T(128)S(1)} %copy-done.3), custom_call_target="tpu_custom_call" | custom-call | tf_op jit(solution)/shard_map/pallas_call | solution.py:42
  80.8 5.4 %all-to-all-start.1 = ((bf16[64,48,128]{2,1,0:T(8,128)(2,1)}), bf16[64,48,128]{2,1,0:T(8,128)(2,1)S(1)}, u32[]{:S(2)}, u32[]{:S(2)}) async-start(bf16[64,48,128]{2,1,0:T(8,128)(2,1)} %shard_map.66), calls=%async_computation.1 | async-start | bytes 1572864 | tf_op jit(solution)/shard_map/all_to_all | solution.py:498
  86.2 0.0 copy-done.1
  86.2 2.1 %shard_map.67 = (f32[16,48,256]{2,1,0:T(8,128)S(1)}, f32[48,128]{1,0:T(8,128)S(1)}, s32[8,128]{1,0:T(8,128)S(1)}) custom-call(bf16[48,16,256]{2,1,0:T(8,128)(2,1)S(1)} %copy-done, bf16[48,16,256]{2,1,0:T(8,128)(2,1)S(1)} %copy-done.1, s32[16,256]{1,0:T(8,128)S(1)} %get-tuple-element.39.slot_ref, bf16[48,256]{1,0:T(8,128)(2,1)S(1)} %collective-permute-done.above_ref, ...), custom_call_target="tpu_custom_call" | custom-call | tf_op jit(solution)/shard_map/pallas_call | solution.py:42
  88.3 20.8 %all-to-all-done.1.ret_ref = bf16[64,48,128]{2,1,0:T(8,128)(2,1)S(1)} async-done(((bf16[64,48,128]{2,1,0:T(8,128)(2,1)}), bf16[64,48,128]{2,1,0:T(8,128)(2,1)S(1)}, u32[]{:S(2)}, u32[]{:S(2)}) %all-to-all-start.1) | async-done | bytes 786464 | tf_op jit(solution)/shard_map/all_to_all | solution.py:498
  109.1 0.9 shard_map.68
  110.0 0.5 collective-permute-start.4
  110.5 1.5 %collective-permute-start.5 = (bf16[48,256]{1,0:T(8,128)(2,1)S(1)}, bf16[48,256]{1,0:T(8,128)(2,1)S(1)}, u32[]{:S(2)}, u32[]{:S(2)}) collective-permute-start(bf16[48,256]{1,0:T(8,128)(2,1)S(1)} %get-tuple-element.47.top_ref), channel_id=1, source_target_pairs={{64,0},{128,64},{192,128},{0,192},{65,1},{129,65},{193,129},{1,193... | collective-permute-start | bytes 73736 | tf_op jit(solution)/shard_map/ppermute | solution.py:486
  112.1 0.0 collective-permute-start.6
  112.1 5.1 %collective-permute-start.7 = (bf16[48,128]{1,0:T(8,128)(2,1)S(1)}, bf16[48,128]{1,0:T(8,128)(2,1)S(1)}, u32[]{:S(2)}, u32[]{:S(2)}) collective-permute-start(bf16[48,128]{1,0:T(8,128)(2,1)S(1)} %get-tuple-element.50), channel_id=1, source_target_pairs={{1,0},{2,1},{3,2},{4,3},{5,4},{6,5},{7,6},{8,7},{9,8},{10,9},{11,1... | collective-permute-start | bytes 36872 | tf_op jit(solution)/shard_map/ppermute | solution.py:488
  117.1 3.1 %shard_map.69.second_ref = bf16[16,48,256]{2,1,0:T(8,128)(2,1)S(1)} custom-call(bf16[64,48,128]{2,1,0:T(8,128)(2,1)S(1)} %all-to-all-done.1.ret_ref, s32[16,256]{1,0:T(8,128)S(1)} %get-tuple-element.39.slot_ref, f32[16,48,256]{2,1,0:T(8,128)S(1)} %get-tuple-element.44.base_ref, bf16[48,256]{1,0:T(8,128)(2,1)S(1)} %get-tuple-element.47.top_ref, ...), custom_call_target="tpu_custom_call" | custom-call | tf_op jit(solution)/shard_map/pallas_call | solution.py:42
  120.2 0.0 collective-permute-done.6.left_ref
  120.2 0.0 collective-permute-done.7.right_ref
  120.2 0.0 collective-permute-done.4.above_ref
  120.3 0.0 collective-permute-done.5.below_ref
  120.3 1.6 %shard_map.70 = bf16[48,16,256]{2,1,0:T(8,128)(2,1)} custom-call(bf16[16,48,256]{2,1,0:T(8,128)(2,1)S(1)} %shard_map.69.second_ref, bf16[48,256]{1,0:T(8,128)(2,1)S(1)} %collective-permute-done.4.above_ref, bf16[48,256]{1,0:T(8,128)(2,1)S(1)} %collective-permute-done.5.below_ref, bf16[48,128]{1,0:T(8,128)(2,1)S(1)} %collective-permute-done.6.left_ref, ...), custom_call_target="tpu_custom_call" | custom-call | tf_op jit(solution)/shard_map/pallas_call | solution.py:42
  (1 shorter events, 0.0 us)
Async XLA Ops:
  10.6 12.3 %copy-start = (bf16[48,16,256]{2,1,0:T(8,128)(2,1)S(1)}, bf16[48,16,256]{2,1,0:T(8,128)(2,1)}, u32[]{:S(2)}) copy-start(bf16[48,16,256]{2,1,0:T(8,128)(2,1)} %temp_ref.5) | copy-start | bytes 1179652
  10.6 20.6 %copy-start.4 = (f32[112,48]{0,1:T(8,128)S(1)}, f32[112,48]{0,1:T(8,128)}, u32[]{:S(2)}) copy-start(f32[112,48]{0,1:T(8,128)} %param.9) | copy-start | bytes 64516
  10.7 55.6 %copy-start.2 = (f32[112]{0:T(128)S(1)}, f32[112]{0:T(128)}, u32[]{:S(2)}) copy-start(f32[112]{0:T(128)} %planck_ref.1) | copy-start | bytes 1348
  10.7 55.6 %copy-start.3 = (f32[112]{0:T(128)S(1)}, f32[112]{0:T(128)}, u32[]{:S(2)}) copy-start(f32[112]{0:T(128)} %top_ref.1) | copy-start | bytes 1348
  10.7 55.6 %all-to-all-start = ((bf16[64,104,128]{2,1,0:T(8,128)(2,1)}), bf16[64,104,128]{2,1,0:T(8,128)(2,1)S(1)}, u32[]{:S(2)}, u32[]{:S(2)}) async-start(bf16[64,104,128]{2,1,0:T(8,128)(2,1)} %get-tuple-element.28), calls=%async_computation | async-start | bytes 3407872 | tf_op jit(solution)/shard_map/all_to_all | solution.py:494
  24.1 39.0 %collective-permute-start = (bf16[48,256]{1,0:T(8,128)(2,1)S(1)}, bf16[48,256]{1,0:T(8,128)(2,1)S(1)}, u32[]{:S(2)}, u32[]{:S(2)}) collective-permute-start(bf16[48,256]{1,0:T(8,128)(2,1)S(1)} %get-tuple-element.29), channel_id=1, source_target_pairs={{0,64},{64,128},{128,192},{192,0},{1,65},{65,129},{129,193},{193,1... | collective-permute-start | bytes 73736 | tf_op jit(solution)/shard_map/ppermute | solution.py:485
  24.6 38.5 %collective-permute-start.1 = (bf16[48,256]{1,0:T(8,128)(2,1)S(1)}, bf16[48,256]{1,0:T(8,128)(2,1)S(1)}, u32[]{:S(2)}, u32[]{:S(2)}) collective-permute-start(bf16[48,256]{1,0:T(8,128)(2,1)S(1)} %get-tuple-element.30), channel_id=1, source_target_pairs={{64,0},{128,64},{192,128},{0,192},{65,1},{129,65},{193,129},{1,193... | collective-permute-start | bytes 73736 | tf_op jit(solution)/shard_map/ppermute | solution.py:486
  26.2 36.9 %collective-permute-start.2 = (bf16[48,128]{1,0:T(8,128)(2,1)S(1)}, bf16[48,128]{1,0:T(8,128)(2,1)S(1)}, u32[]{:S(2)}, u32[]{:S(2)}) collective-permute-start(bf16[48,128]{1,0:T(8,128)(2,1)S(1)} %get-tuple-element.31), channel_id=1, source_target_pairs={{0,1},{1,2},{2,3},{3,4},{4,5},{5,6},{6,7},{7,8},{8,9},{9,10},{10,1... | collective-permute-start | bytes 36872 | tf_op jit(solution)/shard_map/ppermute | solution.py:487
  26.2 36.9 %collective-permute-start.3 = (bf16[48,128]{1,0:T(8,128)(2,1)S(1)}, bf16[48,128]{1,0:T(8,128)(2,1)S(1)}, u32[]{:S(2)}, u32[]{:S(2)}) collective-permute-start(bf16[48,128]{1,0:T(8,128)(2,1)S(1)} %get-tuple-element.32), channel_id=1, source_target_pairs={{1,0},{2,1},{3,2},{4,3},{5,4},{6,5},{7,6},{8,7},{9,8},{10,9},{11,1... | collective-permute-start | bytes 36872 | tf_op jit(solution)/shard_map/ppermute | solution.py:488
  31.4 54.8 %copy-start.1 = (bf16[48,16,256]{2,1,0:T(8,128)(2,1)S(1)}, bf16[48,16,256]{2,1,0:T(8,128)(2,1)}, u32[]{:S(2)}) copy-start(bf16[48,16,256]{2,1,0:T(8,128)(2,1)} %humid_ref.3) | copy-start | bytes 1179652
  80.8 28.3 %all-to-all-start.1 = ((bf16[64,48,128]{2,1,0:T(8,128)(2,1)}), bf16[64,48,128]{2,1,0:T(8,128)(2,1)S(1)}, u32[]{:S(2)}, u32[]{:S(2)}) async-start(bf16[64,48,128]{2,1,0:T(8,128)(2,1)} %shard_map.66), calls=%async_computation.1 | async-start | bytes 1572864 | tf_op jit(solution)/shard_map/all_to_all | solution.py:498
  110.0 10.2 %collective-permute-start.4 = (bf16[48,256]{1,0:T(8,128)(2,1)S(1)}, bf16[48,256]{1,0:T(8,128)(2,1)S(1)}, u32[]{:S(2)}, u32[]{:S(2)}) collective-permute-start(bf16[48,256]{1,0:T(8,128)(2,1)S(1)} %get-tuple-element.48.bottom_ref), channel_id=1, source_target_pairs={{0,64},{64,128},{128,192},{192,0},{1,65},{65,129},{129,193},{193,1... | collective-permute-start | bytes 73736 | tf_op jit(solution)/shard_map/ppermute | solution.py:485
  110.5 9.8 %collective-permute-start.5 = (bf16[48,256]{1,0:T(8,128)(2,1)S(1)}, bf16[48,256]{1,0:T(8,128)(2,1)S(1)}, u32[]{:S(2)}, u32[]{:S(2)}) collective-permute-start(bf16[48,256]{1,0:T(8,128)(2,1)S(1)} %get-tuple-element.47.top_ref), channel_id=1, source_target_pairs={{64,0},{128,64},{192,128},{0,192},{65,1},{129,65},{193,129},{1,193... | collective-permute-start | bytes 73736 | tf_op jit(solution)/shard_map/ppermute | solution.py:486
  112.1 8.2 %collective-permute-start.6 = (bf16[48,128]{1,0:T(8,128)(2,1)S(1)}, bf16[48,128]{1,0:T(8,128)(2,1)S(1)}, u32[]{:S(2)}, u32[]{:S(2)}) collective-permute-start(bf16[48,128]{1,0:T(8,128)(2,1)S(1)} %get-tuple-element.49), channel_id=1, source_target_pairs={{0,1},{1,2},{2,3},{3,4},{4,5},{5,6},{6,7},{7,8},{8,9},{9,10},{10,1... | collective-permute-start | bytes 36872 | tf_op jit(solution)/shard_map/ppermute | solution.py:487
  112.1 8.2 %collective-permute-start.7 = (bf16[48,128]{1,0:T(8,128)(2,1)S(1)}, bf16[48,128]{1,0:T(8,128)(2,1)S(1)}, u32[]{:S(2)}, u32[]{:S(2)}) collective-permute-start(bf16[48,128]{1,0:T(8,128)(2,1)S(1)} %get-tuple-element.50), channel_id=1, source_target_pairs={{1,0},{2,1},{3,2},{4,3},{5,4},{6,5},{7,6},{8,7},{9,8},{10,9},{11,1... | collective-permute-start | bytes 36872 | tf_op jit(solution)/shard_map/ppermute | solution.py:488

commit v6 on v5

--- a/solution.py
+++ b/solution.py
@@ -178,10 +178,10 @@
     return jnp.where(hit, jnp.ones_like(index), jnp.zeros_like(index))
 
 
-def owner_kernel(recv_ref, kabs_in, planck_ref, top_ref, out_ref,
-                 kabs_ref, kabs_sem, b_ref, absorb_ref, emit_ref, step_ref, hmean_ref, net_ref, trans_ref, rise_ref, sum_ref, q_ref,
+def owner_kernel(recv_ref, table_in, out_ref,
+                 table_ref, table_sem, b_ref, absorb_ref, emit_ref, step_ref, hmean_ref, net_ref, trans_ref, rise_ref, sum_ref, q_ref,
                  answer_ref, out_sem):
-    arriving = pltpu.make_async_copy(kabs_in, kabs_ref, kabs_sem)
+    arriving = pltpu.make_async_copy(table_in, table_ref, table_sem)
     arriving.start()
     lows = jnp.concatenate([recv_ref[s, BLK_ROW:SEND, :].astype(F32)[1:2] for s in range(TILES)], axis=0)
     low_cols = lows.T.astype(BF16)
@@ -228,14 +228,14 @@
 
     def one_block(block, top_net):
         first = block * GB
-        tops = [top_ref[first + j] for j in range(GB)]
-        planck = [planck_ref[first + j] for j in range(GB)]
+        tops = [table_ref[first + j, LEV + 1] for j in range(GB)]
+        planck = [table_ref[first + j, LEV] for j in range(GB)]
         state = [tops[j] - emit_top * planck[j] for j in range(GB)]
         for k in range(LEV):
             absorb = absorb_ref[k]
             total = None
             for j in range(GB):
-                t = jnp.exp2(absorb * kabs_ref[first + j, k])
+                t = jnp.exp2(absorb * table_ref[first + j, k])
                 trans_ref[k, j] = t
                 state[j] = t * state[j]
                 total = state[j] if total is None else total + state[j]
@@ -297,9 +297,9 @@
     return call(
         owner_kernel,
         jax.ShapeDtypeStruct((TILES, LEV, CAP), BF16),
-        (recv, kabs * (-LOG2E), planck, top_flux),
+        (recv, jnp.concatenate([kabs * (-LOG2E), planck[:, None], top_flux[:, None]], axis=1)),
         [
-            pltpu.SMEM((G, LEV), F32),
+            pltpu.SMEM((G, LEV + 2), F32),
             pltpu.SemaphoreType.DMA,
             pltpu.VMEM((PAIRS, 256, 256), BF16),
             column,
@@ -314,7 +314,6 @@
             pltpu.VMEM((TILES, LEV, CAP), BF16),
             pltpu.SemaphoreType.DMA((4,)),
         ],
-        scalars=2,
         out_space=pltpu.HBM,
     )
 

time: 122 us -> 122 us (level)
  no operation moved by 1% of the time
where the time goes in v6:
time: 122 us
  waiting for transfers between devices  55.3 us (45%)
  Pallas kernels  33.6 us (28%)
  starting transfers between devices  31.9 us (26%)
    ppermute x2, waiting for transfers between devices, exchange(): west = lax.ppermute(right, 'tile', along)  31.4 us
    pallas_call x6, Pallas kernels, call(): pl.pallas_call(kernel, out_shape=out_shape, in_specs=[vmem] * arrays + [s...  23 us
    all_to_all x1, waiting for transfers between devices, on_device(): lax.all_to_all(answer, 'tile', split_axis=0, concat_axis=0, tiled=True)  20.8 us
    all_to_all x1, starting transfers between devices, on_device(): recv = lax.all_to_all(send, 'tile', split_axis=0, concat_axis=0, tiled=True)  12.3 us
    pallas_call x1, Pallas kernels, pack(): pl.pallas_call(pack_kernel, out_shape=(pltpu.HBM((TILES, SEND, CAP), BF16...  10.6 us
    ppermute x2, starting transfers between devices, exchange(): east = lax.ppermute(left, 'tile', [(b, a) for a, b in along])  10.1 us
    all_to_all x1, starting transfers between devices, on_device(): lax.all_to_all(answer, 'tile', split_axis=0, concat_axis=0, tiled=True)  5.38 us
    all_to_all x1, waiting for transfers between devices, on_device(): recv = lax.all_to_all(send, 'tile', split_axis=0, concat_axis=0, tiled=True)  3.15 us
  transfers between devices with their start and end apart: 10, of which 3 were waited for; matrix products, arithmetic and copies ran while one was open for 0% of the time, Pallas kernels for 5%

profile of v6, /device:TPU:6, one launch (start us, length us, event | category | flops | bytes accessed | tf_op | source)
XLA Modules:
  0.0 121.6 jit_solution(17473013191870917833)
XLA Ops:
  0.0 10.6 %shard_map.64 = (bf16[64,104,128]{2,1,0:T(8,128)(2,1)}, s32[16,256]{1,0:T(8,128)S(1)}) custom-call(bf16[48,16,256]{2,1,0:T(8,128)(2,1)} %temp_ref.5, bf16[48,16,256]{2,1,0:T(8,128)(2,1)} %humid_ref.3, s32[16,256]{1,0:T(8,128)} %parent_ref.1), custom_call_target="tpu_custom_call" | custom-call | tf_op jit(solution)/shard_map/pallas_call | solution.py:137
  10.6 0.0 copy-start
  10.6 0.0 copy-start.3
  10.7 0.0 copy-start.4
  10.7 0.0 copy-start.2
  10.7 12.3 %all-to-all-start = ((bf16[64,104,128]{2,1,0:T(8,128)(2,1)}), bf16[64,104,128]{2,1,0:T(8,128)(2,1)S(1)}, u32[]{:S(2)}, u32[]{:S(2)}) async-start(bf16[64,104,128]{2,1,0:T(8,128)(2,1)} %get-tuple-element.28), calls=%async_computation | async-start | bytes 3407872 | tf_op jit(solution)/shard_map/all_to_all | solution.py:493
  22.9 0.0 copy-done
  22.9 1.2 shard_map.65
  24.1 0.5 collective-permute-start
  24.6 1.5 %collective-permute-start.1 = (bf16[48,256]{1,0:T(8,128)(2,1)S(1)}, bf16[48,256]{1,0:T(8,128)(2,1)S(1)}, u32[]{:S(2)}, u32[]{:S(2)}) collective-permute-start(bf16[48,256]{1,0:T(8,128)(2,1)S(1)} %get-tuple-element.30), channel_id=1, source_target_pairs={{64,0},{128,64},{192,128},{0,192},{65,1},{129,65},{193,129},{1,193... | collective-permute-start | bytes 73736 | tf_op jit(solution)/shard_map/ppermute | solution.py:485
  26.2 0.0 collective-permute-start.2
  26.2 5.1 %collective-permute-start.3 = (bf16[48,128]{1,0:T(8,128)(2,1)S(1)}, bf16[48,128]{1,0:T(8,128)(2,1)S(1)}, u32[]{:S(2)}, u32[]{:S(2)}) collective-permute-start(bf16[48,128]{1,0:T(8,128)(2,1)S(1)} %get-tuple-element.32), channel_id=1, source_target_pairs={{1,0},{2,1},{3,2},{4,3},{5,4},{6,5},{7,6},{8,7},{9,8},{10,9},{11,1... | collective-permute-start | bytes 36872 | tf_op jit(solution)/shard_map/ppermute | solution.py:487
  31.3 0.0 copy-done.3
  31.3 0.1 copy.13
  31.4 0.0 copy-done.4
  31.4 0.1 copy.12
  31.5 0.0 copy-done.2
  31.5 0.1 copy.10
  31.6 0.1 pad_maximum_fusion.table_in
  31.7 0.0 copy-start.1
  31.7 31.4 %collective-permute-done.2.left_ref = bf16[48,128]{1,0:T(8,128)(2,1)S(1)} collective-permute-done((bf16[48,128]{1,0:T(8,128)(2,1)S(1)}, bf16[48,128]{1,0:T(8,128)(2,1)S(1)}, u32[]{:S(2)}, u32[]{:S(2)}) %collective-permute-start.2) | collective-permute-done | bytes 12320 | tf_op jit(solution)/shard_map/ppermute | solution.py:486
  63.1 0.0 collective-permute-done.3.right_ref
  63.1 0.0 collective-permute-done.above_ref
  63.1 0.0 collective-permute-done.1.below_ref
  63.1 3.1 %all-to-all-done.recv_ref = bf16[64,104,128]{2,1,0:T(8,128)(2,1)S(1)} async-done(((bf16[64,104,128]{2,1,0:T(8,128)(2,1)}), bf16[64,104,128]{2,1,0:T(8,128)(2,1)S(1)}, u32[]{:S(2)}, u32[]{:S(2)}) %all-to-all-start) | async-done | bytes 1703968 | tf_op jit(solution)/shard_map/all_to_all | solution.py:493
  66.3 14.0 %shard_map.66 = bf16[64,48,128]{2,1,0:T(8,128)(2,1)} custom-call(bf16[64,104,128]{2,1,0:T(8,128)(2,1)S(1)} %all-to-all-done.recv_ref, f32[112,50]{1,0:T(8,128)S(1)} %pad_maximum_fusion.table_in), custom_call_target="tpu_custom_call" | custom-call | tf_op jit(solution)/shard_map/pallas_call | solution.py:42
  80.3 5.4 %all-to-all-start.1 = ((bf16[64,48,128]{2,1,0:T(8,128)(2,1)}), bf16[64,48,128]{2,1,0:T(8,128)(2,1)S(1)}, u32[]{:S(2)}, u32[]{:S(2)}) async-start(bf16[64,48,128]{2,1,0:T(8,128)(2,1)} %shard_map.66), calls=%async_computation.1 | async-start | bytes 1572864 | tf_op jit(solution)/shard_map/all_to_all | solution.py:497
  85.6 0.0 copy-done.1
  85.7 2.1 %shard_map.67 = (f32[16,48,256]{2,1,0:T(8,128)S(1)}, f32[48,128]{1,0:T(8,128)S(1)}, s32[8,128]{1,0:T(8,128)S(1)}) custom-call(bf16[48,16,256]{2,1,0:T(8,128)(2,1)S(1)} %copy-done, bf16[48,16,256]{2,1,0:T(8,128)(2,1)S(1)} %copy-done.1, s32[16,256]{1,0:T(8,128)S(1)} %get-tuple-element.39.slot_ref, bf16[48,256]{1,0:T(8,128)(2,1)S(1)} %collective-permute-done.above_ref, ...), custom_call_target="tpu_custom_call" | custom-call | tf_op jit(solution)/shard_map/pallas_call | solution.py:42
  87.8 20.8 %all-to-all-done.1.ret_ref = bf16[64,48,128]{2,1,0:T(8,128)(2,1)S(1)} async-done(((bf16[64,48,128]{2,1,0:T(8,128)(2,1)}), bf16[64,48,128]{2,1,0:T(8,128)(2,1)S(1)}, u32[]{:S(2)}, u32[]{:S(2)}) %all-to-all-start.1) | async-done | bytes 786464 | tf_op jit(solution)/shard_map/all_to_all | solution.py:497
  108.6 0.9 shard_map.68
  109.5 0.5 collective-permute-start.4
  110.0 1.5 %collective-permute-start.5 = (bf16[48,256]{1,0:T(8,128)(2,1)S(1)}, bf16[48,256]{1,0:T(8,128)(2,1)S(1)}, u32[]{:S(2)}, u32[]{:S(2)}) collective-permute-start(bf16[48,256]{1,0:T(8,128)(2,1)S(1)} %get-tuple-element.47.top_ref), channel_id=1, source_target_pairs={{64,0},{128,64},{192,128},{0,192},{65,1},{129,65},{193,129},{1,193... | collective-permute-start | bytes 73736 | tf_op jit(solution)/shard_map/ppermute | solution.py:485
  111.5 0.0 collective-permute-start.6
  111.6 5.1 %collective-permute-start.7 = (bf16[48,128]{1,0:T(8,128)(2,1)S(1)}, bf16[48,128]{1,0:T(8,128)(2,1)S(1)}, u32[]{:S(2)}, u32[]{:S(2)}) collective-permute-start(bf16[48,128]{1,0:T(8,128)(2,1)S(1)} %get-tuple-element.50), channel_id=1, source_target_pairs={{1,0},{2,1},{3,2},{4,3},{5,4},{6,5},{7,6},{8,7},{9,8},{10,9},{11,1... | collective-permute-start | bytes 36872 | tf_op jit(solution)/shard_map/ppermute | solution.py:487
  116.6 3.1 %shard_map.69.second_ref = bf16[16,48,256]{2,1,0:T(8,128)(2,1)S(1)} custom-call(bf16[64,48,128]{2,1,0:T(8,128)(2,1)S(1)} %all-to-all-done.1.ret_ref, s32[16,256]{1,0:T(8,128)S(1)} %get-tuple-element.39.slot_ref, f32[16,48,256]{2,1,0:T(8,128)S(1)} %get-tuple-element.44.base_ref, bf16[48,256]{1,0:T(8,128)(2,1)S(1)} %get-tuple-element.47.top_ref, ...), custom_call_target="tpu_custom_call" | custom-call | tf_op jit(solution)/shard_map/pallas_call | solution.py:42
  119.7 0.0 collective-permute-done.6.left_ref
  119.7 0.0 collective-permute-done.7.right_ref
  119.7 0.0 collective-permute-done.4.above_ref
  119.8 0.0 collective-permute-done.5.below_ref
  119.8 1.6 %shard_map.70 = bf16[48,16,256]{2,1,0:T(8,128)(2,1)} custom-call(bf16[16,48,256]{2,1,0:T(8,128)(2,1)S(1)} %shard_map.69.second_ref, bf16[48,256]{1,0:T(8,128)(2,1)S(1)} %collective-permute-done.4.above_ref, bf16[48,256]{1,0:T(8,128)(2,1)S(1)} %collective-permute-done.5.below_ref, bf16[48,128]{1,0:T(8,128)(2,1)S(1)} %collective-permute-done.6.left_ref, ...), custom_call_target="tpu_custom_call" | custom-call | tf_op jit(solution)/shard_map/pallas_call | solution.py:42
  (1 shorter events, 0.0 us)
Async XLA Ops:
  10.6 12.3 %copy-start = (bf16[48,16,256]{2,1,0:T(8,128)(2,1)S(1)}, bf16[48,16,256]{2,1,0:T(8,128)(2,1)}, u32[]{:S(2)}) copy-start(bf16[48,16,256]{2,1,0:T(8,128)(2,1)} %temp_ref.5) | copy-start | bytes 1179652
  10.6 20.6 %copy-start.3 = (f32[112]{0:T(128)S(1)}, f32[112]{0:T(128)}, u32[]{:S(2)}) copy-start(f32[112]{0:T(128)} %param.11) | copy-start | bytes 1348
  10.7 20.7 %copy-start.4 = (f32[112]{0:T(128)S(1)}, f32[112]{0:T(128)}, u32[]{:S(2)}) copy-start(f32[112]{0:T(128)} %param.10) | copy-start | bytes 1348
  10.7 20.8 %copy-start.2 = (f32[112,48]{0,1:T(8,128)S(1)}, f32[112,48]{0,1:T(8,128)}, u32[]{:S(2)}) copy-start(f32[112,48]{0,1:T(8,128)} %param.9) | copy-start | bytes 64516
  10.7 55.6 %all-to-all-start = ((bf16[64,104,128]{2,1,0:T(8,128)(2,1)}), bf16[64,104,128]{2,1,0:T(8,128)(2,1)S(1)}, u32[]{:S(2)}, u32[]{:S(2)}) async-start(bf16[64,104,128]{2,1,0:T(8,128)(2,1)} %get-tuple-element.28), calls=%async_computation | async-start | bytes 3407872 | tf_op jit(solution)/shard_map/all_to_all | solution.py:493
  24.1 39.0 %collective-permute-start = (bf16[48,256]{1,0:T(8,128)(2,1)S(1)}, bf16[48,256]{1,0:T(8,128)(2,1)S(1)}, u32[]{:S(2)}, u32[]{:S(2)}) collective-permute-start(bf16[48,256]{1,0:T(8,128)(2,1)S(1)} %get-tuple-element.29), channel_id=1, source_target_pairs={{0,64},{64,128},{128,192},{192,0},{1,65},{65,129},{129,193},{193,1... | collective-permute-start | bytes 73736 | tf_op jit(solution)/shard_map/ppermute | solution.py:484
  24.6 38.5 %collective-permute-start.1 = (bf16[48,256]{1,0:T(8,128)(2,1)S(1)}, bf16[48,256]{1,0:T(8,128)(2,1)S(1)}, u32[]{:S(2)}, u32[]{:S(2)}) collective-permute-start(bf16[48,256]{1,0:T(8,128)(2,1)S(1)} %get-tuple-element.30), channel_id=1, source_target_pairs={{64,0},{128,64},{192,128},{0,192},{65,1},{129,65},{193,129},{1,193... | collective-permute-start | bytes 73736 | tf_op jit(solution)/shard_map/ppermute | solution.py:485
  26.2 36.9 %collective-permute-start.2 = (bf16[48,128]{1,0:T(8,128)(2,1)S(1)}, bf16[48,128]{1,0:T(8,128)(2,1)S(1)}, u32[]{:S(2)}, u32[]{:S(2)}) collective-permute-start(bf16[48,128]{1,0:T(8,128)(2,1)S(1)} %get-tuple-element.31), channel_id=1, source_target_pairs={{0,1},{1,2},{2,3},{3,4},{4,5},{5,6},{6,7},{7,8},{8,9},{9,10},{10,1... | collective-permute-start | bytes 36872 | tf_op jit(solution)/shard_map/ppermute | solution.py:486
  26.2 36.9 %collective-permute-start.3 = (bf16[48,128]{1,0:T(8,128)(2,1)S(1)}, bf16[48,128]{1,0:T(8,128)(2,1)S(1)}, u32[]{:S(2)}, u32[]{:S(2)}) collective-permute-start(bf16[48,128]{1,0:T(8,128)(2,1)S(1)} %get-tuple-element.32), channel_id=1, source_target_pairs={{1,0},{2,1},{3,2},{4,3},{5,4},{6,5},{7,6},{8,7},{9,8},{10,9},{11,1... | collective-permute-start | bytes 36872 | tf_op jit(solution)/shard_map/ppermute | solution.py:487
  31.7 54.0 %copy-start.1 = (bf16[48,16,256]{2,1,0:T(8,128)(2,1)S(1)}, bf16[48,16,256]{2,1,0:T(8,128)(2,1)}, u32[]{:S(2)}) copy-start(bf16[48,16,256]{2,1,0:T(8,128)(2,1)} %humid_ref.3) | copy-start | bytes 1179652
  80.3 28.3 %all-to-all-start.1 = ((bf16[64,48,128]{2,1,0:T(8,128)(2,1)}), bf16[64,48,128]{2,1,0:T(8,128)(2,1)S(1)}, u32[]{:S(2)}, u32[]{:S(2)}) async-start(bf16[64,48,128]{2,1,0:T(8,128)(2,1)} %shard_map.66), calls=%async_computation.1 | async-start | bytes 1572864 | tf_op jit(solution)/shard_map/all_to_all | solution.py:497
  109.5 10.2 %collective-permute-start.4 = (bf16[48,256]{1,0:T(8,128)(2,1)S(1)}, bf16[48,256]{1,0:T(8,128)(2,1)S(1)}, u32[]{:S(2)}, u32[]{:S(2)}) collective-permute-start(bf16[48,256]{1,0:T(8,128)(2,1)S(1)} %get-tuple-element.48.bottom_ref), channel_id=1, source_target_pairs={{0,64},{64,128},{128,192},{192,0},{1,65},{65,129},{129,193},{193,1... | collective-permute-start | bytes 73736 | tf_op jit(solution)/shard_map/ppermute | solution.py:484
  110.0 9.8 %collective-permute-start.5 = (bf16[48,256]{1,0:T(8,128)(2,1)S(1)}, bf16[48,256]{1,0:T(8,128)(2,1)S(1)}, u32[]{:S(2)}, u32[]{:S(2)}) collective-permute-start(bf16[48,256]{1,0:T(8,128)(2,1)S(1)} %get-tuple-element.47.top_ref), channel_id=1, source_target_pairs={{64,0},{128,64},{192,128},{0,192},{65,1},{129,65},{193,129},{1,193... | collective-permute-start | bytes 73736 | tf_op jit(solution)/shard_map/ppermute | solution.py:485
  111.5 8.2 %collective-permute-start.6 = (bf16[48,128]{1,0:T(8,128)(2,1)S(1)}, bf16[48,128]{1,0:T(8,128)(2,1)S(1)}, u32[]{:S(2)}, u32[]{:S(2)}) collective-permute-start(bf16[48,128]{1,0:T(8,128)(2,1)S(1)} %get-tuple-element.49), channel_id=1, source_target_pairs={{0,1},{1,2},{2,3},{3,4},{4,5},{5,6},{6,7},{7,8},{8,9},{9,10},{10,1... | collective-permute-start | bytes 36872 | tf_op jit(solution)/shard_map/ppermute | solution.py:486
  111.6 8.2 %collective-permute-start.7 = (bf16[48,128]{1,0:T(8,128)(2,1)S(1)}, bf16[48,128]{1,0:T(8,128)(2,1)S(1)}, u32[]{:S(2)}, u32[]{:S(2)}) collective-permute-start(bf16[48,128]{1,0:T(8,128)(2,1)S(1)} %get-tuple-element.50), channel_id=1, source_target_pairs={{1,0},{2,1},{3,2},{4,3},{5,4},{6,5},{7,6},{8,7},{9,8},{10,9},{11,1... | collective-permute-start | bytes 36872 | tf_op jit(solution)/shard_map/ppermute | solution.py:487

commit v7 on v6

--- a/solution.py
+++ b/solution.py
@@ -371,7 +371,7 @@
 
 
 def base_kernel(temp_ref, humid_ref, slot_ref, above_ref, below_ref, left_ref, right_ref,
-                base_ref, base_cols_ref, slot_cols_ref, t_ref, h_ref):
+                base_ref, base_cols_ref, slot_cols_ref, hot_ref, hot_cols_ref, t_ref, h_ref):
     t_ref[...] = temp_ref[...].astype(F32)
     h_ref[...] = humid_ref[...].astype(F32)
     for r, first in stencil_rows(lambda r: t_ref[:, r, :], above_ref, below_ref, left_ref, right_ref):
@@ -380,6 +380,9 @@
     slot = slot_ref[...]
     slots = gather_columns(lambda r: slot[r : r + 1])
     slot_cols_ref[...] = jnp.broadcast_to(slots, (8, 128))
+    hot_cols_ref[...] = hot_down((slots % 256).astype(F32))
+    for r in range(ROWS):
+        hot_ref[r] = hot_down((slot[r : r + 1] % 256).astype(F32))
 
 
 def base_step(temp, humid, slot, halo):
@@ -389,6 +392,8 @@
             jax.ShapeDtypeStruct((ROWS, LEV, COLS), F32),
             jax.ShapeDtypeStruct((LEV, 128), F32),
             jax.ShapeDtypeStruct((8, 128), jnp.int32),
+            jax.ShapeDtypeStruct((ROWS, 256, COLS), BF16),
+            jax.ShapeDtypeStruct((256, 128), BF16),
         ),
         (temp, humid, slot, *halo),
         [pltpu.VMEM((LEV, ROWS, COLS), F32), pltpu.VMEM((LEV, ROWS, COLS), F32)],
@@ -401,51 +406,52 @@
             r_ref[p * LEV : (p + 1) * LEV, h * CAP : (h + 1) * CAP] = ret_ref[2 * p + h]
 
 
-def picked(r_ref, slot):
+def picked(r_ref, slot, hot):
     count = slot.shape[1]
     pair = slot // 256
-    moved = jnp.dot(r_ref[...], hot_down((slot % 256).astype(F32)), preferred_element_type=F32)
+    moved = jnp.dot(r_ref[...], hot, preferred_element_type=F32)
     q = jnp.zeros((LEV, count), F32)
     for p in range(PAIRS):
         q = jnp.where(pair == p, moved[p * LEV : (p + 1) * LEV], q)
     return q
 
 
-def rim_kernel(ret_ref, slot_ref, slot_cols_ref, base_ref, base_cols_ref,
+def rim_kernel(ret_ref, slot_ref, slot_cols_ref, base_ref, base_cols_ref, hot_ref, hot_cols_ref,
                top_ref, bottom_ref, left_ref, right_ref, r_ref):
     in_pairs(ret_ref, r_ref)
     slot = jnp.concatenate(
         [slot_ref[0:1, :], slot_ref[ROWS - 1 : ROWS, :], slot_cols_ref[0:1, :]], axis=1
     )
-    q = 0.5 * picked(r_ref, slot)
+    hot = jnp.concatenate([hot_ref[0], hot_ref[ROWS - 1], hot_cols_ref[...]], axis=1)
+    q = 0.5 * picked(r_ref, slot, hot)
     top_ref[...] = (base_ref[0] + q[:, 0:COLS]).astype(BF16)
     bottom_ref[...] = (base_ref[ROWS - 1] + q[:, COLS : 2 * COLS]).astype(BF16)
     left_ref[...], right_ref[...] = split_columns(base_cols_ref[...] + q[:, 2 * COLS :])
 
 
-def rim(ret, slot, slot_cols, base, base_cols):
+def rim(ret, slot, slot_cols, base, base_cols, hot, hot_cols):
     return call(
         rim_kernel,
         edge_shapes(),
-        (ret, slot, slot_cols, base, base_cols),
+        (ret, slot, slot_cols, base, base_cols, hot, hot_cols),
         [pltpu.VMEM((PAIRS * LEV, 256), BF16)],
     )
 
 
-def unpack_kernel(ret_ref, slot_ref, base_ref, top_ref, bottom_ref, second_ref, r_ref):
+def unpack_kernel(ret_ref, slot_ref, hot_ref, base_ref, top_ref, bottom_ref, second_ref, r_ref):
     in_pairs(ret_ref, r_ref)
     second_ref[0] = top_ref[...]
     second_ref[ROWS - 1] = bottom_ref[...]
     for r in range(1, ROWS - 1):
-        q = picked(r_ref, slot_ref[r : r + 1, :])
+        q = picked(r_ref, slot_ref[r : r + 1, :], hot_ref[r])
         second_ref[r] = (base_ref[r] + 0.5 * q).astype(BF16)
 
 
-def unpack(ret, slot, base, top, bottom):
+def unpack(ret, slot, hot, base, top, bottom):
     return call(
         unpack_kernel,
         jax.ShapeDtypeStruct((ROWS, LEV, COLS), BF16),
-        (ret, slot, base, top, bottom),
+        (ret, slot, hot, base, top, bottom),
         [pltpu.VMEM((PAIRS * LEV, 256), BF16)],
     )
 
@@ -495,10 +501,10 @@
     answer = owner_step(recv, kabs, planck, top_flux)
     answer, halo = lax.optimization_barrier((answer, halo))
     ret = lax.all_to_all(answer, "tile", split_axis=0, concat_axis=0, tiled=True)
-    base, base_cols, slot_cols = base_step(temp, humid, slot, halo)
-    top, bottom, left, right = rim(ret, slot, slot_cols, base, base_cols)
+    base, base_cols, slot_cols, hot, hot_cols = base_step(temp, humid, slot, halo)
+    top, bottom, left, right = rim(ret, slot, slot_cols, base, base_cols, hot, hot_cols)
     halo = exchange(top, bottom, left, right)
-    second = unpack(ret, slot, base, top, bottom)
+    second = unpack(ret, slot, hot, base, top, bottom)
     return last_step(second, halo)
 
 

time: 122 us -> 124 us (1.016)
  local copies, waits for them, and re-layouts: 0.34 us -> 3.36 us
  waiting for transfers between devices: 55.3 us -> 53.4 us
    unnamed x11 -> x15, local copies, waits for them, and re-layouts: 0.12 us -> 3.14 us
    all_to_all x1, waiting for transfers between devices: 20.8 us -> 18.8 us  [on_device(): lax.all_to_all(answer, 'tile', split_axis=0, concat_axis=0, tiled=True)]
    ppermute x2, starting transfers between devices: 0.99 us -> 2.88 us  [exchange(): above = lax.ppermute(bottom, 'grp', up)]
where the time goes in v7:
time: 124 us
  waiting for transfers between devices  53.4 us (43%)
  Pallas kernels  33.6 us (27%)
  starting transfers between devices  33.1 us (27%)
  local copies, waits for them, and re-layouts  3.36 us (3%)
    ppermute x2, waiting for transfers between devices, exchange(): west = lax.ppermute(right, 'tile', along)  31.4 us
    pallas_call x6, Pallas kernels, call(): pl.pallas_call(kernel, out_shape=out_shape, in_specs=[vmem] * arrays + [s...  23 us
    all_to_all x1, waiting for transfers between devices, on_device(): lax.all_to_all(answer, 'tile', split_axis=0, concat_axis=0, tiled=True)  18.8 us
    all_to_all x1, starting transfers between devices, on_device(): recv = lax.all_to_all(send, 'tile', split_axis=0, concat_axis=0, tiled=True)  12.3 us
    pallas_call x1, Pallas kernels, pack(): pl.pallas_call(pack_kernel, out_shape=(pltpu.HBM((TILES, SEND, CAP), BF16...  10.6 us
    ppermute x2, starting transfers between devices, exchange(): east = lax.ppermute(left, 'tile', [(b, a) for a, b in along])  10.1 us
    all_to_all x1, starting transfers between devices, on_device(): lax.all_to_all(answer, 'tile', split_axis=0, concat_axis=0, tiled=True)  5.38 us
    all_to_all x1, waiting for transfers between devices, on_device(): recv = lax.all_to_all(send, 'tile', split_axis=0, concat_axis=0, tiled=True)  3.15 us
  transfers between devices with their start and end apart: 10, of which 3 were waited for; matrix products, arithmetic and copies ran while one was open for 0% of the time, Pallas kernels for 5%

profile of v7, /device:TPU:6, one launch (start us, length us, event | category | flops | bytes accessed | tf_op | source)
XLA Modules:
  0.0 123.9 jit_solution(13019295122115857338)
XLA Ops:
  0.0 10.6 %shard_map.64 = (bf16[64,104,128]{2,1,0:T(8,128)(2,1)}, s32[16,256]{1,0:T(8,128)S(1)}) custom-call(bf16[48,16,256]{2,1,0:T(8,128)(2,1)} %temp_ref.5, bf16[48,16,256]{2,1,0:T(8,128)(2,1)} %humid_ref.3, s32[16,256]{1,0:T(8,128)} %parent_ref.1), custom_call_target="tpu_custom_call" | custom-call | tf_op jit(solution)/shard_map/pallas_call | solution.py:137
  10.7 0.0 copy-start
  10.7 0.0 copy-start.4
  10.7 0.0 copy-start.5
  10.7 0.0 copy-start.6
  10.7 12.3 %all-to-all-start = ((bf16[64,104,128]{2,1,0:T(8,128)(2,1)}), bf16[64,104,128]{2,1,0:T(8,128)(2,1)S(1)}, u32[]{:S(2)}, u32[]{:S(2)}) async-start(bf16[64,104,128]{2,1,0:T(8,128)(2,1)} %get-tuple-element.30), calls=%async_computation | async-start | bytes 3407872 | tf_op jit(solution)/shard_map/all_to_all | solution.py:499
  23.0 0.0 copy-done
  23.0 1.2 shard_map.65
  24.2 0.1 collective-permute-start.2
  24.3 5.0 %collective-permute-start.3 = (bf16[48,128]{1,0:T(8,128)(2,1)S(1)}, bf16[48,128]{1,0:T(8,128)(2,1)S(1)}, u32[]{:S(2)}, u32[]{:S(2)}) collective-permute-start(bf16[48,128]{1,0:T(8,128)(2,1)S(1)} %get-tuple-element.34), channel_id=1, source_target_pairs={{1,0},{2,1},{3,2},{4,3},{5,4},{6,5},{7,6},{8,7},{9,8},{10,9},{11,1... | collective-permute-start | bytes 36872 | tf_op jit(solution)/shard_map/ppermute | solution.py:493
  29.3 0.5 collective-permute-start
  29.7 1.5 %collective-permute-start.1 = (bf16[48,256]{1,0:T(8,128)(2,1)S(1)}, bf16[48,256]{1,0:T(8,128)(2,1)S(1)}, u32[]{:S(2)}, u32[]{:S(2)}) collective-permute-start(bf16[48,256]{1,0:T(8,128)(2,1)S(1)} %get-tuple-element.32), channel_id=1, source_target_pairs={{64,0},{128,64},{192,128},{0,192},{65,1},{129,65},{193,129},{1,193... | collective-permute-start | bytes 73736 | tf_op jit(solution)/shard_map/ppermute | solution.py:491
  31.3 0.0 copy-done.4
  31.3 0.1 copy.10
  31.4 0.0 copy-done.5
  31.4 0.1 copy.12
  31.5 0.0 copy-done.6
  31.5 0.1 copy.13
  31.6 0.1 pad_maximum_fusion.table_in
  31.7 31.4 %collective-permute-done.2.left_ref = bf16[48,128]{1,0:T(8,128)(2,1)S(1)} collective-permute-done((bf16[48,128]{1,0:T(8,128)(2,1)S(1)}, bf16[48,128]{1,0:T(8,128)(2,1)S(1)}, u32[]{:S(2)}, u32[]{:S(2)}) %collective-permute-start.2) | collective-permute-done | bytes 12320 | tf_op jit(solution)/shard_map/ppermute | solution.py:492
  63.1 0.0 collective-permute-done.3.right_ref
  63.1 0.0 collective-permute-done.above_ref
  63.2 0.0 collective-permute-done.1.below_ref
  63.2 3.1 %all-to-all-done.recv_ref = bf16[64,104,128]{2,1,0:T(8,128)(2,1)S(1)} async-done(((bf16[64,104,128]{2,1,0:T(8,128)(2,1)}), bf16[64,104,128]{2,1,0:T(8,128)(2,1)S(1)}, u32[]{:S(2)}, u32[]{:S(2)}) %all-to-all-start) | async-done | bytes 1703968 | tf_op jit(solution)/shard_map/all_to_all | solution.py:499
  66.3 14.0 %shard_map.66 = bf16[64,48,128]{2,1,0:T(8,128)(2,1)} custom-call(bf16[64,104,128]{2,1,0:T(8,128)(2,1)S(1)} %all-to-all-done.recv_ref, f32[112,50]{1,0:T(8,128)S(1)} %pad_maximum_fusion.table_in), custom_call_target="tpu_custom_call" | custom-call | tf_op jit(solution)/shard_map/pallas_call | solution.py:42
  80.3 5.4 %all-to-all-start.1 = ((bf16[64,48,128]{2,1,0:T(8,128)(2,1)}), bf16[64,48,128]{2,1,0:T(8,128)(2,1)S(1)}, u32[]{:S(2)}, u32[]{:S(2)}) async-start(bf16[64,48,128]{2,1,0:T(8,128)(2,1)} %shard_map.66), calls=%async_computation.1 | async-start | bytes 1572864 | tf_op jit(solution)/shard_map/all_to_all | solution.py:503
  85.7 0.0 copy-start.3
  85.7 1.0 copy-done.3
  86.7 2.2 %shard_map.67 = (f32[16,48,256]{2,1,0:T(8,128)S(1)}, f32[48,128]{1,0:T(8,128)S(1)}, s32[8,128]{1,0:T(8,128)S(1)}, bf16[16,256,256]{2,1,0:T(8,128)(2,1)S(1)}, bf16[256,128]{1,0:T(8,128)(2,1)S(1)}) custom-call(bf16[48,16,256]{2,1,0:T(8,128)(2,1)S(1)} %copy-done, bf16[48,16,256]{2,1,0:T(8,128)(2,1)S(1)} %copy-done.3, s32[16,256]{1,0:T(8,128)S(1)} %get-tuple-element.41.slot_ref, ...), custom_call_target="tpu_custom_call" | custom-call | tf_op jit(solution)/shard_map/pallas_call | solution.py:42
  88.9 0.0 copy-start.1
  88.9 0.9 copy-done.1
  89.8 18.8 %all-to-all-done.1.ret_ref = bf16[64,48,128]{2,1,0:T(8,128)(2,1)S(1)} async-done(((bf16[64,48,128]{2,1,0:T(8,128)(2,1)}), bf16[64,48,128]{2,1,0:T(8,128)(2,1)S(1)}, u32[]{:S(2)}, u32[]{:S(2)}) %all-to-all-start.1) | async-done | bytes 786464 | tf_op jit(solution)/shard_map/all_to_all | solution.py:503
  108.6 0.0 copy-start.2
  108.6 1.1 copy-done.2
  109.7 0.9 shard_map.68
  110.6 0.9 collective-permute-start.5
  111.5 2.4 %collective-permute-start.4 = (bf16[48,256]{1,0:T(8,128)(2,1)S(1)}, bf16[48,256]{1,0:T(8,128)(2,1)S(1)}, u32[]{:S(2)}, u32[]{:S(2)}) collective-permute-start(bf16[48,256]{1,0:T(8,128)(2,1)S(1)} %get-tuple-element.52.bottom_ref), channel_id=1, source_target_pairs={{0,64},{64,128},{128,192},{192,0},{1,65},{65,129},{129,193},{193,1... | collective-permute-start | bytes 73736 | tf_op jit(solution)/shard_map/ppermute | solution.py:490
  113.9 0.0 collective-permute-start.6
  113.9 5.1 %collective-permute-start.7 = (bf16[48,128]{1,0:T(8,128)(2,1)S(1)}, bf16[48,128]{1,0:T(8,128)(2,1)S(1)}, u32[]{:S(2)}, u32[]{:S(2)}) collective-permute-start(bf16[48,128]{1,0:T(8,128)(2,1)S(1)} %get-tuple-element.54), channel_id=1, source_target_pairs={{1,0},{2,1},{3,2},{4,3},{5,4},{6,5},{7,6},{8,7},{9,8},{10,9},{11,1... | collective-permute-start | bytes 36872 | tf_op jit(solution)/shard_map/ppermute | solution.py:493
  119.0 3.1 %shard_map.69.second_ref = bf16[16,48,256]{2,1,0:T(8,128)(2,1)S(1)} custom-call(bf16[64,48,128]{2,1,0:T(8,128)(2,1)S(1)} %all-to-all-done.1.ret_ref, s32[16,256]{1,0:T(8,128)S(1)} %get-tuple-element.41.slot_ref, bf16[16,256,256]{2,1,0:T(8,128)(2,1)S(1)} %get-tuple-element.46.hot_ref, f32[16,48,256]{2,1,0:T(8,128)S(1)} %copy-done.2, ...), custom_call_target="tpu_custom_call" | custom-call | tf_op jit(solution)/shard_map/pallas_call | solution.py:42
  122.0 0.0 collective-permute-done.6.left_ref
  122.0 0.0 collective-permute-done.7.right_ref
  122.0 0.0 collective-permute-done.5.below_ref
  122.1 0.0 collective-permute-done.4.above_ref
  122.1 1.6 %shard_map.70 = bf16[48,16,256]{2,1,0:T(8,128)(2,1)} custom-call(bf16[16,48,256]{2,1,0:T(8,128)(2,1)S(1)} %shard_map.69.second_ref, bf16[48,256]{1,0:T(8,128)(2,1)S(1)} %collective-permute-done.4.above_ref, bf16[48,256]{1,0:T(8,128)(2,1)S(1)} %collective-permute-done.5.below_ref, bf16[48,128]{1,0:T(8,128)(2,1)S(1)} %collective-permute-done.6.left_ref, ...), custom_call_target="tpu_custom_call" | custom-call | tf_op jit(solution)/shard_map/pallas_call | solution.py:42
  (1 shorter events, 0.0 us)
Async XLA Ops:
  10.7 12.3 %copy-start = (bf16[48,16,256]{2,1,0:T(8,128)(2,1)S(1)}, bf16[48,16,256]{2,1,0:T(8,128)(2,1)}, u32[]{:S(2)}) copy-start(bf16[48,16,256]{2,1,0:T(8,128)(2,1)} %temp_ref.5) | copy-start | bytes 1179652
  10.7 20.6 %copy-start.4 = (f32[112,48]{0,1:T(8,128)S(1)}, f32[112,48]{0,1:T(8,128)}, u32[]{:S(2)}) copy-start(f32[112,48]{0,1:T(8,128)} %param.9) | copy-start | bytes 64516
  10.7 20.7 %copy-start.5 = (f32[112]{0:T(128)S(1)}, f32[112]{0:T(128)}, u32[]{:S(2)}) copy-start(f32[112]{0:T(128)} %param.10) | copy-start | bytes 1348
  10.7 20.8 %copy-start.6 = (f32[112]{0:T(128)S(1)}, f32[112]{0:T(128)}, u32[]{:S(2)}) copy-start(f32[112]{0:T(128)} %param.11) | copy-start | bytes 1348
  10.7 55.6 %all-to-all-start = ((bf16[64,104,128]{2,1,0:T(8,128)(2,1)}), bf16[64,104,128]{2,1,0:T(8,128)(2,1)S(1)}, u32[]{:S(2)}, u32[]{:S(2)}) async-start(bf16[64,104,128]{2,1,0:T(8,128)(2,1)} %get-tuple-element.30), calls=%async_computation | async-start | bytes 3407872 | tf_op jit(solution)/shard_map/all_to_all | solution.py:499
  24.2 39.0 %collective-permute-start.2 = (bf16[48,128]{1,0:T(8,128)(2,1)S(1)}, bf16[48,128]{1,0:T(8,128)(2,1)S(1)}, u32[]{:S(2)}, u32[]{:S(2)}) collective-permute-start(bf16[48,128]{1,0:T(8,128)(2,1)S(1)} %get-tuple-element.33), channel_id=1, source_target_pairs={{0,1},{1,2},{2,3},{3,4},{4,5},{5,6},{6,7},{7,8},{8,9},{9,10},{10,1... | collective-permute-start | bytes 36872 | tf_op jit(solution)/shard_map/ppermute | solution.py:492
  24.3 38.9 %collective-permute-start.3 = (bf16[48,128]{1,0:T(8,128)(2,1)S(1)}, bf16[48,128]{1,0:T(8,128)(2,1)S(1)}, u32[]{:S(2)}, u32[]{:S(2)}) collective-permute-start(bf16[48,128]{1,0:T(8,128)(2,1)S(1)} %get-tuple-element.34), channel_id=1, source_target_pairs={{1,0},{2,1},{3,2},{4,3},{5,4},{6,5},{7,6},{8,7},{9,8},{10,9},{11,1... | collective-permute-start | bytes 36872 | tf_op jit(solution)/shard_map/ppermute | solution.py:493
  29.3 33.9 %collective-permute-start = (bf16[48,256]{1,0:T(8,128)(2,1)S(1)}, bf16[48,256]{1,0:T(8,128)(2,1)S(1)}, u32[]{:S(2)}, u32[]{:S(2)}) collective-permute-start(bf16[48,256]{1,0:T(8,128)(2,1)S(1)} %get-tuple-element.31), channel_id=1, source_target_pairs={{0,64},{64,128},{128,192},{192,0},{1,65},{65,129},{129,193},{193,1... | collective-permute-start | bytes 73736 | tf_op jit(solution)/shard_map/ppermute | solution.py:490
  29.7 33.4 %collective-permute-start.1 = (bf16[48,256]{1,0:T(8,128)(2,1)S(1)}, bf16[48,256]{1,0:T(8,128)(2,1)S(1)}, u32[]{:S(2)}, u32[]{:S(2)}) collective-permute-start(bf16[48,256]{1,0:T(8,128)(2,1)S(1)} %get-tuple-element.32), channel_id=1, source_target_pairs={{64,0},{128,64},{192,128},{0,192},{65,1},{129,65},{193,129},{1,193... | collective-permute-start | bytes 73736 | tf_op jit(solution)/shard_map/ppermute | solution.py:491
  80.3 28.3 %all-to-all-start.1 = ((bf16[64,48,128]{2,1,0:T(8,128)(2,1)}), bf16[64,48,128]{2,1,0:T(8,128)(2,1)S(1)}, u32[]{:S(2)}, u32[]{:S(2)}) async-start(bf16[64,48,128]{2,1,0:T(8,128)(2,1)} %shard_map.66), calls=%async_computation.1 | async-start | bytes 1572864 | tf_op jit(solution)/shard_map/all_to_all | solution.py:503
  85.7 1.0 copy-start.3
  88.9 0.9 copy-start.1
  108.6 1.1 copy-start.2
  110.6 11.4 %collective-permute-start.5 = (bf16[48,256]{1,0:T(8,128)(2,1)S(1)}, bf16[48,256]{1,0:T(8,128)(2,1)S(1)}, u32[]{:S(2)}, u32[]{:S(2)}) collective-permute-start(bf16[48,256]{1,0:T(8,128)(2,1)S(1)} %get-tuple-element.51.top_ref), channel_id=1, source_target_pairs={{64,0},{128,64},{192,128},{0,192},{65,1},{129,65},{193,129},{1,193... | collective-permute-start | bytes 73736 | tf_op jit(solution)/shard_map/ppermute | solution.py:491
  111.5 10.6 %collective-permute-start.4 = (bf16[48,256]{1,0:T(8,128)(2,1)S(1)}, bf16[48,256]{1,0:T(8,128)(2,1)S(1)}, u32[]{:S(2)}, u32[]{:S(2)}) collective-permute-start(bf16[48,256]{1,0:T(8,128)(2,1)S(1)} %get-tuple-element.52.bottom_ref), channel_id=1, source_target_pairs={{0,64},{64,128},{128,192},{192,0},{1,65},{65,129},{129,193},{193,1... | collective-permute-start | bytes 73736 | tf_op jit(solution)/shard_map/ppermute | solution.py:490
  113.9 8.1 %collective-permute-start.6 = (bf16[48,128]{1,0:T(8,128)(2,1)S(1)}, bf16[48,128]{1,0:T(8,128)(2,1)S(1)}, u32[]{:S(2)}, u32[]{:S(2)}) collective-permute-start(bf16[48,128]{1,0:T(8,128)(2,1)S(1)} %get-tuple-element.53), channel_id=1, source_target_pairs={{0,1},{1,2},{2,3},{3,4},{4,5},{5,6},{6,7},{7,8},{8,9},{9,10},{10,1... | collective-permute-start | bytes 36872 | tf_op jit(solution)/shard_map/ppermute | solution.py:492
  113.9 8.2 %collective-permute-start.7 = (bf16[48,128]{1,0:T(8,128)(2,1)S(1)}, bf16[48,128]{1,0:T(8,128)(2,1)S(1)}, u32[]{:S(2)}, u32[]{:S(2)}) collective-permute-start(bf16[48,128]{1,0:T(8,128)(2,1)S(1)} %get-tuple-element.54), channel_id=1, source_target_pairs={{1,0},{2,1},{3,2},{4,3},{5,4},{6,5},{7,6},{8,7},{9,8},{10,9},{11,1... | collective-permute-start | bytes 36872 | tf_op jit(solution)/shard_map/ppermute | solution.py:493
